TPU v7x, 256 devices: a whole 4x4x8 slice. The times are simulated.
256 devices in a mesh: seq: 32 (over z, x), head: 8 (over y, core).
Axes of the slice: x: 4, y: 4, z: 8, core: 2. Of those that a mesh axis runs over, the one named last changes fastest.
Arguments:
- layer_input: bfloat16 [4096, 8192], P('seq'), may hold values from -6 to 6
- beta_weight: bfloat16 [32, 8192], P('head'), may hold values from -0.0625 to 0.0625
- decay_weight: bfloat16 [32, 8192], P('head'), may hold values from -0.0625 to 0.0625
- log_rate: float32 [32], P('head'), may hold values from -11.5 to -3
- decay_bias: float32 [32], P('head'), may hold values from -2 to 1
- delta_query: bfloat16 [4096, 4096], P('seq', 'head'), may hold values from -6 to 6
- delta_key: bfloat16 [4096, 4096], P('seq', 'head'), may hold values from -6 to 6
- delta_value: bfloat16 [4096, 4096], P('seq', 'head'), may hold values from -6 to 6
- delta_out_grad: bfloat16 [4096, 4096], P('seq', 'head'), may hold values from -6 to 6
- state_init: float32 [32, 128, 128], P('head'), may hold values from -6 to 6
- state_grad_next: float32 [32, 128, 128], P('head'), may hold values from -6 to 6
- attn_query: bfloat16 [4096, 1024], P('seq', 'head'), may hold values from -80 to 80
- attn_key: bfloat16 [4096, 1024], P('seq', 'head'), may hold values from -12 to 12
- attn_value: bfloat16 [4096, 1024], P('seq', 'head'), may hold values from -6 to 6
- attn_out_grad: bfloat16 [4096, 1024], P('seq', 'head'), may hold values from -6 to 6
Outputs:
- delta_query_grad: float32 [4096, 4096], P('seq', 'head')
- delta_key_grad: float32 [4096, 4096], P('seq', 'head')
- delta_value_grad: float32 [4096, 4096], P('seq', 'head')
- boundary_grads: float32 [32, 32, 128, 128], P('seq', 'head')
- input_grad: float32 [4096, 8192], P('seq', 'head')
- beta_weight_grad: float32 [32, 8192], P('head', 'seq')
- decay_weight_grad: float32 [32, 8192], P('head', 'seq')
- log_rate_grad: float32 [32], P('head')
- decay_bias_grad: float32 [32], P('head')
- attn_query_grad: float32 [4096, 1024], P('seq', 'head')
- attn_key_grad: float32 [4096, 1024], P('seq', 'head')
- attn_value_grad: float32 [4096, 1024], P('seq', 'head')
All inputs are finite; a program needn't handle non-finite values.
Results may differ from a plain program's by a relative error of at most 0.00035.
Values may be sent and summed in bfloat16 or wider, within the bound.
No kernel may reach another device: no remote copies, remote signals or barrier semaphores. Data moves between devices by JAX's collectives and lax.ppermute only.
A program may use at most 128 MiB of HBM per device.

v0:
```python
import math

import jax
import jax.numpy as jnp
from jax import lax
from jax.sharding import Mesh
from jax.sharding import PartitionSpec as P

STRETCH = 64
AHD = 128
WINDOW = 1024
SEQ = ("seq_0", "seq_1")


PRECISE = lax.Precision.HIGHEST


def neutral_like(value, identity):
    return jax.tree.map(
        lambda a, e: jnp.broadcast_to(jnp.asarray(e, a.dtype), a.shape), value, identity
    )


def carried_in(value, axes, combine, identity, reverse):
    before = start = neutral_like(value, identity)
    so_far = value
    for axis in reversed(axes):
        length, index = (lax.axis_size(axis), lax.axis_index(axis))
        pieces = jax.tree.map(lambda part: lax.all_gather(part, axis), so_far)
        inside, so_far = (start, start)
        for k in reversed(range(length)) if reverse else range(length):
            passed = k > index if reverse else k < index
            so_far = combine(so_far, jax.tree.map(lambda part: part[k], pieces))
            inside = jax.tree.map(lambda new, old: jnp.where(passed, new, old), so_far, inside)
        before = combine(inside, before)
    return before


def turned_gather(arrays, axis, dims):
    turned = [jnp.moveaxis(a, dim, 0) for a, dim in zip(arrays, dims)]
    both = jnp.concatenate([t.reshape(len(t), -1) for t in turned], axis=1)
    result, at, finished = (lax.all_gather(both, axis, axis=0, tiled=True), 0, [])
    for t, dim in zip(turned, dims):
        piece = result[:, at : at + t[0].size].reshape(-1, *t.shape[1:])
        finished.append(jnp.moveaxis(piece, 0, dim))
        at += t[0].size
    return tuple(finished)


def side_by_side(arrays, axis, dim, along):
    widths = [a.shape[along] for a in arrays]
    both = jnp.concatenate(arrays, axis=along)
    result = lax.psum_scatter(both, axis, scatter_dimension=dim, tiled=True)
    return tuple(jnp.split(result, [sum(widths[:k]) for k in range(1, len(widths))], axis=along))


def from_everyone(value, axis):
    copies = jnp.broadcast_to(value, (lax.axis_size(axis), *value.shape))
    return lax.all_to_all(copies, axis, split_axis=0, concat_axis=0, tiled=True)


def of_everyone(value, axis):
    everything = from_everyone(value, axis)
    return jnp.sum(everything, axis=0)


def in_one(arrays, axis):
    ends = [0]
    for a in arrays:
        ends.append(ends[-1] + a.size)
    so_far = of_everyone(jnp.concatenate([a.ravel() for a in arrays]), axis)
    return tuple((so_far[b:e].reshape(a.shape) for a, b, e in zip(arrays, ends, ends[1:])))


def shifted(value, axis, by):
    length = lax.axis_size(axis)
    pairs = [(i, i + by) for i in range(length) if 0 <= i + by < length]
    return lax.ppermute(value, axis, pairs)


def dot_high(left_mat, right_mat):
    return jnp.matmul(left_mat, right_mat, precision=PRECISE)


def chain_mul(left_mat, right_mat):
    return jnp.einsum("hij,hjk->hik", left_mat, right_mat, precision=PRECISE)


def compose(earlier_map, later_map):
    return (
        chain_mul(later_map[0], earlier_map[0]),
        chain_mul(later_map[0], earlier_map[1]) + later_map[1],
    )


def unit_rows(values):
    return values * lax.rsqrt(jnp.sum(values * values, axis=-1, keepdims=True) + 1e-06)


def stretch_step(memory, queries, key_rows, values, beta_rows, decay_log):
    span_len = queries.shape[0]
    cumulative = jnp.cumsum(decay_log)
    row_ids = lax.broadcasted_iota(jnp.int32, (span_len, span_len), 0)
    col_ids = lax.broadcasted_iota(jnp.int32, (span_len, span_len), 1)
    lower_mask = row_ids >= col_ids
    strict_mask = row_ids > col_ids
    ratios = jnp.where(
        lower_mask,
        jnp.exp(jnp.where(lower_mask, cumulative[:, None] - cumulative[None, :], 0.0)),
        0.0,
    )
    gram_keys = dot_high(key_rows, key_rows.T)
    system_mat = jnp.eye(span_len, dtype=queries.dtype) + jnp.where(
        strict_mask, beta_rows[:, None] * ratios * gram_keys, 0.0
    )
    growths = jnp.exp(cumulative)
    right_side = beta_rows[:, None] * (values - growths[:, None] * dot_high(key_rows, memory))
    updates = jax.scipy.linalg.solve_triangular(
        system_mat, right_side, lower=True, unit_diagonal=True
    )
    output = growths[:, None] * dot_high(queries, memory) + dot_high(
        ratios * dot_high(queries, key_rows.T), updates
    )
    tail_decay = jnp.exp(cumulative[-1] - cumulative)
    new_memory = jnp.exp(cumulative[-1]) * memory + dot_high(
        (key_rows * tail_decay[:, None]).T, updates
    )
    return (new_memory, output)


def block_forward(memory, q_raw, k_raw, values, beta_rows, decay_rows):
    head_count, tok_count, key_width = q_raw.shape
    span_count = tok_count // STRETCH
    queries = unit_rows(q_raw) / math.sqrt(key_width)
    key_rows = unit_rows(k_raw)

    def in_stretches(array_in):
        return jnp.swapaxes(
            array_in.reshape((head_count, span_count, STRETCH) + array_in.shape[2:]), 0, 1
        )

    pieces_all = (
        in_stretches(queries),
        in_stretches(key_rows),
        in_stretches(values),
        in_stretches(beta_rows),
        in_stretches(decay_rows),
    )
    stepper = jax.vmap(stretch_step)

    def advance(carried, pieces):
        return stepper(carried, pieces[0], pieces[1], pieces[2], pieces[3], pieces[4])

    final_mem, outputs = lax.scan(advance, memory, pieces_all)
    outputs = jnp.swapaxes(outputs, 0, 1).reshape(head_count, tok_count, values.shape[2])
    return (outputs, final_mem)


def gate_values(beta_logit, decay_input, log_rate, decay_bias):
    betas = jax.nn.sigmoid(beta_logit)
    decays = -jnp.exp(log_rate)[None, :] * jax.nn.softplus(decay_input + decay_bias[None, :])
    return (betas, decays)


def heads_first(flat_rows, head_count):
    return jnp.swapaxes(flat_rows.reshape(flat_rows.shape[0], head_count, -1), 0, 1)


def tokens_first(split_heads):
    return jnp.swapaxes(split_heads, 0, 1).reshape(split_heads.shape[1], -1)


def window_grads(q_block, k_block, v_block, grad_block, q_places, k_places):
    q_heads = q_block.reshape(q_block.shape[0], -1, AHD)
    k_heads = k_block.reshape(k_block.shape[0], -1, AHD)
    v_heads = v_block.reshape(v_block.shape[0], -1, AHD)
    g_heads = grad_block.reshape(grad_block.shape[0], -1, AHD)
    scale = 1.0 / math.sqrt(AHD)
    scores = (
        jnp.einsum("qhd,khd->hqk", q_heads, k_heads, preferred_element_type=jnp.float32) * scale
    )
    spread = q_places[:, None] - k_places[None, :]
    allowed = (spread >= 0) & (spread < WINDOW) & (k_places[None, :] >= 0)
    scores = jnp.where(allowed[None], scores, -1e30)
    weights = jax.nn.softmax(scores, axis=-1)
    g_wide = g_heads.astype(jnp.float32)
    mixed = jnp.einsum("hqk,khd->qhd", weights, v_heads.astype(jnp.float32), precision=PRECISE)
    weight_grad = jnp.einsum("qhd,khd->hqk", g_heads, v_heads, preferred_element_type=jnp.float32)
    value_grad = jnp.einsum("hqk,qhd->khd", weights, g_wide, precision=PRECISE)
    row_terms = jnp.swapaxes(jnp.sum(g_wide * mixed, axis=-1), 0, 1)
    score_grad = weights * (weight_grad - row_terms[:, :, None]) * scale
    query_grad = jnp.einsum(
        "hqk,khd->qhd", score_grad, k_heads.astype(jnp.float32), precision=PRECISE
    )
    key_grad = jnp.einsum(
        "hqk,qhd->khd", score_grad, q_heads.astype(jnp.float32), precision=PRECISE
    )
    return (
        query_grad.reshape(q_block.shape[0], -1),
        key_grad.reshape(k_block.shape[0], -1),
        value_grad.reshape(k_block.shape[0], -1),
    )


def shards(
    layer_input,
    beta_weight,
    decay_weight,
    log_rate,
    decay_bias,
    delta_query,
    delta_key,
    delta_value,
    delta_out_grad,
    state_init,
    state_grad_next,
    attn_query,
    attn_key,
    attn_value,
    attn_out_grad,
):
    seq_count = lax.axis_size(SEQ)
    seq_index = lax.axis_index(SEQ)
    local_heads = beta_weight.shape[0]
    beta_logit = jnp.dot(layer_input, beta_weight.T, preferred_element_type=jnp.float32)
    decay_input = jnp.dot(layer_input, decay_weight.T, preferred_element_type=jnp.float32)
    (betas, decays), pull_gate = jax.vjp(gate_values, beta_logit, decay_input, log_rate, decay_bias)
    queries = heads_first(delta_query.astype(jnp.float32), local_heads)
    key_rows = heads_first(delta_key.astype(jnp.float32), local_heads)
    value_rows = heads_first(delta_value.astype(jnp.float32), local_heads)
    out_grad = heads_first(delta_out_grad.astype(jnp.float32), local_heads)
    beta_rows = betas.T
    decay_rows = decays.T
    key_width = key_rows.shape[2]
    identity_mat = jnp.broadcast_to(
        jnp.eye(key_width, dtype=jnp.float32), (local_heads, key_width, key_width)
    )
    zero_mem = jnp.zeros_like(state_init)
    transit = block_forward(
        identity_mat, queries, key_rows, jnp.zeros_like(key_rows), beta_rows, decay_rows
    )[1]
    transit_t = jnp.swapaxes(transit, 1, 2)

    def from_memory(memory):
        return block_forward(memory, queries, key_rows, value_rows, beta_rows, decay_rows)

    primal_zero, pull_zero = jax.vjp(from_memory, zero_mem)
    offset = primal_zero[1]
    local_grad = pull_zero((out_grad, zero_mem))[0]
    head_mat, head_vec = carried_in(
        (transit, offset), SEQ, compose, (identity_mat, zero_mem), False
    )
    mem_in = chain_mul(head_mat, state_init) + head_vec
    tail_mat, tail_vec = carried_in(
        (transit_t, local_grad), SEQ, compose, (identity_mat, zero_mem), True
    )
    grad_end = chain_mul(tail_mat, state_grad_next) + tail_vec
    primal_full, pull_full = jax.vjp(
        block_forward, mem_in, queries, key_rows, value_rows, beta_rows, decay_rows
    )
    grad_in, grad_q, grad_k, grad_v, grad_beta, grad_decay = pull_full((out_grad, grad_end))
    grad_logit_b, grad_logit_d, grad_rate, grad_bias = pull_gate((grad_beta.T, grad_decay.T))
    every_b, every_d = turned_gather((grad_logit_b, grad_logit_d), "head", (1, 1))
    cols_b, cols_d = (
        lax.all_to_all(beta_weight, "head", split_axis=1, concat_axis=0, tiled=True),
        lax.all_to_all(decay_weight, "head", split_axis=1, concat_axis=0, tiled=True),
    )
    input_grad = dot_high(every_b, cols_b.astype(jnp.float32)) + dot_high(
        every_d, cols_d.astype(jnp.float32)
    )
    input_rows = layer_input.astype(jnp.float32)
    weight_terms = (dot_high(grad_logit_b.T, input_rows), dot_high(grad_logit_d.T, input_rows))
    beta_weight_grad, decay_weight_grad = side_by_side(
        (weight_terms[0], weight_terms[1]), SEQ, 1, 0
    )
    log_rate_grad, decay_bias_grad = in_one((grad_rate, grad_bias), SEQ)
    tok_len = attn_query.shape[0]
    reach_blocks = min(WINDOW // tok_len, seq_count - 1)
    pair_local = jnp.stack([attn_key, attn_value])
    fetched = []
    moving = pair_local
    for distance in range(1, reach_blocks + 1):
        moving = shifted(moving, SEQ, 1)
        fetched.append(moving)
    ordered = [fetched[distance - 1] for distance in range(reach_blocks, 0, -1)] + [pair_local]
    window_pair = jnp.concatenate(ordered, axis=1)
    q_places = seq_index * tok_len + lax.iota(jnp.int32, tok_len)
    k_places = (seq_index - reach_blocks) * tok_len + lax.iota(
        jnp.int32, (reach_blocks + 1) * tok_len
    )
    grad_aq, grad_window_k, grad_window_v = window_grads(
        attn_query, window_pair[0], window_pair[1], attn_out_grad, q_places, k_places
    )
    grad_pairs = jnp.stack([grad_window_k, grad_window_v])
    own_grads = grad_pairs[:, reach_blocks * tok_len :]
    carried = jnp.zeros_like(own_grads)
    for distance in range(reach_blocks, 0, -1):
        carried = shifted(
            carried
            + grad_pairs[
                :, (reach_blocks - distance) * tok_len : (reach_blocks - distance + 1) * tok_len
            ],
            SEQ,
            -1,
        )
    total_grads = own_grads + carried
    boundary = grad_in[None]
    return (
        tokens_first(grad_q),
        tokens_first(grad_k),
        tokens_first(grad_v),
        boundary,
        input_grad,
        beta_weight_grad,
        decay_weight_grad,
        log_rate_grad,
        decay_bias_grad,
        grad_aq,
        total_grads[0],
        total_grads[1],
    )


def solution(mesh):
    torus = Mesh(mesh.devices.reshape(8, 4, mesh.shape["head"]), ("seq_0", "seq_1", "head"))
    in_specs = (
        P(SEQ, None),
        P("head", None),
        P("head", None),
        P("head"),
        P("head"),
        P(SEQ, "head"),
        P(SEQ, "head"),
        P(SEQ, "head"),
        P(SEQ, "head"),
        P("head", None, None),
        P("head", None, None),
        P(SEQ, "head"),
        P(SEQ, "head"),
        P(SEQ, "head"),
        P(SEQ, "head"),
    )
    out_specs = (
        P(SEQ, "head"),
        P(SEQ, "head"),
        P(SEQ, "head"),
        P(SEQ, "head", None, None),
        P(SEQ, "head"),
        P("head", SEQ),
        P("head", SEQ),
        P("head"),
        P("head"),
        P(SEQ, "head"),
        P(SEQ, "head"),
        P(SEQ, "head"),
    )
    return jax.shard_map(
        shards, mesh=torus, in_specs=in_specs, out_specs=out_specs, check_vma=False
    )
```

profile of v0, /device:TPU:8, one launch (start us, length us, event | category | flops | bytes accessed | tf_op | source)
XLA Modules:
  0.0 943.8 jit_solution(3198341212730141561)
XLA Ops:
  13.2 45.7 %while.142 = (s32[]{:T(128)}, f32[4,128,128]{2,1,0:T(8,128)S(1)}, f32[2,4,64]{2,1,0:T(4,128)}, f32[2,4,64,128]{3,2,1,0:T(8,128)S(1)}, f32[2,4,64]{2,1,0:T(4,128)}, /*index=5*/s32[]{:T(128)}, f32[]{:T(128)}) while((s32[]{:T(128)}, f32[4,128,128]{2,1,0:T(8,128)S(1)}, f32[2,4,64]{2,1,0:T(4,128)}, f32[2,4,64,128]{3,2,1,0:T(8,128)S(1)}, ...), condition=%wide.region_3.5_spmd, body=%wide.region_1.4_spmd.sunk | while | flops 151449664 | bytes 1992889 | solution.py:154
  15.3 19.7 %custom-call.44 = f32[4,1,64,64]{2,3,1,0:T(8,128)S(1)} custom-call(f32[4,1,64,64]{3,2,1,0:T(8,128)S(1)} %fusion.613), custom_call_target="InvertDiagBlocksLowerTriangular" | custom-call | tf_op jit(solution)/shard_map/while/body/eval_jaxpr/vmap(jit(_solve_triangular))/triangular_solve/custom-call.1 | solution.py:118
  38.2 19.7 %custom-call.44 = f32[4,1,64,64]{2,3,1,0:T(8,128)S(1)} custom-call(f32[4,1,64,64]{3,2,1,0:T(8,128)S(1)} %fusion.613), custom_call_target="InvertDiagBlocksLowerTriangular" | custom-call | tf_op jit(solution)/shard_map/while/body/eval_jaxpr/vmap(jit(_solve_triangular))/triangular_solve/custom-call.1 | solution.py:118
  71.0 62.4 %while.146 = (s32[]{:T(128)}, f32[4,128,128]{2,1,0:T(8,128)S(1)}, f32[2,4,64,1]{2,1,3,0:T(4,128)}, f32[2,4,64,1]{2,1,3,0:T(4,128)}, f32[2,4,64,64]{3,2,1,0:T(8,1...) while((s32[]{:T(128)}, f32[4,128,128]{2,1,0:T(8,128)S(1)}, ...), condition=%wide.region_7.9_spmd.clone.clone, body=%wide.region_5.8_spmd.clone.clone.sunk | while | flops 176836672 | bytes 3038607 | solution.py:154
  76.6 19.7 %custom-call.49 = f32[4,1,64,64]{2,3,1,0:T(8,128)S(1)} custom-call(f32[4,1,64,64]{3,2,1,0:T(8,128)S(1)} %add_bitcast_fusion.8), custom_call_target="InvertDiagBlocksLowerTriangular" | custom-call | tf_op jit(solution)/shard_map/jvp()/while/body/eval_jaxpr/vmap(jit(_solve_triangular))/triangular_solve/custom-call.1 | solution.py:118
  107.8 19.7 %custom-call.49 = f32[4,1,64,64]{2,3,1,0:T(8,128)S(1)} custom-call(f32[4,1,64,64]{3,2,1,0:T(8,128)S(1)} %add_bitcast_fusion.8), custom_call_target="InvertDiagBlocksLowerTriangular" | custom-call | tf_op jit(solution)/shard_map/jvp()/while/body/eval_jaxpr/vmap(jit(_solve_triangular))/triangular_solve/custom-call.1 | solution.py:118
  136.3 52.4 %while.145 = (s32[]{:T(128)}, f32[4,128,128]{2,1,0:T(8,128)S(1)}, f32[2,4,1,1]{1,3,2,0:T(1,128)}, f32[2,4,64,128]{3,2,1,0:T(8,128)S(1)}, f32[2,4,64,1]{2,1,3,0:T...) while((s32[]{:T(128)}, f32[4,128,128]{2,1,0:T(8,128)S(1)}, ...), condition=%wide.region_9.12_spmd.clone, body=%wide.region_8.11_spmd.clone.sunk | while | flops 201863232 | bytes 3133135 | solution.py:154
  142.0 19.7 %custom-call.48 = f32[4,1,64,64]{2,3,1,0:T(8,128)S(1)} custom-call(f32[4,1,64,64]{3,2,1,0:T(8,128)S(1)} %fusion.677), custom_call_target="InvertDiagBlocksLowerTriangular" | custom-call | tf_op jit(solution)/shard_map/transpose(jvp())/while/body/eval_jaxpr/vmap(jit(_solve_triangular))/triangular_solve/custom-call.0 | solution.py:118
  168.2 19.7 %custom-call.48 = f32[4,1,64,64]{2,3,1,0:T(8,128)S(1)} custom-call(f32[4,1,64,64]{3,2,1,0:T(8,128)S(1)} %fusion.677), custom_call_target="InvertDiagBlocksLowerTriangular" | custom-call | tf_op jit(solution)/shard_map/transpose(jvp())/while/body/eval_jaxpr/vmap(jit(_solve_triangular))/triangular_solve/custom-call.0 | solution.py:118
  237.4 5.4 collective-permute-start.6
  246.2 5.2 collective-permute-start.7
  263.6 10.2 %collective-permute-done.8 = f32[2,128,128]{2,1,0:T(8,128)S(1)} collective-permute-done((f32[2,128,128]{2,1,0:T(8,128)S(1)}, f32[2,128,128]{2,1,0:T(8,128)S(1)}, u32[]{:S(2)}, u32[]{:S(2)}) %collective-permute-start.8) | collective-permute-done | bytes 131104 | tf_op jit(solution)/shard_map/ppermute | solution.py:78
  285.8 9.9 %collective-permute-done.10 = f32[2,128,128]{2,1,0:T(8,128)S(1)} collective-permute-done((f32[2,128,128]{2,1,0:T(8,128)S(1)}, f32[2,128,128]{2,1,0:T(8,128)S(1)}, u32[]{:S(2)}, u32[]{:S(2)}) %collective-permute-start.10) | collective-permute-done | bytes 131104 | tf_op jit(solution)/shard_map/ppermute | solution.py:78
  297.8 5.6 collective-permute-done.11
  304.7 6.1 collective-permute-done.12
  312.8 5.1 all-to-all-start
  317.9 6.0 collective-permute-done.13
  326.7 5.2 all-to-all-start.1
  344.4 7.7 collective-permute-done.15
  382.6 23.8 %all-gather.28.cloned.1.call-done = f32[32,128,128]{2,1,0:T(8,128)} async-done(((f32[4,128,128]{2,1,0:T(8,128)}), f32[32,128,128]{2,1,0:T(8,128)}) %all-gather.28.cloned.1.call-update) | async-done | bytes 2097168 | tf_op jit(solution)/shard_map/all_gather | solution.py:29
  412.8 34.3 %all-gather.32.cloned.1.call-done = f32[32,128,128]{2,1,0:T(8,128)} async-done(((f32[4,128,128]{2,1,0:T(8,128)}), f32[32,128,128]{2,1,0:T(8,128)}) %all-gather.32.cloned.1.call-update) | async-done | bytes 2097168 | tf_op jit(solution)/shard_map/all_gather | solution.py:29
  464.8 84.7 %while.143 = (s32[]{:T(128)}, f32[4,128,128]{2,1,0:T(8,128)S(1)}, f32[2,4,64,64]{3,2,1,0:T(8,128)}, f32[2,4,128,64]{2,3,1,0:T(8,128)}, f32[2,4,64,64]{3,2,1,0:T(...) while((s32[]{:T(128)}, f32[4,128,128]{2,1,0:T(8,128)S(1)}, ...), condition=%wide.region_12.15_spmd.clone.clone, body=%wide.region_10.14_spmd.clone.clone.sunk | while | flops 227234368 | bytes 7799065 | solution.py:154
  474.1 21.0 %custom-call.45 = f32[4,1,64,64]{2,3,1,0:T(8,128)} custom-call(f32[4,1,64,64]{3,2,1,0:T(8,128)} %add_bitcast_fusion.6), custom_call_target="InvertDiagBlocksLowerTriangular" | custom-call | tf_op jit(solution)/shard_map/jvp()/while/body/eval_jaxpr/vmap(jit(_solve_triangular))/triangular_solve/custom-call.1 | solution.py:118
  516.4 21.0 %custom-call.45 = f32[4,1,64,64]{2,3,1,0:T(8,128)} custom-call(f32[4,1,64,64]{3,2,1,0:T(8,128)} %add_bitcast_fusion.6), custom_call_target="InvertDiagBlocksLowerTriangular" | custom-call | tf_op jit(solution)/shard_map/jvp()/while/body/eval_jaxpr/vmap(jit(_solve_triangular))/triangular_solve/custom-call.1 | solution.py:118
  555.9 142.2 %while.144 = (s32[]{:T(128)}, f32[4,128,128]{2,1,0:T(8,128)S(1)}, f32[2,4,64,128]{3,2,0,1:T(8,128)}, f32[2,4,64,128]{3,2,0,1:T(8,128)}, f32[2,4,64,128]{3,2,0,1:...) while((s32[]{:T(128)}, f32[4,128,128]{2,1,0:T(8,128)S(1)}, ...), condition=%wide.region_24.27_spmd.clone.clone, body=%wide.region_13.26_spmd.clone.clone.sunk | while | flops 517469504 | bytes 24436968 | solution.py:154
  566.2 19.7 %custom-call.46 = f32[4,1,64,64]{2,3,1,0:T(8,128)S(1)} custom-call(f32[4,1,64,64]{3,2,1,0:T(8,128)S(1)} %fusion.649), custom_call_target="InvertDiagBlocksLowerTriangular" | custom-call | tf_op jit(solution)/shard_map/transpose(jvp())/while/body/eval_jaxpr/vmap(jit(_solve_triangular))/triangular_solve/custom-call.0 | solution.py:118
  592.0 21.0 %custom-call.47 = f32[4,1,64,64]{2,3,1,0:T(8,128)} custom-call(f32[4,1,64,64]{3,2,1,0:T(8,128)} %add_bitcast_fusion.7), custom_call_target="InvertDiagBlocksLowerTriangular" | custom-call | tf_op jit(solution)/shard_map/transpose(jvp())/while/body/eval_jaxpr/vmap(jit(_solve_triangular))/triangular_solve | solution.py:118
  637.2 19.7 %custom-call.46 = f32[4,1,64,64]{2,3,1,0:T(8,128)S(1)} custom-call(f32[4,1,64,64]{3,2,1,0:T(8,128)S(1)} %fusion.649), custom_call_target="InvertDiagBlocksLowerTriangular" | custom-call | tf_op jit(solution)/shard_map/transpose(jvp())/while/body/eval_jaxpr/vmap(jit(_solve_triangular))/triangular_solve/custom-call.0 | solution.py:118
  663.0 21.0 %custom-call.47 = f32[4,1,64,64]{2,3,1,0:T(8,128)} custom-call(f32[4,1,64,64]{3,2,1,0:T(8,128)} %add_bitcast_fusion.7), custom_call_target="InvertDiagBlocksLowerTriangular" | custom-call | tf_op jit(solution)/shard_map/transpose(jvp())/while/body/eval_jaxpr/vmap(jit(_solve_triangular))/triangular_solve | solution.py:118
  706.7 13.0 %all-gather.8 = f32[8,4,256]{2,1,0:T(4,128)S(1)} all-gather(f32[1,4,256]{2,1,0:T(4,128)S(1)} %maximum_bitcast_fusion), channel_id=1, replica_groups=mesh['seq_0'=8,'seq_1'=4,'head'=8] {'head'}, dimensions={0}, use_global_device_ids=true | all-gather | bytes 36864 | tf_op jit(solution)/shard_map/all_gather | solution.py:42
  723.5 6.9 all-to-all-start.2
  740.8 194.8 %reduce-scatter.2.cloned.1.call-done = f32[8,256]{1,0:T(8,128)} async-done(((f32[8,8192]{1,0:T(8,128)}), f32[8,256]{1,0:T(8,128)}) %reduce-scatter.2.cloned.1.call-update) | async-done | bytes 8208 | tf_op jit(solution)/shard_map/reduce_scatter | solution.py:53
  (715 shorter events, 346.1 us)
Async XLA Ops:
  7.2 183.6 %all-gather.18.cloned.1.call-start = ((), (), s32[]{:S(2)}) async-start(), calls=%async_computation.5 | async-start | bytes 1310720 | tf_op jit(solution)/shard_map/all_gather | solution.py:29
  59.9 191.6 %all-gather.22.cloned.1.call-start = ((), (), s32[]{:S(2)}) async-start(), calls=%async_computation.7 | async-start | bytes 1310720 | tf_op jit(solution)/shard_map/all_gather | solution.py:29
  189.5 86.3 %all-gather.26.cloned.1.call-start = ((), (), s32[]{:S(2)}) async-start(), calls=%async_computation.9 | async-start | bytes 1310720 | tf_op jit(solution)/shard_map/all_gather | solution.py:29
  190.2 163.6 %all-gather.30.cloned.1.call-start = ((), (), s32[]{:S(2)}) async-start(), calls=%async_computation.11 | async-start | bytes 1310720 | tf_op jit(solution)/shard_map/all_gather | solution.py:29
  190.8 172.5 %all-gather.20.cloned.1.call-start = ((), (), s32[]{:S(2)}) async-start(), calls=%async_computation.6 | async-start | bytes 2359296 | tf_op jit(solution)/shard_map/all_gather | solution.py:29
  193.0 28.2 %copy-start.95 = (bf16[128,128]{1,0:T(8,128)(2,1)S(1)}, bf16[128,128]{1,0:T(8,128)(2,1)}, u32[]{:S(2)}) copy-start(bf16[128,128]{1,0:T(8,128)(2,1)} %param.43) | copy-start | bytes 98308
  197.3 175.1 %all-gather.24.cloned.1.call-start = ((), (), s32[]{:S(2)}) async-start(), calls=%async_computation.8 | async-start | bytes 2359296 | tf_op jit(solution)/shard_map/all_gather | solution.py:29
  197.3 5.3 collective-permute-start
  202.6 7.0 collective-permute-start.1
  209.7 7.1 collective-permute-start.2
  216.8 6.3 collective-permute-start.3
  223.1 6.4 collective-permute-start.4
  229.4 7.9 collective-permute-start.5
  237.4 8.8 collective-permute-start.6
  246.2 11.9 %collective-permute-start.7 = (bf16[2,128,128]{2,1,0:T(8,128)(2,1)S(1)}, bf16[2,128,128]{2,1,0:T(8,128)(2,1)S(1)}, u32[]{:S(2)}, u32[]{:S(2)}) collective-permute-start(bf16[2,128,128]{2,1,0:T(8,128)(2,1)S(1)} %collective-permute-done.6), channel_id=1, source_target_pairs={{0,8},{8,16},{16,24},{24,32},{32,40},{40,48},{48,56},{56,64},{64,7... | collective-permute-start | bytes 196616 | tf_op jit(solution)/shard_map/ppermute | solution.py:78
  258.1 148.4 %all-gather.28.cloned.1.call-start = ((), (), s32[]{:S(2)}) async-start(), calls=%async_computation.10 | async-start | bytes 2359296 | tf_op jit(solution)/shard_map/all_gather | solution.py:29
  262.3 11.5 %collective-permute-start.8 = (f32[2,128,128]{2,1,0:T(8,128)S(1)}, f32[2,128,128]{2,1,0:T(8,128)S(1)}, u32[]{:S(2)}, u32[]{:S(2)}) collective-permute-start(f32[2,128,128]{2,1,0:T(8,128)S(1)} %fusion.281), channel_id=1, source_target_pairs={{8,0},{16,8},{24,16},{32,24},{40,32},{48,40},{56,48},{64,56},{72,6... | collective-permute-start | bytes 393224 | tf_op jit(solution)/shard_map/ppermute | solution.py:78
  274.4 9.1 collective-permute-start.9
  284.5 11.2 %collective-permute-start.10 = (f32[2,128,128]{2,1,0:T(8,128)S(1)}, f32[2,128,128]{2,1,0:T(8,128)S(1)}, u32[]{:S(2)}, u32[]{:S(2)}) collective-permute-start(f32[2,128,128]{2,1,0:T(8,128)S(1)} %fusion.285), channel_id=1, source_target_pairs={{8,0},{16,8},{24,16},{32,24},{40,32},{48,40},{56,48},{64,56},{72,6... | collective-permute-start | bytes 393224 | tf_op jit(solution)/shard_map/ppermute | solution.py:78
  296.5 6.9 collective-permute-start.11
  303.4 7.4 collective-permute-start.12
  311.5 12.4 %collective-permute-start.13 = (f32[2,128,128]{2,1,0:T(8,128)}, f32[2,128,128]{2,1,0:T(8,128)}, u32[]{:S(2)}, u32[]{:S(2)}) collective-permute-start(f32[2,128,128]{2,1,0:T(8,128)} %fusion.291), channel_id=1, source_target_pairs={{8,0},{16,8},{24,16},{32,24},{40,32},{48,40},{56,48},{64,56},{72,6... | collective-permute-start | bytes 393224 | tf_op jit(solution)/shard_map/ppermute | solution.py:78
  312.8 14.0 %all-to-all-start = ((bf16[4,8,1024]{2,0,1:T(4,128)(2,1)}), bf16[4,8,1024]{2,0,1:T(4,128)(2,1)}, u32[]{:S(2)}, u32[]{:S(2)}) async-start(bf16[4,8,1024]{2,0,1:T(4,128)(2,1)} %bitcast.933), calls=%async_computation | async-start | bytes 131072 | tf_op jit(solution)/shard_map/all_to_all | solution.py:265
  325.4 12.2 %collective-permute-start.14 = (f32[2,128,128]{2,1,0:T(8,128)}, f32[2,128,128]{2,1,0:T(8,128)}, u32[]{:S(2)}, u32[]{:S(2)}) collective-permute-start(f32[2,128,128]{2,1,0:T(8,128)} %fusion.278), channel_id=1, source_target_pairs={{8,0},{16,8},{24,16},{32,24},{40,32},{48,40},{56,48},{64,56},{72,6... | collective-permute-start | bytes 393224 | tf_op jit(solution)/shard_map/ppermute | solution.py:78
  326.7 9.5 %all-to-all-start.1 = ((bf16[4,8,1024]{2,0,1:T(4,128)(2,1)}), bf16[4,8,1024]{2,0,1:T(4,128)(2,1)}, u32[]{:S(2)}, u32[]{:S(2)}) async-start(bf16[4,8,1024]{2,0,1:T(4,128)(2,1)} %bitcast.938), calls=%async_computation.1 | async-start | bytes 131072 | tf_op jit(solution)/shard_map/all_to_all | solution.py:266
  331.9 115.2 %all-gather.32.cloned.1.call-start = ((), (), s32[]{:S(2)}) async-start(), calls=%async_computation.12 | async-start | bytes 2359296 | tf_op jit(solution)/shard_map/all_gather | solution.py:29
  339.3 12.9 %collective-permute-start.15 = (f32[2,128,128]{2,1,0:T(8,128)}, f32[2,128,128]{2,1,0:T(8,128)}, u32[]{:S(2)}, u32[]{:S(2)}) collective-permute-start(f32[2,128,128]{2,1,0:T(8,128)} %fusion.292), channel_id=1, source_target_pairs={{8,0},{16,8},{24,16},{32,24},{40,32},{48,40},{56,48},{64,56},{72,6... | collective-permute-start | bytes 393224 | tf_op jit(solution)/shard_map/ppermute | solution.py:78
  360.5 575.2 %reduce-scatter.2.cloned.1.call-start = ((), (), s32[]{:S(2)}) async-start(), calls=%async_computation.4 | async-start | bytes 270336 | tf_op jit(solution)/shard_map/reduce_scatter | solution.py:53
  590.3 30.0 %copy-start.17 = (f32[2,4,64,64]{3,2,1,0:T(8,128)S(1)}, f32[2,4,64,64]{3,2,1,0:T(8,128)}, u32[]{:S(2)}) copy-start(f32[2,4,64,64]{3,2,1,0:T(8,128)} %copy-done.16) | copy-start | bytes 393220 | tf_op jit(solution)/shard_map/transpose(jvp())/while
  661.3 30.0 %copy-start.17 = (f32[2,4,64,64]{3,2,1,0:T(8,128)S(1)}, f32[2,4,64,64]{3,2,1,0:T(8,128)}, u32[]{:S(2)}) copy-start(f32[2,4,64,64]{3,2,1,0:T(8,128)} %copy-done.16) | copy-start | bytes 393220 | tf_op jit(solution)/shard_map/transpose(jvp())/while
  706.7 23.7 %copy-start.84 = (bf16[32,1024]{1,0:T(8,128)(2,1)S(1)}, bf16[32,1024]{1,0:T(8,128)(2,1)}, u32[]{:S(2)}) copy-start(bf16[32,1024]{1,0:T(8,128)(2,1)} %all_to_all.35) | copy-start | bytes 196612
  723.5 16.7 %all-to-all-start.2 = ((f32[32,1,8]{2,1,0:T(1,128)}), f32[32,1,8]{2,1,0:T(1,128)S(1)}, u32[]{:S(2)}, u32[]{:S(2)}) async-start(f32[32,1,8]{2,1,0:T(1,128)} %broadcast_in_dim.398), calls=%async_computation.3 | async-start | bytes 32768 | tf_op jit(solution)/shard_map/all_to_all | solution.py:59
  (134 other events, 546.3 us)
Sparse Core Ops, SparseCore 0:
  60.0 29.5 all-gather.17
  189.6 29.8 all-gather.21
  221.3 27.4 all-gather.25
  250.4 29.3 all-gather.29
  282.0 43.4 all-gather.19
  327.2 41.0 all-gather.23
  370.1 36.3 all-gather.27
  408.3 38.7 all-gather.31
  721.6 214.0 reduce-scatter.1
where the time goes:
time: 956 us; the launch traced here: 944 us
  waiting for transfers between devices  325 us (34%)
  other arithmetic  287 us (30%)
  matrix products  140 us (15%)
  local copies, waits for them, and re-layouts  98.8 us (10%)
  starting transfers between devices  63.6 us (7%)
  between operations  15.8 us (2%)
  blocking collectives  13 us (1%)
    another operation x46, other arithmetic, stretch_step(): jax.scipy.linalg.solve_triangular(system_mat, right_side, lower=True, uni...  250 us
    reduce_scatter x1, waiting for transfers between devices, side_by_side(): result = lax.psum_scatter(both, axis, scatter_dimension=dim, tiled=True)  195 us
    dot_general x60, matrix products, dot_high(): return jnp.matmul(left_mat, right_mat, precision=PRECISE)  64.4 us
    ppermute x16, waiting for transfers between devices, shifted(): return lax.ppermute(value, axis, pairs)  63.9 us
    all_gather x8, waiting for transfers between devices, carried_in(): pieces = jax.tree.map(lambda part: lax.all_gather(part, axis), so_far)  58.2 us
    dot_general x58, matrix products, chain_mul(): return jnp.einsum('hij,hjk->hik', left_mat, right_mat, precision=PRECISE)  52.6 us
    ppermute x16, starting transfers between devices, shifted(): return lax.ppermute(value, axis, pairs)  45.9 us
    unnamed x185, local copies, waits for them, and re-layouts  27.6 us
  transfers between devices with their start and end apart: 28, of which 19 were waited for; matrix products, arithmetic and copies ran while one was open for 21% of the time, Pallas kernels for 0%

commit v1 on v0

v1 whole, which is shorter than its diff:
```python
import math

import jax
import jax.numpy as jnp
from jax import lax
from jax.experimental import pallas as pl
from jax.experimental.pallas import tpu as pltpu
from jax.sharding import Mesh
from jax.sharding import PartitionSpec as P

WINDOW = 1024
T = 128
SEQ = ("seq_0", "seq_1")
F32 = jnp.float32
BF16 = jnp.bfloat16
NN = (((1,), (0,)), ((), ()))
NT = (((1,), (1,)), ((), ()))
TN = (((0,), (0,)), ((), ()))


def split(value):
    high = value.astype(BF16)
    return high, (value - high.astype(F32)).astype(BF16)


def split3(value):
    high = value.astype(BF16)
    rest = value - high.astype(F32)
    mid = rest.astype(BF16)
    return high, mid, (rest - mid.astype(F32)).astype(BF16)


def mm(left, right, dims):
    lefts = left if isinstance(left, tuple) else (left,)
    rights = right if isinstance(right, tuple) else (right,)
    total = None
    for i, a in enumerate(lefts):
        for j, b in enumerate(rights):
            if i + j < max(len(lefts), len(rights)):
                term = lax.dot_general(a, b, dims, preferred_element_type=F32)
                total = term if total is None else total + term
    return total


def ids(shape):
    return (
        lax.broadcasted_iota(jnp.int32, shape, 0),
        lax.broadcasted_iota(jnp.int32, shape, 1),
    )


def place(columns, lane):
    result = jnp.zeros((T, T), F32)
    for at, column in enumerate(columns):
        result = jnp.where(lane == at, column, result)
    return result


def prepare_kernel(
    x_ref, w_ref, rate_ref, bias_ref, q_ref, k_ref, v_ref, g_ref,
    maps_ref, inv_ref, ratio_ref, rk_ref, p_ref, w_out_ref, y_ref, du_ref, rows_ref, cols_ref,
):
    heads = maps_ref.shape[0]
    row, lane = ids((T, T))
    lower, strict = row >= lane, row > lane
    eye = jnp.where(row == lane, 1.0, 0.0)
    logits = lax.dot_general(w_ref[...], x_ref[...], NT, preferred_element_type=F32)
    rates = jnp.concatenate([jnp.full((1, T), rate_ref[h], F32) for h in range(heads)], axis=0)
    biases = jnp.concatenate([jnp.full((1, T), bias_ref[h], F32) for h in range(heads)], axis=0)
    beta_row = jax.nn.sigmoid(logits[:heads])
    shifted = logits[heads:] + biases
    soft = jnp.maximum(shifted, 0.0) + jnp.log1p(jnp.exp(-jnp.abs(shifted)))
    decay_row = -jnp.exp(rates) * soft
    upper_ones = jnp.where(row <= lane, 1.0, 0.0).astype(BF16)
    cum_row = mm(split3(decay_row), upper_ones, NN)
    gate_slope = -jnp.exp(rates) * jax.nn.sigmoid(shifted)
    packed = jnp.concatenate(
        [beta_row, cum_row, jnp.zeros((T - 2 * heads, T), F32)], axis=0
    )
    turned = packed.T
    hs = range(heads)
    span = [slice(h * T, (h + 1) * T) for h in hs]
    k = [k_ref[:, span[h]] for h in hs]
    q = [q_ref[:, span[h]] for h in hs]
    v = [v_ref[:, span[h]] for h in hs]
    g = [g_ref[:, span[h]] for h in hs]
    beta_c = [turned[:, h : h + 1] for h in hs]
    cum_c = [turned[:, heads + h : heads + h + 1] for h in hs]
    norm_k, norm_q = [], []
    for h in hs:
        kf, qf = k[h].astype(F32), q[h].astype(F32)
        norm_k.append(lax.rsqrt(jnp.sum(kf * kf, axis=1, keepdims=True) + 1e-6))
        norm_q.append(
            lax.rsqrt(jnp.sum(qf * qf, axis=1, keepdims=True) + 1e-6)
        )
    norms = place(norm_k + norm_q, lane)
    norm_rows = norms.T
    norm_k_row = norm_rows[:heads]
    norm_q_row = norm_rows[heads : 2 * heads]
    last = cum_row[:, T - 1 : T]
    rows_ref[...] = jnp.concatenate(
        [beta_row, cum_row, norm_k_row, norm_q_row, decay_row, gate_slope], axis=0
    )
    col_list = beta_c + cum_c + norm_k + norm_q
    cols_ref[...] = place(col_list, lane)
    scale = 1.0 / math.sqrt(T)
    ratio, solve, low = [], [], []
    for h in hs:
        r = jnp.where(
            lower, jnp.exp(jnp.where(lower, cum_c[h] - cum_row[h : h + 1], 0.0)), 0.0
        )
        ratio.append(r)
        ratio_ref[h] = r
        kk = mm(k[h], k[h], NT) * norm_k[h] * norm_k_row[h : h + 1]
        rk = jnp.where(strict, r * kk, 0.0)
        rk_ref[h] = rk
        low.append(rk * beta_c[h])
    for h in hs:
        same = (row // 2) == (lane // 2)
        solve.append(jnp.where(same, -low[h], 0.0) + eye)
    size = 2
    while size < T:
        block = (row // (2 * size) == lane // (2 * size)) & (row // size != lane // size)
        parts = [split(s) for s in solve]
        corner = [split(jnp.where(block, low[h], 0.0)) for h in hs]
        inner = [split(mm(corner[h], parts[h], NN)) for h in hs]
        solve = [solve[h] - mm(parts[h], inner[h], NN) for h in hs]
        size *= 2
    for h in hs:
        inv_ref[h] = solve[h]
        grow_c, grow_row = jnp.exp(cum_c[h]), jnp.exp(cum_row[h : h + 1])
        end = last[h : h + 1]
        tail_c = jnp.exp(end - cum_c[h])
        bv = beta_row[h : h + 1]
        w = mm(split(solve[h] * bv), v[h], NN)
        y = mm(split(solve[h] * (bv * grow_row * norm_k_row[h : h + 1])), k[h], NN)
        w_out_ref[h] = w
        y_ref[h] = y
        p = ratio[h] * mm(q[h], k[h], NT) * (norm_q[h] * scale) * norm_k_row[h : h + 1]
        p_ref[h] = p
        du = mm(split(p), g[h], TN)
        du_ref[h] = du
        out_scale = tail_c * norm_k[h]
        maps_ref[h, 0] = jnp.exp(end) * eye - mm(k[h], split(out_scale * y), TN)
        maps_ref[h, 1] = mm(k[h], split(out_scale * w), TN)
        own = mm(q[h], split((grow_c * norm_q[h] * scale) * g[h].astype(F32)), TN)
        maps_ref[h, 2] = own - mm(split(y), split(du), TN)


def group_kernel(maps_ref, up_ref, down_ref):
    phi = [split(maps_ref[x, 0]) for x in range(4)]
    off = [maps_ref[x, 1] for x in range(4)]
    loc = [maps_ref[x, 2] for x in range(4)]
    first = split(mm(phi[1], phi[0], NN))
    second = split(mm(phi[3], phi[2], NN))
    off_a = mm(phi[1], split(off[0]), NN) + off[1]
    off_b = mm(phi[3], split(off[2]), NN) + off[3]
    loc_a = mm(phi[0], split(loc[1]), TN) + loc[0]
    loc_b = mm(phi[2], split(loc[3]), TN) + loc[2]
    whole = mm(second, first, NN)
    up_ref[0] = whole
    down_ref[0] = whole
    up_ref[1] = mm(second, split(off_a), NN) + off_b
    down_ref[1] = mm(first, split(loc_b), TN) + loc_a


def pair_kernel(at_ref, up_ref, down_ref, from_up_ref, from_down_ref, up_out_ref, down_out_ref):
    z, count = at_ref[0], at_ref[1]
    own = split(up_ref[0])
    has_up, has_down = z >= 1, z < count - 1
    up_out_ref[0] = jnp.where(has_up, mm(own, split(from_up_ref[0]), NN), up_ref[0])
    up_out_ref[1] = jnp.where(
        has_up, mm(own, split(from_up_ref[1]), NN) + up_ref[1], up_ref[1]
    )
    down_out_ref[0] = jnp.where(has_down, mm(split(from_down_ref[0]), own, NN), down_ref[0])
    down_out_ref[1] = jnp.where(
        has_down, mm(own, split(from_down_ref[1]), TN) + down_ref[1], down_ref[1]
    )


def reach_kernel(
    at_ref, start_ref, end_ref, up_ref, down_ref, from_up_ref, from_down_ref, leave_ref, enter_ref
):
    z, count, x = at_ref[0], at_ref[1], at_ref[2]
    start, end = start_ref[x], end_ref[x]
    ahead = mm(split(from_up_ref[0]), split(start), NN) + from_up_ref[1]
    state = jnp.where(z >= 2, ahead, start)
    leave_ref[...] = mm(split(up_ref[0]), split(state), NN) + up_ref[1]
    behind = mm(split(from_down_ref[0]), split(end), TN) + from_down_ref[1]
    grad = jnp.where(z < count - 2, behind, end)
    enter_ref[...] = mm(split(down_ref[0]), split(grad), TN) + down_ref[1]


def spread_kernel(
    at_ref, start_ref, end_ref, leave_ref, enter_ref, up2_ref, down2_ref, up1_ref, down1_ref,
    maps_ref, out_ref,
):
    z, count, x = at_ref[0], at_ref[1], at_ref[2]
    state = jnp.where(z >= 4, leave_ref[...], start_ref[x])
    grad = jnp.where(z < count - 4, enter_ref[...], end_ref[x])
    state_two = mm(split(up2_ref[0]), split(state), NN) + up2_ref[1]
    grad_two = mm(split(down2_ref[0]), split(grad), TN) + down2_ref[1]
    state = jnp.where(z >= 2, state_two, state)
    grad = jnp.where(z < count - 2, grad_two, grad)
    state_one = mm(split(up1_ref[0]), split(state), NN) + up1_ref[1]
    grad_one = mm(split(down1_ref[0]), split(grad), TN) + down1_ref[1]
    state = jnp.where(z >= 1, state_one, state)
    grad = jnp.where(z < count - 1, grad_one, grad)
    for step in range(4):
        back = 3 - step
        out_ref[step, 0] = state
        out_ref[back, 1] = grad
        if step < 3:
            state = mm(split(maps_ref[step, 0]), split(state), NN) + maps_ref[step, 1]
            grad = mm(split(maps_ref[back, 0]), split(grad), TN) + maps_ref[back, 2]


def finish_kernel(
    ends_ref, maps_ref, q_ref, k_ref, v_ref, g_ref, inv_ref, ratio_ref, rk_ref, p_ref, w_ref,
    y_ref, du_ref, rows_ref, cols_ref,
    dq_ref, dk_ref, dv_ref, bound_ref, logit_ref, param_ref,
):
    heads = maps_ref.shape[0]
    hs = range(heads)
    row, lane = ids((T, T))
    strict = row > lane
    scale = 1.0 / math.sqrt(T)
    cols, rows = cols_ref[...], rows_ref[...]
    decay_cols, beta_cols, decay_rows, ends = [], [], [], []
    for h in hs:
        span = slice(h * T, (h + 1) * T)
        q, k, g = q_ref[:, span], k_ref[:, span], g_ref[:, span]
        qf, kf, vf = q.astype(F32), k.astype(F32), v_ref[:, span].astype(F32)
        beta = cols[:, h : h + 1]
        cum = cols[:, heads + h : heads + h + 1]
        norm_k = cols[:, 2 * heads + h : 2 * heads + h + 1]
        norm_q = cols[:, 3 * heads + h : 3 * heads + h + 1]
        norm_k_row = rows[2 * heads + h : 2 * heads + h + 1]
        norm_q_row = rows[3 * heads + h : 3 * heads + h + 1]
        end = rows[heads + h : heads + h + 1, T - 1 : T]
        grow, tail = jnp.exp(cum), jnp.exp(end - cum)
        m0, d = ends_ref[h, 0], ends_ref[h, 1]
        m_parts, d_parts = split(m0), split(d)
        u = w_ref[h] - mm(split(y_ref[h]), m_parts, NN)
        du = du_ref[h] + (tail * norm_k) * mm(k, d_parts, NN)
        u_parts = split(u)
        db = mm(split(inv_ref[h]), split(du), TN)
        db_parts = split(db)
        bound_ref[0, h] = mm(split(maps_ref[h, 0]), d_parts, TN) + maps_ref[h, 2]
        km = norm_k * mm(k, m_parts, NN)
        z = vf - grow * km
        dv_ref[:, span] = beta * db
        kn = norm_k * kf
        qn = (norm_q * scale) * qf
        dkn = -(beta * grow) * mm(db_parts, m_parts, NT)
        da = jnp.where(strict, -mm(db_parts, u_parts, NT), 0.0)
        ratio = ratio_ref[h]
        rka = da * rk_ref[h]
        hm = beta * ratio * da
        dkn = dkn + mm(split((hm + hm.T) * norm_k_row), k, NN)
        dp = mm(g, u_parts, NT)
        ds = ratio * dp
        dqn = mm(split(ds * norm_k_row), k, NN)
        dkn = dkn + mm(split(ds * (norm_q * scale)), q, TN)
        dom = mm(g, m_parts, NT)
        dqn = dqn + grow * dom
        dkt = tail * mm(u_parts, d_parts, NT)
        dkn = dkn + dkt
        both = beta * rka + dp * p_ref[h]
        tails = dkt * kn
        decay_cols.append(
            jnp.sum(both + grow * (dom * qn - beta * (db * km)) - tails, axis=1, keepdims=True)
        )
        beta_cols.append(jnp.sum(db * z + rka, axis=1, keepdims=True))
        decay_rows.append(jnp.sum(both, axis=0, keepdims=True))
        last = jnp.sum(
            jnp.sum(jnp.exp(end) * (d * m0) + tails, axis=0, keepdims=True), axis=1, keepdims=True
        )
        ends.append(jnp.broadcast_to(last, (1, T)))
        dot_q = jnp.sum(qf * dqn, axis=1, keepdims=True)
        dot_k = jnp.sum(kf * dkn, axis=1, keepdims=True)
        dq_ref[:, span] = (norm_q * scale) * (dqn - qf * (norm_q * norm_q * dot_q))
        dk_ref[:, span] = norm_k * (dkn - kf * (norm_k * norm_k * dot_k))
    turned = place(decay_cols + beta_cols, lane).T
    lane_one = lane[:heads]
    dcum = turned[:heads] - jnp.concatenate(decay_rows, axis=0)
    dcum = dcum + jnp.where(lane_one == T - 1, jnp.concatenate(ends, axis=0), 0.0)
    lower_ones = jnp.where(row >= lane, 1.0, 0.0).astype(BF16)
    ddecay = mm(split3(dcum), lower_ones, NN)
    beta_row = rows[:heads]
    dbeta = turned[heads : 2 * heads] * beta_row * (1.0 - beta_row)
    dshift = ddecay * rows[5 * heads : 6 * heads]
    logit_ref[...] = jnp.concatenate([dbeta, dshift], axis=0)
    rate_sum = jnp.sum(ddecay * rows[4 * heads : 5 * heads], axis=1, keepdims=True)
    bias_sum = jnp.sum(dshift, axis=1, keepdims=True)
    param_ref[...] = jnp.broadcast_to(
        jnp.concatenate([rate_sum, bias_sum], axis=0), (2 * heads, T)
    )


def window_kernel(at_ref, q_ref, g_ref, kv_ref, dq_ref, dkv_ref):
    z, x = at_ref[0], at_ref[2]
    row, lane = ids((T, T))
    gap = row - lane
    scale = 1.0 / math.sqrt(T)
    q, g = q_ref[...], g_ref[...]
    scores, slopes = [], []
    tiles = [(a, b) for a in range(4) for b in range(3)]
    for a, b in tiles:
        spread = gap + (x - a + 4 * b) * T
        ok = (spread >= 0) & (spread < jnp.where(z >= b, WINDOW, 0))
        s = lax.dot_general(q, kv_ref[a, b, 0], NT, preferred_element_type=F32) * scale
        scores.append(jnp.where(ok, s, -1e30))
    top = scores[0]
    for s in scores[1:]:
        top = jnp.maximum(top, s)
    top = jnp.max(top, axis=1, keepdims=True)
    weights = [jnp.exp(s - top) for s in scores]
    total = weights[0]
    for w in weights[1:]:
        total = total + w
    total = 1.0 / jnp.sum(total, axis=1, keepdims=True)
    weights = [w * total for w in weights]
    terms = None
    for (a, b), w in zip(tiles, weights):
        slope = lax.dot_general(g, kv_ref[a, b, 1], NT, preferred_element_type=F32)
        slopes.append(slope)
        terms = w * slope if terms is None else terms + w * slope
    terms = jnp.sum(terms, axis=1, keepdims=True)
    dq = None
    for (a, b), w, slope in zip(tiles, weights, slopes):
        ds = split(w * (slope - terms) * scale)
        part = mm(ds, kv_ref[a, b, 0], NN)
        dq = part if dq is None else dq + part
        dkv_ref[a, b, 0] = mm(ds, q, TN)
        dkv_ref[a, b, 1] = mm(split(w), g, TN)
    dq_ref[...] = dq


def input_kernel(d_ref, w_ref, out_ref):
    high, low = split(d_ref[...])
    w = w_ref[...]
    out_ref[...] = lax.dot_general(high, w, TN, preferred_element_type=F32) + lax.dot_general(
        low, w, TN, preferred_element_type=F32
    )


def weight_kernel(d_ref, param_ref, x_ref, out_ref):
    high, low = split(d_ref[...])
    pieces = out_ref.shape[0]
    width = x_ref.shape[1] // pieces
    for s in range(pieces):
        x = x_ref[:, s * width : (s + 1) * width]
        out_ref[s, :, :width] = lax.dot_general(
            high, x, NN, preferred_element_type=F32
        ) + lax.dot_general(low, x, NN, preferred_element_type=F32)
        out_ref[s, :, width:] = param_ref[...]


VM = pl.BlockSpec(memory_space=pltpu.VMEM)
SM = pl.BlockSpec(memory_space=pltpu.SMEM)


def f32(*shape):
    return jax.ShapeDtypeStruct(shape, F32)


def call(kernel, outs, specs, *args, flops=10**8):
    return pl.pallas_call(
        kernel,
        out_shape=outs,
        in_specs=specs,
        out_specs=jax.tree.map(lambda _: VM, outs),
        cost_estimate=pl.CostEstimate(flops=flops, bytes_accessed=4 * 10**6, transcendentals=0),
    )(*args)


def up_by(value, by, count):
    pairs = [(i, i + by) for i in range(count) if 0 <= i + by < count]
    return lax.ppermute(value, "seq_0", pairs)


def shards(
    layer_input, beta_weight, decay_weight, log_rate, decay_bias, delta_query, delta_key,
    delta_value, delta_out_grad, state_init, state_grad_next, attn_query, attn_key, attn_value,
    attn_out_grad,
):
    z_count, x_count = lax.axis_size("seq_0"), lax.axis_size("seq_1")
    head_count = lax.axis_size("head")
    heads = beta_weight.shape[0]
    width = layer_input.shape[1]
    at = jnp.stack(
        [lax.axis_index("seq_0"), jnp.int32(z_count), lax.axis_index("seq_1")]
    ).astype(jnp.int32)

    pair = jnp.stack([attn_key, attn_value])
    near, far = up_by(pair, 1, z_count), up_by(pair, 2, z_count)
    both_weights = jnp.concatenate([beta_weight, decay_weight], axis=0)

    maps, inv, ratio, rk, p, w, y, du, rows, cols = call(
        prepare_kernel,
        (f32(heads, 3, T, T),) + (f32(heads, T, T),) * 7 + (f32(6 * heads, T), f32(T, T)),
        [VM, VM, SM, SM, VM, VM, VM, VM],
        layer_input, both_weights, log_rate, decay_bias, delta_query, delta_key, delta_value,
        delta_out_grad,
    )
    blocks = lax.all_to_all(maps, "seq_1", split_axis=0, concat_axis=0, tiled=True)

    triple = jnp.stack([pair, near, far])
    copies = jnp.broadcast_to(triple[None], (x_count, *triple.shape))
    window = lax.all_to_all(copies, "seq_1", split_axis=0, concat_axis=0, tiled=True)
    weight_cols = jnp.swapaxes(both_weights.reshape(2 * heads, head_count, -1), 0, 1)
    weight_cols = lax.all_to_all(weight_cols, "head", split_axis=0, concat_axis=0, tiled=True)
    weight_cols = weight_cols.reshape(head_count * 2 * heads, -1)

    dq_attn, dkv = call(
        window_kernel,
        (f32(T, T), f32(x_count, 3, 2, T, T)),
        [SM, VM, VM, VM],
        at, attn_query, attn_out_grad, window,
    )

    up, down = call(group_kernel, (f32(2, T, T), f32(2, T, T)), [VM], blocks)
    up1, down1 = up_by(up, 1, z_count), up_by(down, -1, z_count)
    up, down = call(
        pair_kernel, (f32(2, T, T), f32(2, T, T)), [SM, VM, VM, VM, VM], at, up, down, up1, down1
    )
    up2, down2 = up_by(up, 2, z_count), up_by(down, -2, z_count)
    leave, enter = call(
        reach_kernel,
        (f32(T, T), f32(T, T)),
        [SM, VM, VM, VM, VM, VM, VM],
        at, state_init, state_grad_next, up, down, up2, down2,
    )
    leave, enter = up_by(leave, 4, z_count), up_by(enter, -4, z_count)
    ends = call(
        spread_kernel,
        f32(x_count, 2, T, T),
        [SM] + [VM] * 9,
        at, state_init, state_grad_next, leave, enter, up2, down2, up1, down1, blocks,
    )
    ends = lax.all_to_all(ends, "seq_1", split_axis=0, concat_axis=0, tiled=True)

    dkv = lax.all_to_all(dkv, "seq_1", split_axis=0, concat_axis=0, tiled=True)
    dkv = jnp.sum(dkv, axis=0)
    dkv_near, dkv_far = up_by(dkv[1], -1, z_count), up_by(dkv[2], -2, z_count)

    dq, dk, dv, bound, logit, param = call(
        finish_kernel,
        (f32(T, heads * T),) * 3 + (f32(1, heads, T, T), f32(2 * heads, T), f32(2 * heads, T)),
        [VM] * 15,
        ends, maps, delta_query, delta_key, delta_value, delta_out_grad, inv, ratio, rk, p, w, y,
        du, rows, cols,
    )
    logit_copies = jnp.broadcast_to(logit[None], (head_count, *logit.shape))
    every = lax.all_to_all(logit_copies, "head", split_axis=0, concat_axis=0, tiled=True)
    pieces = z_count * x_count
    terms = call(
        weight_kernel,
        f32(pieces, 2 * heads, width // pieces + T),
        [VM, VM, VM],
        logit, param, layer_input,
    )
    terms = lax.all_to_all(terms, SEQ, split_axis=0, concat_axis=0, tiled=True)
    input_grad = call(
        input_kernel,
        f32(T, weight_cols.shape[1]),
        [VM, VM],
        every.reshape(-1, T), weight_cols,
    )
    terms = jnp.sum(terms, axis=0)
    part = width // pieces
    total = dkv[0] + dkv_near + dkv_far
    return (
        dq, dk, dv, bound, input_grad,
        terms[:heads, :part], terms[heads:, :part],
        terms[:heads, part], terms[heads:, part],
        dq_attn, total[0], total[1],
    )


def solution(mesh):
    torus = Mesh(mesh.devices.reshape(8, 4, mesh.shape["head"]), ("seq_0", "seq_1", "head"))
    tokens, by_head = P(SEQ, "head"), P("head", None, None)
    in_specs = (
        P(SEQ, None), P("head", None), P("head", None), P("head"), P("head"),
        tokens, tokens, tokens, tokens, by_head, by_head, tokens, tokens, tokens, tokens,
    )
    out_specs = (
        tokens, tokens, tokens, P(SEQ, "head", None, None), tokens,
        P("head", SEQ), P("head", SEQ), P("head"), P("head"), tokens, tokens, tokens,
    )
    return jax.shard_map(
        shards, mesh=torus, in_specs=in_specs, out_specs=out_specs, check_vma=False
    )
```

time: 956 us -> 160 us (0.17)
  other arithmetic: 287 us -> 2.39 us
  waiting for transfers between devices: 325 us -> 51.7 us
  matrix products: 140 us -> 0 us
  local copies, waits for them, and re-layouts: 98.8 us -> 7.18 us
  Pallas kernels: 0 us -> 34.5 us
  between operations: 15.8 us -> 0.86 us
  blocking collectives: 13 us -> 0 us
    another operation x63 -> x3, other arithmetic: 254 us -> 0.62 us  [the longest x1 0.59 us: shards(): jnp.stack([lax.axis_index('seq_0'), jnp.int32(z_count), lax.axis_index('s...]
    reduce_scatter x1 -> x0, waiting for transfers between devices: 195 us -> none  [side_by_side(): result = lax.psum_scatter(both, axis, scatter_dimension=dim, tiled=True)]
    dot_general x128 -> x0, matrix products: 129 us -> none  [the longest x60 64.4 us: dot_high(): return jnp.matmul(left_mat, right_mat, precision=PRECISE)]
    all_gather x8 -> x0, waiting for transfers between devices: 58.2 us -> none  [carried_in(): pieces = jax.tree.map(lambda part: lax.all_gather(part, axis), so_far)]
    pallas_call x0 -> x9, Pallas kernels: none -> 34.5 us  [call(): pl.pallas_call(kernel, out_shape=outs, in_specs=specs, out_specs=jax.tree...]
    ppermute x16 -> x10, waiting for transfers between devices: 63.9 us -> 37.2 us  [up_by(): return lax.ppermute(value, 'seq_0', pairs)]
    unnamed x185 -> x26, local copies, waits for them, and re-layouts: 27.6 us -> 2.77 us
    another operation x26 -> x0, local copies, waits for them, and re-layouts: 16.7 us -> none
  transfers between devices with their start and end apart: 28 -> 17, of which waited for: 19 -> 12; matrix products, arithmetic and copies ran while one was open for 21% -> 1% of each run, Pallas kernels for 0% -> 22%
where the time goes in v1:
time: 160 us; the launch traced here: 157 us
  starting transfers between devices  60.3 us (38%)
  waiting for transfers between devices  51.7 us (32%)
  Pallas kernels  34.5 us (22%)
  local copies, waits for them, and re-layouts  7.18 us (4%)
  other arithmetic  2.39 us (1%)
    ppermute x10, waiting for transfers between devices, up_by(): return lax.ppermute(value, 'seq_0', pairs)  37.2 us
    pallas_call x9, Pallas kernels, call(): pl.pallas_call(kernel, out_shape=outs, in_specs=specs, out_specs=jax.tree...  34.5 us
    ppermute x10, starting transfers between devices, up_by(): return lax.ppermute(value, 'seq_0', pairs)  30.6 us
    all_to_all x1, waiting for transfers between devices, shards(): dkv = lax.all_to_all(dkv, 'seq_1', split_axis=0, concat_axis=0, tiled=True)  8.01 us
    all_to_all x1, starting transfers between devices, shards(): lax.all_to_all(weight_cols, 'head', split_axis=0, concat_axis=0, tiled=True)  5.44 us
    all_to_all x1, starting transfers between devices, shards(): lax.all_to_all(logit_copies, 'head', split_axis=0, concat_axis=0, tiled=T...  4.8 us
    all_to_all x1, starting transfers between devices, shards(): lax.all_to_all(ends, 'seq_1', split_axis=0, concat_axis=0, tiled=True)  4.76 us
    all_to_all x1, waiting for transfers between devices, shards(): lax.all_to_all(ends, 'seq_1', split_axis=0, concat_axis=0, tiled=True)  4.02 us
  transfers between devices with their start and end apart: 17, of which 12 were waited for; matrix products, arithmetic and copies ran while one was open for 1% of the time, Pallas kernels for 22%

profile of v1, /device:TPU:8, one launch (start us, length us, event | category | flops | bytes accessed | tf_op | source)
XLA Modules:
  0.0 156.9 jit_solution(9926991363853638618)
XLA Ops:
  0.6 1.6 %pad_maximum_fusion.1.w_ref = bf16[8,8192]{1,0:T(8,128)(2,1)} fusion(bf16[4,8192]{1,0:T(4,128)(2,1)} %param.17, bf16[4,8192]{1,0:T(4,128)(2,1)} %param.16), kind=kLoop, calls=%fused_computation.6 | loop fusion | flops 262144 | bytes 262144 | tf_op jit(solution)/shard_map/concatenate | solution.py:398
  2.2 5.4 %all-to-all-start.3 = ((bf16[8,8,1024]{2,1,0:T(8,128)(2,1)}), bf16[8,8,1024]{2,1,0:T(8,128)(2,1)S(1)}, u32[]{:S(2)}, u32[]{:S(2)}) async-start(bf16[8,8,1024]{2,1,0:T(8,128)(2,1)} %bitcast.4), calls=%async_computation.3 | async-start | bytes 262144 | tf_op jit(solution)/shard_map/all_to_all | solution.py:413
  7.7 8.6 %shard_map.238 = (f32[4,3,128,128]{3,2,1,0:T(8,128)}, f32[4,128,128]{2,1,0:T(8,128)}, f32[4,128,128]{2,1,0:T(8,128)}, f32[4,128,128]{2,1,0:T(8,128)}, f32[4,128,...) custom-call(bf16[128,8192]{1,0:T(8,128)(2,1)} %x_ref.3, ...), custom_call_target="tpu_custom_call" | custom-call | flops 100000000 | bytes 4000000 | tf_op jit(solution)/shard_map/pallas_call | solution.py:369
  16.3 3.8 %all-to-all-start = ((f32[4,3,128,128]{3,2,1,0:T(8,128)}), f32[4,3,128,128]{3,2,1,0:T(8,128)S(1)}, u32[]{:S(2)}, u32[]{:S(2)}) async-start(f32[4,3,128,128]{3,2,1,0:T(8,128)} %get-tuple-element.36.maps_ref), calls=%async_computation | async-start | bytes 1572864 | tf_op jit(solution)/shard_map/all_to_all | solution.py:407
  20.1 5.2 %collective-permute-start.7 = (bf16[2,128,128]{2,1,0:T(8,128)(2,1)S(1)}, bf16[2,128,128]{2,1,0:T(8,128)(2,1)S(1)}, u32[]{:S(2)}, u32[]{:S(2)}) collective-permute-start(bf16[2,128,128]{2,1,0:T(8,128)(2,1)S(1)} %get-tuple-element.67), channel_id=1, source_target_pairs={{0,64},{32,96},{64,128},{96,160},{128,192},{160,224},{1,65},{33,97... | collective-permute-start | bytes 196616 | tf_op jit(solution)/shard_map/ppermute | solution.py:380
  25.3 3.8 %collective-permute-start.6 = (bf16[2,128,128]{2,1,0:T(8,128)(2,1)S(1)}, bf16[2,128,128]{2,1,0:T(8,128)(2,1)S(1)}, u32[]{:S(2)}, u32[]{:S(2)}) collective-permute-start(bf16[2,128,128]{2,1,0:T(8,128)(2,1)S(1)} %get-tuple-element.67), channel_id=1, source_target_pairs={{0,32},{32,64},{64,96},{96,128},{128,160},{160,192},{192,224},{1,3... | collective-permute-start | bytes 196616 | tf_op jit(solution)/shard_map/ppermute | solution.py:380
  29.1 1.9 %collective-permute-done.6 = bf16[2,128,128]{2,1,0:T(8,128)(2,1)S(1)} collective-permute-done((bf16[2,128,128]{2,1,0:T(8,128)(2,1)S(1)}, bf16[2,128,128]{2,1,0:T(8,128)(2,1)S(1)}, u32[]{:S(2)}, u32[]{:S(2)}) %collective-permute-start.6) | collective-permute-done | bytes 65568 | tf_op jit(solution)/shard_map/ppermute | solution.py:380
  31.0 1.6 %all-to-all-done.maps_ref = f32[4,3,128,128]{3,2,1,0:T(8,128)S(1)} async-done(((f32[4,3,128,128]{3,2,1,0:T(8,128)}), f32[4,3,128,128]{3,2,1,0:T(8,128)S(1)}, u32[]{:S(2)}, u32[]{:S(2)}) %all-to-all-start) | async-done | bytes 786464 | tf_op jit(solution)/shard_map/all_to_all | solution.py:407
  33.8 3.5 %all-to-all-start.5 = ((bf16[4,3,2,128,128]{4,3,2,1,0:T(8,128)(2,1)}), bf16[4,3,2,128,128]{4,3,2,1,0:T(8,128)(2,1)S(1)}, u32[]{:S(2)}, u32[]{:S(2)}) async-start(bf16[4,3,2,128,128]{4,3,2,1,0:T(8,128)(2,1)} %broadcast_in_dim.5), calls=%async_computation.5 | async-start | bytes 1572864 | tf_op jit(solution)/shard_map/all_to_all | solution.py:411
  37.3 2.3 %shard_map.239 = (f32[2,128,128]{2,1,0:T(8,128)}, f32[2,128,128]{2,1,0:T(8,128)}) custom-call(f32[4,3,128,128]{3,2,1,0:T(8,128)} %copy-done), custom_call_target="tpu_custom_call" | custom-call | flops 100000000 | bytes 4000000 | tf_op jit(solution)/shard_map/pallas_call | solution.py:369
  39.6 4.7 %collective-permute-start = (f32[2,128,128]{2,1,0:T(8,128)}, f32[2,128,128]{2,1,0:T(8,128)S(1)}, u32[]{:S(2)}, u32[]{:S(2)}) collective-permute-start(f32[2,128,128]{2,1,0:T(8,128)} %get-tuple-element.37.up_ref), channel_id=1, source_target_pairs={{0,32},{32,64},{64,96},{96,128},{128,160},{160,192},{192,224},{1,3... | collective-permute-start | bytes 393224 | tf_op jit(solution)/shard_map/ppermute | solution.py:380
  47.2 4.6 %collective-permute-done.1.from_down_ref.down1_ref = f32[2,128,128]{2,1,0:T(8,128)S(1)} collective-permute-done((f32[2,128,128]{2,1,0:T(8,128)}, f32[2,128,128]{2,1,0:T(8,128)S(1)}, u32[]{:S(2)}, u32[]{:S(2)}) %collective-permute-start.1) | collective-permute-done | bytes 131104 | tf_op jit(solution)/shard_map/ppermute | solution.py:380
  52.4 2.0 %shard_map.240 = (f32[2,128,128]{2,1,0:T(8,128)}, f32[2,128,128]{2,1,0:T(8,128)}) custom-call(s32[3]{0:T(128)} %pad_add_fusion.at_ref, f32[2,128,128]{2,1,0:T(8,128)} %get-tuple-element.37.up_ref, f32[2,128,128]{2,1,0:T(8,128)} %get-tuple-element.38.down_ref, f32[2,128,128]{2,1,0:T(8,128)} %copy-done.4, f32[2,128,128]{2,1,0:T(8,128)} %copy-done.5), custom_call_target="tpu_custom_call" | custom-call | flops 100000000 | bytes 4000000 | tf_op jit(solution)/shard_map/pallas_call | solution.py:369
  54.4 5.0 %collective-permute-start.2 = (f32[2,128,128]{2,1,0:T(8,128)}, f32[2,128,128]{2,1,0:T(8,128)S(1)}, u32[]{:S(2)}, u32[]{:S(2)}) collective-permute-start(f32[2,128,128]{2,1,0:T(8,128)} %get-tuple-element.39.up_ref), channel_id=1, source_target_pairs={{0,64},{32,96},{64,128},{96,160},{128,192},{160,224},{1,65},{33,97... | collective-permute-start | bytes 393224 | tf_op jit(solution)/shard_map/ppermute | solution.py:380
  60.8 1.5 collective-permute-done.2.from_up_ref.up2_ref
  62.3 5.7 %collective-permute-done.3.from_down_ref.down2_ref = f32[2,128,128]{2,1,0:T(8,128)S(1)} collective-permute-done((f32[2,128,128]{2,1,0:T(8,128)}, f32[2,128,128]{2,1,0:T(8,128)S(1)}, u32[]{:S(2)}, u32[]{:S(2)}) %collective-permute-start.3) | collective-permute-done | bytes 131104 | tf_op jit(solution)/shard_map/ppermute | solution.py:380
  68.7 2.3 %shard_map.241 = (f32[128,128]{1,0:T(8,128)}, f32[128,128]{1,0:T(8,128)}) custom-call(s32[3]{0:T(128)} %pad_add_fusion.at_ref, f32[4,128,128]{2,1,0:T(8,128)} %start_ref.3, f32[4,128,128]{2,1,0:T(8,128)} %end_ref.3, f32[2,128,128]{2,1,0:T(8,128)} %get-tuple-element.39.up_ref, f32[2,128,128]{2,1,0:T(8,128)} %get-tuple-element.40.down_ref, ...), custom_call_target="tpu_custom_call" | custom-call | flops 100000000 | bytes 4000000 | tf_op jit(solution)/shard_map/pallas_call | solution.py:369
  70.9 5.3 %collective-permute-start.4 = (f32[128,128]{1,0:T(8,128)}, f32[128,128]{1,0:T(8,128)S(1)}, u32[]{:S(2)}, u32[]{:S(2)}) collective-permute-start(f32[128,128]{1,0:T(8,128)} %get-tuple-element.41), channel_id=1, source_target_pairs={{0,128},{32,160},{64,192},{96,224},{1,129},{33,161},{65,193},{97,2... | collective-permute-start | bytes 196616 | tf_op jit(solution)/shard_map/ppermute | solution.py:380
  77.6 1.5 collective-permute-done.4.leave_ref
  79.1 7.5 %collective-permute-done.5.enter_ref = f32[128,128]{1,0:T(8,128)S(1)} collective-permute-done((f32[128,128]{1,0:T(8,128)}, f32[128,128]{1,0:T(8,128)S(1)}, u32[]{:S(2)}, u32[]{:S(2)}) %collective-permute-start.5) | collective-permute-done | bytes 65568 | tf_op jit(solution)/shard_map/ppermute | solution.py:380
  87.2 3.3 %shard_map.242 = f32[4,2,128,128]{3,2,1,0:T(8,128)} custom-call(s32[3]{0:T(128)} %pad_add_fusion.at_ref, f32[4,128,128]{2,1,0:T(8,128)} %start_ref.3, f32[4,128,128]{2,1,0:T(8,128)} %end_ref.3, f32[128,128]{1,0:T(8,128)} %copy-done.9, f32[128,128]{1,0:T(8,128)} %copy-done.10, f32[2,128,128]{2,1,0:T(8,128)} %copy-done.6, f32[2,128,128]{2,1,0:T(8,128)} %copy-done.7, ...), custom_call_target="tpu_custom_call" | custom-call | flops 100000000 | bytes 4000000 | tf_op jit(solution)/shard_map/pallas_call | solution.py:369
  90.5 4.8 %all-to-all-start.1 = ((f32[4,2,128,128]{3,2,1,0:T(8,128)}), f32[4,2,128,128]{3,2,1,0:T(8,128)S(1)}, u32[]{:S(2)}, u32[]{:S(2)}) async-start(f32[4,2,128,128]{3,2,1,0:T(8,128)} %shard_map.242), calls=%async_computation.1 | async-start | bytes 1048576 | tf_op jit(solution)/shard_map/all_to_all | solution.py:442
  95.3 4.1 %shard_map.246 = (f32[128,128]{1,0:T(8,128)}, f32[4,3,2,128,128]{4,3,2,1,0:T(8,128)}) custom-call(s32[3]{0:T(128)} %pad_add_fusion.at_ref, bf16[128,128]{1,0:T(8,128)(2,1)} %q_ref.5, bf16[128,128]{1,0:T(8,128)(2,1)} %g_ref.5, bf16[4,3,2,128,128]{4,3,2,1,0:T(8,128)(2,1)} %copy-done.1), custom_call_target="tpu_custom_call" | custom-call | flops 100000000 | bytes 4000000 | tf_op jit(solution)/shard_map/pallas_call | solution.py:369
  99.3 4.0 %all-to-all-done.1.ends_ref = f32[4,2,128,128]{3,2,1,0:T(8,128)S(1)} async-done(((f32[4,2,128,128]{3,2,1,0:T(8,128)}), f32[4,2,128,128]{3,2,1,0:T(8,128)S(1)}, u32[]{:S(2)}, u32[]{:S(2)}) %all-to-all-start.1) | async-done | bytes 524320 | tf_op jit(solution)/shard_map/all_to_all | solution.py:442
  104.2 3.6 %all-to-all-start.6 = ((f32[4,3,2,128,128]{4,3,2,1,0:T(8,128)}), f32[4,3,2,128,128]{4,3,2,1,0:T(8,128)S(1)}, u32[]{:S(2)}, u32[]{:S(2)}) async-start(f32[4,3,2,128,128]{4,3,2,1,0:T(8,128)} %get-tuple-element.59), calls=%async_computation.6 | async-start | bytes 3145728 | tf_op jit(solution)/shard_map/all_to_all | solution.py:444
  107.7 6.9 %shard_map.243 = (f32[128,512]{1,0:T(8,128)}, f32[128,512]{1,0:T(8,128)}, f32[128,512]{1,0:T(8,128)}, f32[1,4,128,128]{3,2,1,0:T(8,128)}, f32[8,128]{1,0:T(8,128)}, /*index=5*/f32[8,128]{1,0:T(8,128)}) custom-call(f32[4,2,128,128]{3,2,1,0:T(8,128)} %copy-done.2, f32[4,3,128,128]{3,2,1,0:T(8,128)} %get-tuple-element.36.maps_ref, bf16[128,512]{1,0:T(8,128)(2,1)} %q_ref.4, ...), custom_call_target="tpu_custom_call" | custom-call | flops 100000000 | bytes 4000000 | tf_op jit(solution)/shard_map/pallas_call | solution.py:369
  114.6 8.0 %all-to-all-done.6 = f32[4,3,2,128,128]{4,3,2,1,0:T(8,128)S(1)} async-done(((f32[4,3,2,128,128]{4,3,2,1,0:T(8,128)}), f32[4,3,2,128,128]{4,3,2,1,0:T(8,128)S(1)}, u32[]{:S(2)}, u32[]{:S(2)}) %all-to-all-start.6) | async-done | bytes 1572896 | tf_op jit(solution)/shard_map/all_to_all | solution.py:444
  124.0 4.8 %all-to-all-start.2 = ((f32[8,8,128]{2,1,0:T(8,128)}), f32[8,8,128]{2,1,0:T(8,128)S(1)}, u32[]{:S(2)}, u32[]{:S(2)}) async-start(f32[8,8,128]{2,1,0:T(8,128)} %broadcast_in_dim.4), calls=%async_computation.2 | async-start | bytes 65536 | tf_op jit(solution)/shard_map/all_to_all | solution.py:456
  128.8 3.0 %shard_map.245 = f32[32,8,384]{2,1,0:T(8,128)} custom-call(f32[8,128]{1,0:T(8,128)} %get-tuple-element.56.d_ref, f32[8,128]{1,0:T(8,128)} %get-tuple-element.57.param_ref, bf16[128,8192]{1,0:T(8,128)(2,1)} %x_ref.3), custom_call_target="tpu_custom_call" | custom-call | flops 100000000 | bytes 4000000 | tf_op jit(solution)/shard_map/pallas_call | solution.py:369
  132.8 3.9 %all-to-all-start.4 = ((f32[32,8,384]{2,1,0:T(8,128)}), f32[32,8,384]{2,1,0:T(8,128)S(1)}, u32[]{:S(2)}, u32[]{:S(2)}) async-start(f32[32,8,384]{2,1,0:T(8,128)} %shard_map.245), calls=%async_computation.4 | async-start | bytes 786432 | tf_op jit(solution)/shard_map/all_to_all | solution.py:464
  139.3 2.0 %shard_map.244 = f32[128,1024]{1,0:T(8,128)} custom-call(f32[64,128]{1,0:T(8,128)} %bitcast.28, bf16[64,1024]{1,0:T(8,128)(2,1)} %bitcast.27), custom_call_target="tpu_custom_call" | custom-call | flops 100000000 | bytes 4000000 | tf_op jit(solution)/shard_map/pallas_call | solution.py:369
  141.3 13.6 %collective-permute-done.9 = f32[2,128,128]{2,1,0:T(8,128)S(1)} collective-permute-done((f32[2,128,128]{2,1,0:T(8,128)S(1)}, f32[2,128,128]{2,1,0:T(8,128)S(1)}, u32[]{:S(2)}, u32[]{:S(2)}) %collective-permute-start.9) | collective-permute-done | bytes 131104 | tf_op jit(solution)/shard_map/ppermute | solution.py:380
  (50 shorter events, 16.2 us)
Async XLA Ops:
  2.2 14.0 %all-to-all-start.3 = ((bf16[8,8,1024]{2,1,0:T(8,128)(2,1)}), bf16[8,8,1024]{2,1,0:T(8,128)(2,1)S(1)}, u32[]{:S(2)}, u32[]{:S(2)}) async-start(bf16[8,8,1024]{2,1,0:T(8,128)(2,1)} %bitcast.4), calls=%async_computation.3 | async-start | bytes 262144 | tf_op jit(solution)/shard_map/all_to_all | solution.py:413
  7.7 12.4 %copy-start.11 = (bf16[128,128]{1,0:T(8,128)(2,1)S(1)}, bf16[128,128]{1,0:T(8,128)(2,1)}, u32[]{:S(2)}) copy-start(bf16[128,128]{1,0:T(8,128)(2,1)} %param.28) | copy-start | bytes 98308
  7.7 12.4 %copy-start.12 = (bf16[128,128]{1,0:T(8,128)(2,1)S(1)}, bf16[128,128]{1,0:T(8,128)(2,1)}, u32[]{:S(2)}) copy-start(bf16[128,128]{1,0:T(8,128)(2,1)} %param.27) | copy-start | bytes 98308
  16.3 17.5 %copy-start.3 = (bf16[8,8,1024]{2,1,0:T(8,128)(2,1)}, bf16[8,8,1024]{2,1,0:T(8,128)(2,1)S(1)}, u32[]{:S(2)}) copy-start(bf16[8,8,1024]{2,1,0:T(8,128)(2,1)S(1)} %all-to-all-done.3) | copy-start | bytes 393220
  16.3 16.4 %all-to-all-start = ((f32[4,3,128,128]{3,2,1,0:T(8,128)}), f32[4,3,128,128]{3,2,1,0:T(8,128)S(1)}, u32[]{:S(2)}, u32[]{:S(2)}) async-start(f32[4,3,128,128]{3,2,1,0:T(8,128)} %get-tuple-element.36.maps_ref), calls=%async_computation | async-start | bytes 1572864 | tf_op jit(solution)/shard_map/all_to_all | solution.py:407
  20.1 9.0 %collective-permute-start.7 = (bf16[2,128,128]{2,1,0:T(8,128)(2,1)S(1)}, bf16[2,128,128]{2,1,0:T(8,128)(2,1)S(1)}, u32[]{:S(2)}, u32[]{:S(2)}) collective-permute-start(bf16[2,128,128]{2,1,0:T(8,128)(2,1)S(1)} %get-tuple-element.67), channel_id=1, source_target_pairs={{0,64},{32,96},{64,128},{96,160},{128,192},{160,224},{1,65},{33,97... | collective-permute-start | bytes 196616 | tf_op jit(solution)/shard_map/ppermute | solution.py:380
  25.3 5.7 %collective-permute-start.6 = (bf16[2,128,128]{2,1,0:T(8,128)(2,1)S(1)}, bf16[2,128,128]{2,1,0:T(8,128)(2,1)S(1)}, u32[]{:S(2)}, u32[]{:S(2)}) collective-permute-start(bf16[2,128,128]{2,1,0:T(8,128)(2,1)S(1)} %get-tuple-element.67), channel_id=1, source_target_pairs={{0,32},{32,64},{64,96},{96,128},{128,160},{160,192},{192,224},{1,3... | collective-permute-start | bytes 196616 | tf_op jit(solution)/shard_map/ppermute | solution.py:380
  32.7 4.7 %copy-start = (f32[4,3,128,128]{3,2,1,0:T(8,128)}, f32[4,3,128,128]{3,2,1,0:T(8,128)S(1)}, u32[]{:S(2)}) copy-start(f32[4,3,128,128]{3,2,1,0:T(8,128)S(1)} %all-to-all-done.maps_ref) | copy-start | bytes 2359300
  33.8 56.7 %all-to-all-start.5 = ((bf16[4,3,2,128,128]{4,3,2,1,0:T(8,128)(2,1)}), bf16[4,3,2,128,128]{4,3,2,1,0:T(8,128)(2,1)S(1)}, u32[]{:S(2)}, u32[]{:S(2)}) async-start(bf16[4,3,2,128,128]{4,3,2,1,0:T(8,128)(2,1)} %broadcast_in_dim.5), calls=%async_computation.5 | async-start | bytes 1572864 | tf_op jit(solution)/shard_map/all_to_all | solution.py:411
  39.6 7.5 %collective-permute-start = (f32[2,128,128]{2,1,0:T(8,128)}, f32[2,128,128]{2,1,0:T(8,128)S(1)}, u32[]{:S(2)}, u32[]{:S(2)}) collective-permute-start(f32[2,128,128]{2,1,0:T(8,128)} %get-tuple-element.37.up_ref), channel_id=1, source_target_pairs={{0,32},{32,64},{64,96},{96,128},{128,160},{160,192},{192,224},{1,3... | collective-permute-start | bytes 393224 | tf_op jit(solution)/shard_map/ppermute | solution.py:380
  44.3 7.4 %collective-permute-start.1 = (f32[2,128,128]{2,1,0:T(8,128)}, f32[2,128,128]{2,1,0:T(8,128)S(1)}, u32[]{:S(2)}, u32[]{:S(2)}) collective-permute-start(f32[2,128,128]{2,1,0:T(8,128)} %get-tuple-element.38.down_ref), channel_id=1, source_target_pairs={{32,0},{64,32},{96,64},{128,96},{160,128},{192,160},{224,192},{33,... | collective-permute-start | bytes 393224 | tf_op jit(solution)/shard_map/ppermute | solution.py:380
  47.2 4.6 %copy-start.4 = (f32[2,128,128]{2,1,0:T(8,128)}, f32[2,128,128]{2,1,0:T(8,128)S(1)}, u32[]{:S(2)}) copy-start(f32[2,128,128]{2,1,0:T(8,128)S(1)} %collective-permute-done.from_up_ref.up1_ref) | copy-start | bytes 393220
  51.8 0.7 copy-start.5
  54.4 7.9 %collective-permute-start.2 = (f32[2,128,128]{2,1,0:T(8,128)}, f32[2,128,128]{2,1,0:T(8,128)S(1)}, u32[]{:S(2)}, u32[]{:S(2)}) collective-permute-start(f32[2,128,128]{2,1,0:T(8,128)} %get-tuple-element.39.up_ref), channel_id=1, source_target_pairs={{0,64},{32,96},{64,128},{96,160},{128,192},{160,224},{1,65},{33,97... | collective-permute-start | bytes 393224 | tf_op jit(solution)/shard_map/ppermute | solution.py:380
  59.5 8.5 %collective-permute-start.3 = (f32[2,128,128]{2,1,0:T(8,128)}, f32[2,128,128]{2,1,0:T(8,128)S(1)}, u32[]{:S(2)}, u32[]{:S(2)}) collective-permute-start(f32[2,128,128]{2,1,0:T(8,128)} %get-tuple-element.40.down_ref), channel_id=1, source_target_pairs={{64,0},{96,32},{128,64},{160,96},{192,128},{224,160},{65,1},{97,33... | collective-permute-start | bytes 393224 | tf_op jit(solution)/shard_map/ppermute | solution.py:380
  62.3 5.7 %copy-start.6 = (f32[2,128,128]{2,1,0:T(8,128)}, f32[2,128,128]{2,1,0:T(8,128)S(1)}, u32[]{:S(2)}) copy-start(f32[2,128,128]{2,1,0:T(8,128)S(1)} %collective-permute-done.2.from_up_ref.up2_ref) | copy-start | bytes 393220
  68.0 0.7 copy-start.7
  70.9 8.2 %collective-permute-start.4 = (f32[128,128]{1,0:T(8,128)}, f32[128,128]{1,0:T(8,128)S(1)}, u32[]{:S(2)}, u32[]{:S(2)}) collective-permute-start(f32[128,128]{1,0:T(8,128)} %get-tuple-element.41), channel_id=1, source_target_pairs={{0,128},{32,160},{64,192},{96,224},{1,129},{33,161},{65,193},{97,2... | collective-permute-start | bytes 196616 | tf_op jit(solution)/shard_map/ppermute | solution.py:380
  76.3 10.3 %collective-permute-start.5 = (f32[128,128]{1,0:T(8,128)}, f32[128,128]{1,0:T(8,128)S(1)}, u32[]{:S(2)}, u32[]{:S(2)}) collective-permute-start(f32[128,128]{1,0:T(8,128)} %get-tuple-element.42), channel_id=1, source_target_pairs={{128,0},{160,32},{192,64},{224,96},{129,1},{161,33},{193,65},{225,... | collective-permute-start | bytes 196616 | tf_op jit(solution)/shard_map/ppermute | solution.py:380
  79.1 7.5 %copy-start.9 = (f32[128,128]{1,0:T(8,128)}, f32[128,128]{1,0:T(8,128)S(1)}, u32[]{:S(2)}) copy-start(f32[128,128]{1,0:T(8,128)S(1)} %collective-permute-done.4.leave_ref) | copy-start | bytes 196612
  86.6 0.6 copy-start.10
  90.5 4.8 %copy-start.1 = (bf16[4,3,2,128,128]{4,3,2,1,0:T(8,128)(2,1)}, bf16[4,3,2,128,128]{4,3,2,1,0:T(8,128)(2,1)S(1)}, u32[]{:S(2)}) copy-start(bf16[4,3,2,128,128]{4,3,2,1,0:T(8,128)(2,1)S(1)} %all-to-all-done.5.kv_ref) | copy-start | bytes 2359300
  90.5 12.8 %all-to-all-start.1 = ((f32[4,2,128,128]{3,2,1,0:T(8,128)}), f32[4,2,128,128]{3,2,1,0:T(8,128)S(1)}, u32[]{:S(2)}, u32[]{:S(2)}) async-start(f32[4,2,128,128]{3,2,1,0:T(8,128)} %shard_map.242), calls=%async_computation.1 | async-start | bytes 1048576 | tf_op jit(solution)/shard_map/all_to_all | solution.py:442
  103.4 0.8 copy-start.2
  104.2 18.5 %all-to-all-start.6 = ((f32[4,3,2,128,128]{4,3,2,1,0:T(8,128)}), f32[4,3,2,128,128]{4,3,2,1,0:T(8,128)S(1)}, u32[]{:S(2)}, u32[]{:S(2)}) async-start(f32[4,3,2,128,128]{4,3,2,1,0:T(8,128)} %get-tuple-element.59), calls=%async_computation.6 | async-start | bytes 3145728 | tf_op jit(solution)/shard_map/all_to_all | solution.py:444
  124.0 8.8 %all-to-all-start.2 = ((f32[8,8,128]{2,1,0:T(8,128)}), f32[8,8,128]{2,1,0:T(8,128)S(1)}, u32[]{:S(2)}, u32[]{:S(2)}) async-start(f32[8,8,128]{2,1,0:T(8,128)} %broadcast_in_dim.4), calls=%async_computation.2 | async-start | bytes 65536 | tf_op jit(solution)/shard_map/all_to_all | solution.py:456
  132.7 6.5 %copy-start.8 = (f32[8,8,128]{2,1,0:T(8,128)}, f32[8,8,128]{2,1,0:T(8,128)S(1)}, u32[]{:S(2)}) copy-start(f32[8,8,128]{2,1,0:T(8,128)S(1)} %all-to-all-done.2) | copy-start | bytes 98308
  132.8 22.8 %all-to-all-start.4 = ((f32[32,8,384]{2,1,0:T(8,128)}), f32[32,8,384]{2,1,0:T(8,128)S(1)}, u32[]{:S(2)}, u32[]{:S(2)}) async-start(f32[32,8,384]{2,1,0:T(8,128)} %shard_map.245), calls=%async_computation.4 | async-start | bytes 786432 | tf_op jit(solution)/shard_map/all_to_all | solution.py:464
  136.7 18.2 %collective-permute-start.9 = (f32[2,128,128]{2,1,0:T(8,128)S(1)}, f32[2,128,128]{2,1,0:T(8,128)S(1)}, u32[]{:S(2)}, u32[]{:S(2)}) collective-permute-start(f32[2,128,128]{2,1,0:T(8,128)S(1)} %get-tuple-element.63), channel_id=1, source_target_pairs={{64,0},{96,32},{128,64},{160,96},{192,128},{224,160},{65,1},{97,33... | collective-permute-start | bytes 393224 | tf_op jit(solution)/shard_map/ppermute | solution.py:380
  138.0 16.9 %collective-permute-start.8 = (f32[2,128,128]{2,1,0:T(8,128)S(1)}, f32[2,128,128]{2,1,0:T(8,128)S(1)}, u32[]{:S(2)}, u32[]{:S(2)}) collective-permute-start(f32[2,128,128]{2,1,0:T(8,128)S(1)} %get-tuple-element.62), channel_id=1, source_target_pairs={{32,0},{64,32},{96,64},{128,96},{160,128},{192,160},{224,192},{33,... | collective-permute-start | bytes 393224 | tf_op jit(solution)/shard_map/ppermute | solution.py:380

commit v2 on v1

--- a/solution.py
+++ b/solution.py
@@ -7,6 +7,7 @@
 from jax.experimental.pallas import tpu as pltpu
 from jax.sharding import Mesh
 from jax.sharding import PartitionSpec as P
+
 
 WINDOW = 1024
 T = 128
@@ -147,7 +148,8 @@
         maps_ref[h, 2] = own - mm(split(y), split(du), TN)
 
 
-def group_kernel(maps_ref, up_ref, down_ref):
+def group_kernel(at_ref, maps_ref, out_ref):
+    z = at_ref[0]
     phi = [split(maps_ref[x, 0]) for x in range(4)]
     off = [maps_ref[x, 1] for x in range(4)]
     loc = [maps_ref[x, 2] for x in range(4)]
@@ -158,54 +160,23 @@
     loc_a = mm(phi[0], split(loc[1]), TN) + loc[0]
     loc_b = mm(phi[2], split(loc[3]), TN) + loc[2]
     whole = mm(second, first, NN)
-    up_ref[0] = whole
-    down_ref[0] = whole
-    up_ref[1] = mm(second, split(off_a), NN) + off_b
-    down_ref[1] = mm(first, split(loc_b), TN) + loc_a
-
-
-def pair_kernel(at_ref, up_ref, down_ref, from_up_ref, from_down_ref, up_out_ref, down_out_ref):
-    z, count = at_ref[0], at_ref[1]
-    own = split(up_ref[0])
-    has_up, has_down = z >= 1, z < count - 1
-    up_out_ref[0] = jnp.where(has_up, mm(own, split(from_up_ref[0]), NN), up_ref[0])
-    up_out_ref[1] = jnp.where(
-        has_up, mm(own, split(from_up_ref[1]), NN) + up_ref[1], up_ref[1]
-    )
-    down_out_ref[0] = jnp.where(has_down, mm(split(from_down_ref[0]), own, NN), down_ref[0])
-    down_out_ref[1] = jnp.where(
-        has_down, mm(own, split(from_down_ref[1]), TN) + down_ref[1], down_ref[1]
-    )
-
-
-def reach_kernel(
-    at_ref, start_ref, end_ref, up_ref, down_ref, from_up_ref, from_down_ref, leave_ref, enter_ref
-):
-    z, count, x = at_ref[0], at_ref[1], at_ref[2]
-    start, end = start_ref[x], end_ref[x]
-    ahead = mm(split(from_up_ref[0]), split(start), NN) + from_up_ref[1]
-    state = jnp.where(z >= 2, ahead, start)
-    leave_ref[...] = mm(split(up_ref[0]), split(state), NN) + up_ref[1]
-    behind = mm(split(from_down_ref[0]), split(end), TN) + from_down_ref[1]
-    grad = jnp.where(z < count - 2, behind, end)
-    enter_ref[...] = mm(split(down_ref[0]), split(grad), TN) + down_ref[1]
-
-
-def spread_kernel(
-    at_ref, start_ref, end_ref, leave_ref, enter_ref, up2_ref, down2_ref, up1_ref, down1_ref,
-    maps_ref, out_ref,
-):
-    z, count, x = at_ref[0], at_ref[1], at_ref[2]
-    state = jnp.where(z >= 4, leave_ref[...], start_ref[x])
-    grad = jnp.where(z < count - 4, enter_ref[...], end_ref[x])
-    state_two = mm(split(up2_ref[0]), split(state), NN) + up2_ref[1]
-    grad_two = mm(split(down2_ref[0]), split(grad), TN) + down2_ref[1]
-    state = jnp.where(z >= 2, state_two, state)
-    grad = jnp.where(z < count - 2, grad_two, grad)
-    state_one = mm(split(up1_ref[0]), split(state), NN) + up1_ref[1]
-    grad_one = mm(split(down1_ref[0]), split(grad), TN) + down1_ref[1]
-    state = jnp.where(z >= 1, state_one, state)
-    grad = jnp.where(z < count - 1, grad_one, grad)
+    later = mm(second, split(off_a), NN) + off_b
+    earlier = mm(first, split(loc_b), TN) + loc_a
+    for to in range(out_ref.shape[0]):
+        out_ref[to, 0] = whole
+        out_ref[to, 1] = jnp.where(to > z, later, earlier)
+
+
+def spread_kernel(at_ref, start_ref, end_ref, groups_ref, maps_ref, out_ref):
+    z, x = at_ref[0], at_ref[1]
+    count = groups_ref.shape[0]
+    state, grad = start_ref[x], end_ref[x]
+    for step in range(count - 1):
+        back = count - 1 - step
+        ahead = mm(split(groups_ref[step, 0]), split(state), NN) + groups_ref[step, 1]
+        behind = mm(split(groups_ref[back, 0]), split(grad), TN) + groups_ref[back, 1]
+        state = jnp.where(step < z, ahead, state)
+        grad = jnp.where(back > z, behind, grad)
     for step in range(4):
         back = 3 - step
         out_ref[step, 0] = state
@@ -236,7 +207,6 @@
         norm_k = cols[:, 2 * heads + h : 2 * heads + h + 1]
         norm_q = cols[:, 3 * heads + h : 3 * heads + h + 1]
         norm_k_row = rows[2 * heads + h : 2 * heads + h + 1]
-        norm_q_row = rows[3 * heads + h : 3 * heads + h + 1]
         end = rows[heads + h : heads + h + 1, T - 1 : T]
         grow, tail = jnp.exp(cum), jnp.exp(end - cum)
         m0, d = ends_ref[h, 0], ends_ref[h, 1]
@@ -298,8 +268,9 @@
     )
 
 
-def window_kernel(at_ref, q_ref, g_ref, kv_ref, dq_ref, dkv_ref):
-    z, x = at_ref[0], at_ref[2]
+def window_kernel(at_ref, q_ref, g_ref, *refs):
+    kv_refs, dq_ref, dkv_refs = refs[:4], refs[4], refs[5:]
+    z, x = at_ref[0], at_ref[1]
     row, lane = ids((T, T))
     gap = row - lane
     scale = 1.0 / math.sqrt(T)
@@ -307,9 +278,9 @@
     scores, slopes = [], []
     tiles = [(a, b) for a in range(4) for b in range(3)]
     for a, b in tiles:
-        spread = gap + (x - a + 4 * b) * T
+        spread = gap + (jnp.where(x >= a, a, a - 4) + 4 * b) * T
         ok = (spread >= 0) & (spread < jnp.where(z >= b, WINDOW, 0))
-        s = lax.dot_general(q, kv_ref[a, b, 0], NT, preferred_element_type=F32) * scale
+        s = lax.dot_general(q, kv_refs[a][b, 0], NT, preferred_element_type=F32) * scale
         scores.append(jnp.where(ok, s, -1e30))
     top = scores[0]
     for s in scores[1:]:
@@ -323,22 +294,27 @@
     weights = [w * total for w in weights]
     terms = None
     for (a, b), w in zip(tiles, weights):
-        slope = lax.dot_general(g, kv_ref[a, b, 1], NT, preferred_element_type=F32)
+        slope = lax.dot_general(g, kv_refs[a][b, 1], NT, preferred_element_type=F32)
         slopes.append(slope)
         terms = w * slope if terms is None else terms + w * slope
     terms = jnp.sum(terms, axis=1, keepdims=True)
     dq = None
     for (a, b), w, slope in zip(tiles, weights, slopes):
         ds = split(w * (slope - terms) * scale)
-        part = mm(ds, kv_ref[a, b, 0], NN)
+        part = mm(ds, kv_refs[a][b, 0], NN)
         dq = part if dq is None else dq + part
-        dkv_ref[a, b, 0] = mm(ds, q, TN)
-        dkv_ref[a, b, 1] = mm(split(w), g, TN)
+        dkv_refs[a][b, 0] = mm(ds, q, TN)
+        dkv_refs[a][b, 1] = mm(split(w), g, TN)
     dq_ref[...] = dq
 
 
-def input_kernel(d_ref, w_ref, out_ref):
-    high, low = split(d_ref[...])
+def input_kernel(at_ref, w_ref, *refs):
+    rows_refs, out_ref, all_ref = refs[:-2], refs[-2], refs[-1]
+    head, count = at_ref[2], len(rows_refs)
+    for d, rows_ref in enumerate(rows_refs):
+        source = jnp.where(head >= d, head - d, head - d + count)
+        all_ref[pl.ds(pl.multiple_of(source * 8, 8), 8), :] = rows_ref[...]
+    high, low = split(all_ref[...])
     w = w_ref[...]
     out_ref[...] = lax.dot_general(high, w, TN, preferred_element_type=F32) + lax.dot_general(
         low, w, TN, preferred_element_type=F32
@@ -365,19 +341,36 @@
     return jax.ShapeDtypeStruct(shape, F32)
 
 
-def call(kernel, outs, specs, *args, flops=10**8):
+def call(kernel, outs, specs, *args, flops=10**8, scratch=(), limit=24 * 2**20):
+    return run(kernel, outs, specs, args, flops, scratch, limit)
+
+
+def exchange(value, axis):
+    return lax.all_to_all(value, axis, split_axis=0, concat_axis=0, tiled=True)
+
+
+def run(kernel, outs, specs, args, flops, scratch, limit):
     return pl.pallas_call(
         kernel,
         out_shape=outs,
         in_specs=specs,
         out_specs=jax.tree.map(lambda _: VM, outs),
+        scratch_shapes=scratch,
         cost_estimate=pl.CostEstimate(flops=flops, bytes_accessed=4 * 10**6, transcendentals=0),
+        compiler_params=pltpu.CompilerParams(vmem_limit_bytes=limit),
     )(*args)
+
+
+WHOLE = 60 * 1024 * 1024
 
 
 def up_by(value, by, count):
     pairs = [(i, i + by) for i in range(count) if 0 <= i + by < count]
     return lax.ppermute(value, "seq_0", pairs)
+
+
+def turn(value, axis, by, count):
+    return lax.ppermute(value, axis, [(i, (i + by) % count) for i in range(count)])
 
 
 def shards(
@@ -389,13 +382,17 @@
     head_count = lax.axis_size("head")
     heads = beta_weight.shape[0]
     width = layer_input.shape[1]
+    pieces = z_count * x_count
     at = jnp.stack(
-        [lax.axis_index("seq_0"), jnp.int32(z_count), lax.axis_index("seq_1")]
+        [lax.axis_index("seq_0"), lax.axis_index("seq_1"), lax.axis_index("head")]
     ).astype(jnp.int32)
 
     pair = jnp.stack([attn_key, attn_value])
     near, far = up_by(pair, 1, z_count), up_by(pair, 2, z_count)
     both_weights = jnp.concatenate([beta_weight, decay_weight], axis=0)
+    weight_cols = jnp.swapaxes(both_weights.reshape(2 * heads, head_count, -1), 0, 1)
+    weight_cols = exchange(weight_cols, "head")
+    weight_cols = weight_cols.reshape(head_count * 2 * heads, -1)
 
     maps, inv, ratio, rk, p, w, y, du, rows, cols = call(
         prepare_kernel,
@@ -403,47 +400,31 @@
         [VM, VM, SM, SM, VM, VM, VM, VM],
         layer_input, both_weights, log_rate, decay_bias, delta_query, delta_key, delta_value,
         delta_out_grad,
-    )
-    blocks = lax.all_to_all(maps, "seq_1", split_axis=0, concat_axis=0, tiled=True)
+        limit=WHOLE,
+    )
+    maps, weight_cols = lax.optimization_barrier((maps, weight_cols))
+    blocks = exchange(maps, "seq_1")
+    groups = call(group_kernel, f32(z_count, 2, T, T), [SM, VM], at, blocks)
 
     triple = jnp.stack([pair, near, far])
-    copies = jnp.broadcast_to(triple[None], (x_count, *triple.shape))
-    window = lax.all_to_all(copies, "seq_1", split_axis=0, concat_axis=0, tiled=True)
-    weight_cols = jnp.swapaxes(both_weights.reshape(2 * heads, head_count, -1), 0, 1)
-    weight_cols = lax.all_to_all(weight_cols, "head", split_axis=0, concat_axis=0, tiled=True)
-    weight_cols = weight_cols.reshape(head_count * 2 * heads, -1)
-
-    dq_attn, dkv = call(
+    triple, groups = lax.optimization_barrier((triple, groups))
+    groups = exchange(groups, "seq_0")
+    windows = [triple] + [turn(triple, "seq_1", d, x_count) for d in range(1, x_count)]
+    dq_attn, *dkv = call(
         window_kernel,
-        (f32(T, T), f32(x_count, 3, 2, T, T)),
-        [SM, VM, VM, VM],
-        at, attn_query, attn_out_grad, window,
-    )
-
-    up, down = call(group_kernel, (f32(2, T, T), f32(2, T, T)), [VM], blocks)
-    up1, down1 = up_by(up, 1, z_count), up_by(down, -1, z_count)
-    up, down = call(
-        pair_kernel, (f32(2, T, T), f32(2, T, T)), [SM, VM, VM, VM, VM], at, up, down, up1, down1
-    )
-    up2, down2 = up_by(up, 2, z_count), up_by(down, -2, z_count)
-    leave, enter = call(
-        reach_kernel,
-        (f32(T, T), f32(T, T)),
-        [SM, VM, VM, VM, VM, VM, VM],
-        at, state_init, state_grad_next, up, down, up2, down2,
-    )
-    leave, enter = up_by(leave, 4, z_count), up_by(enter, -4, z_count)
+        (f32(T, T),) + (f32(3, 2, T, T),) * x_count,
+        [SM] + [VM] * (2 + x_count),
+        at, attn_query, attn_out_grad, *windows,
+    )
+    dkv = [dkv[0]] + [turn(dkv[d], "seq_1", -d, x_count) for d in range(1, x_count)]
+
     ends = call(
         spread_kernel,
         f32(x_count, 2, T, T),
-        [SM] + [VM] * 9,
-        at, state_init, state_grad_next, leave, enter, up2, down2, up1, down1, blocks,
-    )
-    ends = lax.all_to_all(ends, "seq_1", split_axis=0, concat_axis=0, tiled=True)
-
-    dkv = lax.all_to_all(dkv, "seq_1", split_axis=0, concat_axis=0, tiled=True)
-    dkv = jnp.sum(dkv, axis=0)
-    dkv_near, dkv_far = up_by(dkv[1], -1, z_count), up_by(dkv[2], -2, z_count)
+        [SM] + [VM] * 4,
+        at, state_init, state_grad_next, groups, blocks,
+    )
+    ends = exchange(ends, "seq_1")
 
     dq, dk, dv, bound, logit, param = call(
         finish_kernel,
@@ -451,22 +432,25 @@
         [VM] * 15,
         ends, maps, delta_query, delta_key, delta_value, delta_out_grad, inv, ratio, rk, p, w, y,
         du, rows, cols,
-    )
-    logit_copies = jnp.broadcast_to(logit[None], (head_count, *logit.shape))
-    every = lax.all_to_all(logit_copies, "head", split_axis=0, concat_axis=0, tiled=True)
-    pieces = z_count * x_count
+        limit=WHOLE,
+    )
     terms = call(
         weight_kernel,
         f32(pieces, 2 * heads, width // pieces + T),
         [VM, VM, VM],
         logit, param, layer_input,
     )
-    terms = lax.all_to_all(terms, SEQ, split_axis=0, concat_axis=0, tiled=True)
+    terms, logit = lax.optimization_barrier((terms, logit))
+    terms = exchange(terms, SEQ)
+    every = [logit] + [turn(logit, "head", d, head_count) for d in range(1, head_count)]
+    dkv = sum(dkv[1:], dkv[0])
+    dkv_near, dkv_far = up_by(dkv[1], -1, z_count), up_by(dkv[2], -2, z_count)
     input_grad = call(
         input_kernel,
         f32(T, weight_cols.shape[1]),
-        [VM, VM],
-        every.reshape(-1, T), weight_cols,
+        [SM] + [VM] * (1 + head_count),
+        at, weight_cols, *every,
+        scratch=[pltpu.VMEM((2 * heads * head_count, T), F32)],
     )
     terms = jnp.sum(terms, axis=0)
     part = width // pieces
@@ -490,6 +474,7 @@
         tokens, tokens, tokens, P(SEQ, "head", None, None), tokens,
         P("head", SEQ), P("head", SEQ), P("head"), P("head"), tokens, tokens, tokens,
     )
+
     return jax.shard_map(
         shards, mesh=torus, in_specs=in_specs, out_specs=out_specs, check_vma=False
     )

time: 160 us -> 135 us (0.84)
  the two profiles are of different devices: /device:TPU:8 before, /device:TPU:64 now
where the time goes in v2:
time: 135 us
  starting transfers between devices  57.2 us (42%)
  waiting for transfers between devices  42.7 us (32%)
  Pallas kernels  26.6 us (20%)
  local copies, waits for them, and re-layouts  4.14 us (3%)
  other arithmetic  3.1 us (2%)
    all_to_all x5, starting transfers between devices, exchange(): return lax.all_to_all(value, axis, split_axis=0, concat_axis=0, tiled=True)  28.6 us
    pallas_call x7, Pallas kernels, run(): pl.pallas_call(kernel, out_shape=outs, in_specs=specs, out_specs=jax.tree...  26.6 us
    ppermute x4, waiting for transfers between devices, up_by(): return lax.ppermute(value, 'seq_0', pairs)  16.1 us
    ppermute x13, starting transfers between devices, turn(): lax.ppermute(value, axis, [(i, (i + by) % count) for i in range(count)])  14.9 us
    ppermute x13, waiting for transfers between devices, turn(): lax.ppermute(value, axis, [(i, (i + by) % count) for i in range(count)])  14.1 us
    ppermute x4, starting transfers between devices, up_by(): return lax.ppermute(value, 'seq_0', pairs)  13.7 us
    all_to_all x5, waiting for transfers between devices, exchange(): return lax.all_to_all(value, axis, split_axis=0, concat_axis=0, tiled=True)  12.6 us
  transfers between devices with their start and end apart: 22, of which 14 were waited for; matrix products, arithmetic and copies ran while one was open for 2% of the time, Pallas kernels for 12%

profile of v2, /device:TPU:64, one launch (start us, length us, event | category | flops | bytes accessed | tf_op | source)
XLA Modules:
  0.0 134.6 jit_solution(10756171264713476972)
XLA Ops:
  0.6 1.6 %pad_maximum_fusion.1.w_ref = bf16[8,8192]{1,0:T(8,128)(2,1)} fusion(bf16[4,8192]{1,0:T(4,128)(2,1)} %param.17, bf16[4,8192]{1,0:T(4,128)(2,1)} %param.16), kind=kLoop, calls=%fused_computation.7 | loop fusion | flops 262144 | bytes 262144 | tf_op jit(solution)/shard_map/concatenate | solution.py:392
  2.2 4.5 %all-to-all-start = ((bf16[8,8,1024]{2,1,0:T(8,128)(2,1)}), bf16[8,8,1024]{2,1,0:T(8,128)(2,1)S(1)}, u32[]{:S(2)}, u32[]{:S(2)}) async-start(bf16[8,8,1024]{2,1,0:T(8,128)(2,1)} %bitcast.9), calls=%async_computation | async-start | bytes 262144 | tf_op jit(solution)/shard_map/all_to_all | solution.py:349
  6.7 8.6 %shard_map.238 = (f32[4,3,128,128]{3,2,1,0:T(8,128)}, f32[4,128,128]{2,1,0:T(8,128)}, f32[4,128,128]{2,1,0:T(8,128)}, f32[4,128,128]{2,1,0:T(8,128)}, f32[4,128,...) custom-call(bf16[128,8192]{1,0:T(8,128)(2,1)} %x_ref.3, ...), custom_call_target="tpu_custom_call" | custom-call | flops 100000000 | bytes 4000000 | tf_op jit(solution)/shard_map/pallas_call | solution.py:353
  15.3 4.3 %all-to-all-start.1 = ((f32[4,3,128,128]{3,2,1,0:T(8,128)}), f32[4,3,128,128]{3,2,1,0:T(8,128)S(1)}, u32[]{:S(2)}, u32[]{:S(2)}) async-start(f32[4,3,128,128]{3,2,1,0:T(8,128)} %get-tuple-element.40.maps_ref), calls=%async_computation.1 | async-start | bytes 1572864 | tf_op jit(solution)/shard_map/all_to_all | solution.py:349
  19.7 3.8 %collective-permute-start = (bf16[2,128,128]{2,1,0:T(8,128)(2,1)S(1)}, bf16[2,128,128]{2,1,0:T(8,128)(2,1)S(1)}, u32[]{:S(2)}, u32[]{:S(2)}) collective-permute-start(bf16[2,128,128]{2,1,0:T(8,128)(2,1)S(1)} %get-tuple-element.73), channel_id=1, source_target_pairs={{0,32},{32,64},{64,96},{96,128},{128,160},{160,192},{192,224},{1,3... | collective-permute-start | bytes 196616 | tf_op jit(solution)/shard_map/ppermute | solution.py:369
  23.5 5.5 %collective-permute-start.1 = (bf16[2,128,128]{2,1,0:T(8,128)(2,1)S(1)}, bf16[2,128,128]{2,1,0:T(8,128)(2,1)S(1)}, u32[]{:S(2)}, u32[]{:S(2)}) collective-permute-start(bf16[2,128,128]{2,1,0:T(8,128)(2,1)S(1)} %get-tuple-element.73), channel_id=1, source_target_pairs={{0,64},{32,96},{64,128},{96,160},{128,192},{160,224},{1,65},{33,97... | collective-permute-start | bytes 196616 | tf_op jit(solution)/shard_map/ppermute | solution.py:369
  29.1 2.7 %collective-permute-done.1 = bf16[2,128,128]{2,1,0:T(8,128)(2,1)S(1)} collective-permute-done((bf16[2,128,128]{2,1,0:T(8,128)(2,1)S(1)}, bf16[2,128,128]{2,1,0:T(8,128)(2,1)S(1)}, u32[]{:S(2)}, u32[]{:S(2)}) %collective-permute-start.1) | collective-permute-done | bytes 65568 | tf_op jit(solution)/shard_map/ppermute | solution.py:369
  32.6 2.0 %shard_map.239 = f32[8,2,128,128]{3,2,1,0:T(8,128)} custom-call(s32[3]{0:T(128)S(1)} %pad_add_fusion.at_ref, f32[4,3,128,128]{3,2,1,0:T(8,128)S(1)} %all-to-all-done.1.maps_ref), custom_call_target="tpu_custom_call" | custom-call | flops 100000000 | bytes 4000000 | tf_op jit(solution)/shard_map/pallas_call | solution.py:353
  34.6 8.1 %all-to-all-start.2 = ((f32[8,2,128,128]{3,2,1,0:T(8,128)}), f32[8,2,128,128]{3,2,1,0:T(8,128)S(1)}, u32[]{:S(2)}, u32[]{:S(2)}) async-start(f32[8,2,128,128]{3,2,1,0:T(8,128)} %shard_map.239), calls=%async_computation.2 | async-start | bytes 2097152 | tf_op jit(solution)/shard_map/all_to_all | solution.py:349
  42.7 2.5 %collective-permute-start.11 = (bf16[3,2,128,128]{3,2,1,0:T(8,128)(2,1)S(1)}, bf16[3,2,128,128]{3,2,1,0:T(8,128)(2,1)S(1)}, u32[]{:S(2)}, u32[]{:S(2)}) collective-permute-start(bf16[3,2,128,128]{3,2,1,0:T(8,128)(2,1)S(1)} %pad_maximum_fusion.refs_0_), channel_id=1, source_target_pairs={{0,24},{8,0},{16,8},{24,16},{1,25},{9,1},{17,9},{25,17},{2,26},{10... | collective-permute-start | bytes 589832 | tf_op jit(solution)/shard_map/ppermute | solution.py:373
  46.9 5.1 %collective-permute-done.11.refs_3_ = bf16[3,2,128,128]{3,2,1,0:T(8,128)(2,1)S(1)} collective-permute-done((bf16[3,2,128,128]{3,2,1,0:T(8,128)(2,1)S(1)}, bf16[3,2,128,128]{3,2,1,0:T(8,128)(2,1)S(1)}, u32[]{:S(2)}, u32[]{:S(2)}) %collective-permute-start.11) | collective-permute-done | bytes 196640 | tf_op jit(solution)/shard_map/ppermute | solution.py:373
  53.1 2.0 %collective-permute-done.9.refs_1_ = bf16[3,2,128,128]{3,2,1,0:T(8,128)(2,1)S(1)} collective-permute-done((bf16[3,2,128,128]{3,2,1,0:T(8,128)(2,1)S(1)}, bf16[3,2,128,128]{3,2,1,0:T(8,128)(2,1)S(1)}, u32[]{:S(2)}, u32[]{:S(2)}) %collective-permute-start.9) | collective-permute-done | bytes 196640 | tf_op jit(solution)/shard_map/ppermute | solution.py:373
  55.1 2.9 %shard_map.244 = (f32[128,128]{1,0:T(8,128)}, f32[3,2,128,128]{3,2,1,0:T(8,128)S(1)}, f32[3,2,128,128]{3,2,1,0:T(8,128)}, f32[3,2,128,128]{3,2,1,0:T(8,128)}, f32[3,2,128,128]{3,2,1,0:T(8,128)S(1)}) custom-call(s32[3]{0:T(128)S(1)} %pad_add_fusion.at_ref, bf16[128,128]{1,0:T(8,128)(2,1)S(1)} %copy-done.3, bf16[128,128]{1,0:T(8,128)(2,1)S(1)} %copy-done.4, ...), custom_call_target="tpu_custom_call" | custom-call | flops 100000000 | bytes 4000000 | tf_op jit(solution)/shard_map/pallas_call | solution.py:353
  58.6 1.3 collective-permute-start.13
  60.7 7.8 %all-to-all-done.2.groups_ref = f32[8,2,128,128]{3,2,1,0:T(8,128)S(1)} async-done(((f32[8,2,128,128]{3,2,1,0:T(8,128)}), f32[8,2,128,128]{3,2,1,0:T(8,128)S(1)}, u32[]{:S(2)}, u32[]{:S(2)}) %all-to-all-start.2) | async-done | bytes 1048608 | tf_op jit(solution)/shard_map/all_to_all | solution.py:349
  68.5 3.1 %shard_map.240 = f32[4,2,128,128]{3,2,1,0:T(8,128)} custom-call(s32[3]{0:T(128)S(1)} %pad_add_fusion.at_ref, f32[4,128,128]{2,1,0:T(8,128)S(1)} %copy-done.1, f32[4,128,128]{2,1,0:T(8,128)S(1)} %copy-done.2, f32[8,2,128,128]{3,2,1,0:T(8,128)S(1)} %all-to-all-done.2.groups_ref, f32[4,3,128,128]{3,2,1,0:T(8,128)S(1)} %all-to-all-done.1.maps_ref), custom_call_target="tpu_custom_call" | custom-call | flops 100000000 | bytes 4000000 | tf_op jit(solution)/shard_map/pallas_call | solution.py:353
  71.7 3.5 %all-to-all-start.3 = ((f32[4,2,128,128]{3,2,1,0:T(8,128)}), f32[4,2,128,128]{3,2,1,0:T(8,128)S(1)}, u32[]{:S(2)}, u32[]{:S(2)}) async-start(f32[4,2,128,128]{3,2,1,0:T(8,128)} %shard_map.240), calls=%async_computation.3 | async-start | bytes 1048576 | tf_op jit(solution)/shard_map/all_to_all | solution.py:349
  75.2 2.6 %collective-permute-done.14 = f32[3,2,128,128]{3,2,1,0:T(8,128)} collective-permute-done((f32[3,2,128,128]{3,2,1,0:T(8,128)S(1)}, f32[3,2,128,128]{3,2,1,0:T(8,128)}, u32[]{:S(2)}, u32[]{:S(2)}) %collective-permute-start.14) | collective-permute-done | bytes 393248 | tf_op jit(solution)/shard_map/ppermute | solution.py:373
  77.7 1.3 add_add_fusion
  79.1 4.1 %all-to-all-done.3.ends_ref = f32[4,2,128,128]{3,2,1,0:T(8,128)S(1)} async-done(((f32[4,2,128,128]{3,2,1,0:T(8,128)}), f32[4,2,128,128]{3,2,1,0:T(8,128)S(1)}, u32[]{:S(2)}, u32[]{:S(2)}) %all-to-all-start.3) | async-done | bytes 524320 | tf_op jit(solution)/shard_map/all_to_all | solution.py:349
  84.0 6.9 %shard_map.241 = (f32[128,512]{1,0:T(8,128)}, f32[128,512]{1,0:T(8,128)}, f32[128,512]{1,0:T(8,128)}, f32[1,4,128,128]{3,2,1,0:T(8,128)}, f32[8,128]{1,0:T(8,128)}, /*index=5*/f32[8,128]{1,0:T(8,128)}) custom-call(f32[4,2,128,128]{3,2,1,0:T(8,128)} %copy-done.8, f32[4,3,128,128]{3,2,1,0:T(8,128)} %get-tuple-element.40.maps_ref, bf16[128,512]{1,0:T(8,128)(2,1)} %q_ref.4, ...), custom_call_target="tpu_custom_call" | custom-call | flops 100000000 | bytes 4000000 | tf_op jit(solution)/shard_map/pallas_call | solution.py:353
  92.3 1.4 %shard_map.242 = f32[32,8,384]{2,1,0:T(8,128)} custom-call(f32[8,128]{1,0:T(8,128)S(1)} %copy-done.5, f32[8,128]{1,0:T(8,128)S(1)} %copy-done.7, bf16[128,8192]{1,0:T(8,128)(2,1)S(1)} %copy-done), custom_call_target="tpu_custom_call" | custom-call | flops 100000000 | bytes 4000000 | tf_op jit(solution)/shard_map/pallas_call | solution.py:353
  93.7 8.2 %all-to-all-start.4 = ((f32[32,8,384]{2,1,0:T(8,128)}), f32[32,8,384]{2,1,0:T(8,128)S(1)}, u32[]{:S(2)}, u32[]{:S(2)}) async-start(f32[32,8,384]{2,1,0:T(8,128)} %shard_map.242), calls=%async_computation.4 | async-start | bytes 786432 | tf_op jit(solution)/shard_map/all_to_all | solution.py:349
  101.9 2.5 %collective-permute-start.15 = (f32[2,128,128]{2,1,0:T(8,128)S(1)}, f32[2,128,128]{2,1,0:T(8,128)S(1)}, u32[]{:S(2)}, u32[]{:S(2)}) collective-permute-start(f32[2,128,128]{2,1,0:T(8,128)S(1)} %get-tuple-element.68), channel_id=1, source_target_pairs={{32,0},{64,32},{96,64},{128,96},{160,128},{192,160},{224,192},{33,... | collective-permute-start | bytes 393224 | tf_op jit(solution)/shard_map/ppermute | solution.py:369
  104.4 1.9 %collective-permute-start.16 = (f32[2,128,128]{2,1,0:T(8,128)S(1)}, f32[2,128,128]{2,1,0:T(8,128)S(1)}, u32[]{:S(2)}, u32[]{:S(2)}) collective-permute-start(f32[2,128,128]{2,1,0:T(8,128)S(1)} %get-tuple-element.69), channel_id=1, source_target_pairs={{64,0},{96,32},{128,64},{160,96},{192,128},{224,160},{65,1},{97,33... | collective-permute-start | bytes 393224 | tf_op jit(solution)/shard_map/ppermute | solution.py:369
  106.7 1.9 %collective-permute-start.7 = (f32[8,128]{1,0:T(8,128)S(1)}, f32[8,128]{1,0:T(8,128)S(1)}, u32[]{:S(2)}, u32[]{:S(2)}) collective-permute-start(f32[8,128]{1,0:T(8,128)S(1)} %copy-done.6), channel_id=1, source_target_pairs={{0,6},{1,7},{2,0},{3,1},{4,2},{5,3},{6,4},{7,5},{8,14},{9,15},{10,... | collective-permute-start | bytes 12296 | tf_op jit(solution)/shard_map/ppermute | solution.py:373
  108.6 7.0 %collective-permute-done.15 = f32[2,128,128]{2,1,0:T(8,128)S(1)} collective-permute-done((f32[2,128,128]{2,1,0:T(8,128)S(1)}, f32[2,128,128]{2,1,0:T(8,128)S(1)}, u32[]{:S(2)}, u32[]{:S(2)}) %collective-permute-start.15) | collective-permute-done | bytes 131104 | tf_op jit(solution)/shard_map/ppermute | solution.py:369
  115.6 6.3 %collective-permute-done.16 = f32[2,128,128]{2,1,0:T(8,128)S(1)} collective-permute-done((f32[2,128,128]{2,1,0:T(8,128)S(1)}, f32[2,128,128]{2,1,0:T(8,128)S(1)}, u32[]{:S(2)}, u32[]{:S(2)}) %collective-permute-start.16) | collective-permute-done | bytes 131104 | tf_op jit(solution)/shard_map/ppermute | solution.py:369
  121.9 1.9 %collective-permute-start.6 = (f32[8,128]{1,0:T(8,128)S(1)}, f32[8,128]{1,0:T(8,128)S(1)}, u32[]{:S(2)}, u32[]{:S(2)}) collective-permute-start(f32[8,128]{1,0:T(8,128)S(1)} %copy-done.6), channel_id=1, source_target_pairs={{0,5},{1,6},{2,7},{3,0},{4,1},{5,2},{6,3},{7,4},{8,13},{9,14},{10,... | collective-permute-start | bytes 12296 | tf_op jit(solution)/shard_map/ppermute | solution.py:373
  125.6 1.8 %collective-permute-start.3 = (f32[8,128]{1,0:T(8,128)S(1)}, f32[8,128]{1,0:T(8,128)S(1)}, u32[]{:S(2)}, u32[]{:S(2)}) collective-permute-start(f32[8,128]{1,0:T(8,128)S(1)} %copy-done.6), channel_id=1, source_target_pairs={{0,2},{1,3},{2,4},{3,5},{4,6},{5,7},{6,0},{7,1},{8,10},{9,11},{10,... | collective-permute-start | bytes 12296 | tf_op jit(solution)/shard_map/ppermute | solution.py:373
  130.4 1.2 collective-permute-done.2.refs_1_
  131.7 1.7 %shard_map.243 = f32[128,1024]{1,0:T(8,128)} custom-call(s32[3]{0:T(128)S(1)} %pad_add_fusion.at_ref, bf16[64,1024]{1,0:T(8,128)(2,1)S(1)} %bitcast.27, f32[8,128]{1,0:T(8,128)S(1)} %copy-done.6, f32[8,128]{1,0:T(8,128)S(1)} %collective-permute-done.2.refs_1_, f32[8,128]{1,0:T(8,128)S(1)} %collective-permute-done.3.refs_2_, ...), custom_call_target="tpu_custom_call" | custom-call | flops 100000000 | bytes 4000000 | tf_op jit(solution)/shard_map/pallas_call | solution.py:353
  (52 shorter events, 13.8 us)
Async XLA Ops:
  2.2 13.1 %all-to-all-start = ((bf16[8,8,1024]{2,1,0:T(8,128)(2,1)}), bf16[8,8,1024]{2,1,0:T(8,128)(2,1)S(1)}, u32[]{:S(2)}, u32[]{:S(2)}) async-start(bf16[8,8,1024]{2,1,0:T(8,128)(2,1)} %bitcast.9), calls=%async_computation | async-start | bytes 262144 | tf_op jit(solution)/shard_map/all_to_all | solution.py:349
  6.7 12.9 %copy-start.9 = (bf16[128,128]{1,0:T(8,128)(2,1)S(1)}, bf16[128,128]{1,0:T(8,128)(2,1)}, u32[]{:S(2)}) copy-start(bf16[128,128]{1,0:T(8,128)(2,1)} %param.28) | copy-start | bytes 98308
  6.7 12.9 %copy-start.10 = (bf16[128,128]{1,0:T(8,128)(2,1)S(1)}, bf16[128,128]{1,0:T(8,128)(2,1)}, u32[]{:S(2)}) copy-start(bf16[128,128]{1,0:T(8,128)(2,1)} %param.27) | copy-start | bytes 98308
  15.3 17.2 %all-to-all-start.1 = ((f32[4,3,128,128]{3,2,1,0:T(8,128)}), f32[4,3,128,128]{3,2,1,0:T(8,128)S(1)}, u32[]{:S(2)}, u32[]{:S(2)}) async-start(f32[4,3,128,128]{3,2,1,0:T(8,128)} %get-tuple-element.40.maps_ref), calls=%async_computation.1 | async-start | bytes 1572864 | tf_op jit(solution)/shard_map/all_to_all | solution.py:349
  19.7 9.4 %collective-permute-start = (bf16[2,128,128]{2,1,0:T(8,128)(2,1)S(1)}, bf16[2,128,128]{2,1,0:T(8,128)(2,1)S(1)}, u32[]{:S(2)}, u32[]{:S(2)}) collective-permute-start(bf16[2,128,128]{2,1,0:T(8,128)(2,1)S(1)} %get-tuple-element.73), channel_id=1, source_target_pairs={{0,32},{32,64},{64,96},{96,128},{128,160},{160,192},{192,224},{1,3... | collective-permute-start | bytes 196616 | tf_op jit(solution)/shard_map/ppermute | solution.py:369
  23.5 8.3 %collective-permute-start.1 = (bf16[2,128,128]{2,1,0:T(8,128)(2,1)S(1)}, bf16[2,128,128]{2,1,0:T(8,128)(2,1)S(1)}, u32[]{:S(2)}, u32[]{:S(2)}) collective-permute-start(bf16[2,128,128]{2,1,0:T(8,128)(2,1)S(1)} %get-tuple-element.73), channel_id=1, source_target_pairs={{0,64},{32,96},{64,128},{96,160},{128,192},{160,224},{1,65},{33,97... | collective-permute-start | bytes 196616 | tf_op jit(solution)/shard_map/ppermute | solution.py:369
  31.8 23.3 %copy-start.3 = (bf16[128,128]{1,0:T(8,128)(2,1)S(1)}, bf16[128,128]{1,0:T(8,128)(2,1)}, u32[]{:S(2)}) copy-start(bf16[128,128]{1,0:T(8,128)(2,1)} %q_ref.5) | copy-start | bytes 98308
  31.8 23.3 %copy-start.4 = (bf16[128,128]{1,0:T(8,128)(2,1)S(1)}, bf16[128,128]{1,0:T(8,128)(2,1)}, u32[]{:S(2)}) copy-start(bf16[128,128]{1,0:T(8,128)(2,1)} %g_ref.5) | copy-start | bytes 98308
  31.9 36.6 %copy-start.1 = (f32[4,128,128]{2,1,0:T(8,128)S(1)}, f32[4,128,128]{2,1,0:T(8,128)}, u32[]{:S(2)}) copy-start(f32[4,128,128]{2,1,0:T(8,128)} %start_ref.1) | copy-start | bytes 786436
  31.9 36.6 %copy-start.2 = (f32[4,128,128]{2,1,0:T(8,128)S(1)}, f32[4,128,128]{2,1,0:T(8,128)}, u32[]{:S(2)}) copy-start(f32[4,128,128]{2,1,0:T(8,128)} %end_ref.1) | copy-start | bytes 786436
  34.6 33.9 %all-to-all-start.2 = ((f32[8,2,128,128]{3,2,1,0:T(8,128)}), f32[8,2,128,128]{3,2,1,0:T(8,128)S(1)}, u32[]{:S(2)}, u32[]{:S(2)}) async-start(f32[8,2,128,128]{3,2,1,0:T(8,128)} %shard_map.239), calls=%async_computation.2 | async-start | bytes 2097152 | tf_op jit(solution)/shard_map/all_to_all | solution.py:349
  42.7 9.3 %collective-permute-start.11 = (bf16[3,2,128,128]{3,2,1,0:T(8,128)(2,1)S(1)}, bf16[3,2,128,128]{3,2,1,0:T(8,128)(2,1)S(1)}, u32[]{:S(2)}, u32[]{:S(2)}) collective-permute-start(bf16[3,2,128,128]{3,2,1,0:T(8,128)(2,1)S(1)} %pad_maximum_fusion.refs_0_), channel_id=1, source_target_pairs={{0,24},{8,0},{16,8},{24,16},{1,25},{9,1},{17,9},{25,17},{2,26},{10... | collective-permute-start | bytes 589832 | tf_op jit(solution)/shard_map/ppermute | solution.py:373
  45.2 7.9 %collective-permute-start.10 = (bf16[3,2,128,128]{3,2,1,0:T(8,128)(2,1)S(1)}, bf16[3,2,128,128]{3,2,1,0:T(8,128)(2,1)S(1)}, u32[]{:S(2)}, u32[]{:S(2)}) collective-permute-start(bf16[3,2,128,128]{3,2,1,0:T(8,128)(2,1)S(1)} %pad_maximum_fusion.refs_0_), channel_id=1, source_target_pairs={{0,16},{8,24},{16,0},{24,8},{1,17},{9,25},{17,1},{25,9},{2,18},{10... | collective-permute-start | bytes 589832 | tf_op jit(solution)/shard_map/ppermute | solution.py:373
  46.1 9.1 %collective-permute-start.9 = (bf16[3,2,128,128]{3,2,1,0:T(8,128)(2,1)S(1)}, bf16[3,2,128,128]{3,2,1,0:T(8,128)(2,1)S(1)}, u32[]{:S(2)}, u32[]{:S(2)}) collective-permute-start(bf16[3,2,128,128]{3,2,1,0:T(8,128)(2,1)S(1)} %pad_maximum_fusion.refs_0_), channel_id=1, source_target_pairs={{0,8},{8,16},{16,24},{24,0},{1,9},{9,17},{17,25},{25,1},{2,10},{10... | collective-permute-start | bytes 589832 | tf_op jit(solution)/shard_map/ppermute | solution.py:373
  58.0 17.1 %collective-permute-start.12 = (f32[3,2,128,128]{3,2,1,0:T(8,128)}, f32[3,2,128,128]{3,2,1,0:T(8,128)}, u32[]{:S(2)}, u32[]{:S(2)}) collective-permute-start(f32[3,2,128,128]{3,2,1,0:T(8,128)} %get-tuple-element.63), channel_id=1, source_target_pairs={{0,24},{8,0},{16,8},{24,16},{1,25},{9,1},{17,9},{25,17},{2,26},{10... | collective-permute-start | bytes 1179656 | tf_op jit(solution)/shard_map/ppermute | solution.py:373
  58.6 16.5 %collective-permute-start.13 = (f32[3,2,128,128]{3,2,1,0:T(8,128)}, f32[3,2,128,128]{3,2,1,0:T(8,128)}, u32[]{:S(2)}, u32[]{:S(2)}) collective-permute-start(f32[3,2,128,128]{3,2,1,0:T(8,128)} %get-tuple-element.64), channel_id=1, source_target_pairs={{0,16},{8,24},{16,0},{24,8},{1,17},{9,25},{17,1},{25,9},{2,18},{10... | collective-permute-start | bytes 1179656 | tf_op jit(solution)/shard_map/ppermute | solution.py:373
  59.9 17.8 %collective-permute-start.14 = (f32[3,2,128,128]{3,2,1,0:T(8,128)S(1)}, f32[3,2,128,128]{3,2,1,0:T(8,128)}, u32[]{:S(2)}, u32[]{:S(2)}) collective-permute-start(f32[3,2,128,128]{3,2,1,0:T(8,128)S(1)} %get-tuple-element.65), channel_id=1, source_target_pairs={{0,8},{8,16},{16,24},{24,0},{1,9},{9,17},{17,25},{25,1},{2,10},{10... | collective-permute-start | bytes 1179656 | tf_op jit(solution)/shard_map/ppermute | solution.py:373
  71.7 11.6 %all-to-all-start.3 = ((f32[4,2,128,128]{3,2,1,0:T(8,128)}), f32[4,2,128,128]{3,2,1,0:T(8,128)S(1)}, u32[]{:S(2)}, u32[]{:S(2)}) async-start(f32[4,2,128,128]{3,2,1,0:T(8,128)} %shard_map.240), calls=%async_computation.3 | async-start | bytes 1048576 | tf_op jit(solution)/shard_map/all_to_all | solution.py:349
  79.1 11.8 %copy-start = (bf16[128,8192]{1,0:T(8,128)(2,1)S(1)}, bf16[128,8192]{1,0:T(8,128)(2,1)}, u32[]{:S(2)}) copy-start(bf16[128,8192]{1,0:T(8,128)(2,1)} %x_ref.3) | copy-start | bytes 6291460
  83.2 0.8 copy-start.8
  90.9 0.7 copy-start.5
  92.3 14.0 %copy-start.6 = (f32[8,128]{1,0:T(8,128)S(1)}, f32[8,128]{1,0:T(8,128)}, u32[]{:S(2)}) copy-start(f32[8,128]{1,0:T(8,128)} %get-tuple-element.58.d_ref.refs_0_) | copy-start | bytes 12292
  93.7 39.6 %all-to-all-start.4 = ((f32[32,8,384]{2,1,0:T(8,128)}), f32[32,8,384]{2,1,0:T(8,128)S(1)}, u32[]{:S(2)}, u32[]{:S(2)}) async-start(f32[32,8,384]{2,1,0:T(8,128)} %shard_map.242), calls=%async_computation.4 | async-start | bytes 786432 | tf_op jit(solution)/shard_map/all_to_all | solution.py:349
  101.9 13.6 %collective-permute-start.15 = (f32[2,128,128]{2,1,0:T(8,128)S(1)}, f32[2,128,128]{2,1,0:T(8,128)S(1)}, u32[]{:S(2)}, u32[]{:S(2)}) collective-permute-start(f32[2,128,128]{2,1,0:T(8,128)S(1)} %get-tuple-element.68), channel_id=1, source_target_pairs={{32,0},{64,32},{96,64},{128,96},{160,128},{192,160},{224,192},{33,... | collective-permute-start | bytes 393224 | tf_op jit(solution)/shard_map/ppermute | solution.py:369
  104.4 17.5 %collective-permute-start.16 = (f32[2,128,128]{2,1,0:T(8,128)S(1)}, f32[2,128,128]{2,1,0:T(8,128)S(1)}, u32[]{:S(2)}, u32[]{:S(2)}) collective-permute-start(f32[2,128,128]{2,1,0:T(8,128)S(1)} %get-tuple-element.69), channel_id=1, source_target_pairs={{64,0},{96,32},{128,64},{160,96},{192,128},{224,160},{65,1},{97,33... | collective-permute-start | bytes 393224 | tf_op jit(solution)/shard_map/ppermute | solution.py:369
  106.3 19.3 %collective-permute-start.8 = (f32[8,128]{1,0:T(8,128)S(1)}, f32[8,128]{1,0:T(8,128)S(1)}, u32[]{:S(2)}, u32[]{:S(2)}) collective-permute-start(f32[8,128]{1,0:T(8,128)S(1)} %copy-done.6), channel_id=1, source_target_pairs={{0,7},{1,0},{2,1},{3,2},{4,3},{5,4},{6,5},{7,6},{8,15},{9,8},{10,9... | collective-permute-start | bytes 12296 | tf_op jit(solution)/shard_map/ppermute | solution.py:373
  106.7 20.7 %collective-permute-start.7 = (f32[8,128]{1,0:T(8,128)S(1)}, f32[8,128]{1,0:T(8,128)S(1)}, u32[]{:S(2)}, u32[]{:S(2)}) collective-permute-start(f32[8,128]{1,0:T(8,128)S(1)} %copy-done.6), channel_id=1, source_target_pairs={{0,6},{1,7},{2,0},{3,1},{4,2},{5,3},{6,4},{7,5},{8,14},{9,15},{10,... | collective-permute-start | bytes 12296 | tf_op jit(solution)/shard_map/ppermute | solution.py:373
  121.9 6.5 %collective-permute-start.6 = (f32[8,128]{1,0:T(8,128)S(1)}, f32[8,128]{1,0:T(8,128)S(1)}, u32[]{:S(2)}, u32[]{:S(2)}) collective-permute-start(f32[8,128]{1,0:T(8,128)S(1)} %copy-done.6), channel_id=1, source_target_pairs={{0,5},{1,6},{2,7},{3,0},{4,1},{5,2},{6,3},{7,4},{8,13},{9,14},{10,... | collective-permute-start | bytes 12296 | tf_op jit(solution)/shard_map/ppermute | solution.py:373
  123.8 5.1 %collective-permute-start.5 = (f32[8,128]{1,0:T(8,128)S(1)}, f32[8,128]{1,0:T(8,128)S(1)}, u32[]{:S(2)}, u32[]{:S(2)}) collective-permute-start(f32[8,128]{1,0:T(8,128)S(1)} %copy-done.6), channel_id=1, source_target_pairs={{0,4},{1,5},{2,6},{3,7},{4,0},{5,1},{6,2},{7,3},{8,12},{9,13},{10,... | collective-permute-start | bytes 12296 | tf_op jit(solution)/shard_map/ppermute | solution.py:373
  124.9 4.5 %collective-permute-start.4 = (f32[8,128]{1,0:T(8,128)S(1)}, f32[8,128]{1,0:T(8,128)S(1)}, u32[]{:S(2)}, u32[]{:S(2)}) collective-permute-start(f32[8,128]{1,0:T(8,128)S(1)} %copy-done.6), channel_id=1, source_target_pairs={{0,3},{1,4},{2,5},{3,6},{4,7},{5,0},{6,1},{7,2},{8,11},{9,12},{10,... | collective-permute-start | bytes 12296 | tf_op jit(solution)/shard_map/ppermute | solution.py:373
  125.6 4.8 %collective-permute-start.3 = (f32[8,128]{1,0:T(8,128)S(1)}, f32[8,128]{1,0:T(8,128)S(1)}, u32[]{:S(2)}, u32[]{:S(2)}) collective-permute-start(f32[8,128]{1,0:T(8,128)S(1)} %copy-done.6), channel_id=1, source_target_pairs={{0,2},{1,3},{2,4},{3,5},{4,6},{5,7},{6,0},{7,1},{8,10},{9,11},{10,... | collective-permute-start | bytes 12296 | tf_op jit(solution)/shard_map/ppermute | solution.py:373
  127.4 4.2 %collective-permute-start.2 = (f32[8,128]{1,0:T(8,128)S(1)}, f32[8,128]{1,0:T(8,128)S(1)}, u32[]{:S(2)}, u32[]{:S(2)}) collective-permute-start(f32[8,128]{1,0:T(8,128)S(1)} %copy-done.6), channel_id=1, source_target_pairs={{0,1},{1,2},{2,3},{3,4},{4,5},{5,6},{6,7},{7,0},{8,9},{9,10},{10,1... | collective-permute-start | bytes 12296 | tf_op jit(solution)/shard_map/ppermute | solution.py:373
  (1 other events, 0.7 us)

commit v3 on v2

--- a/solution.py
+++ b/solution.py
@@ -58,16 +58,47 @@
 
 
 def prepare_kernel(
-    x_ref, w_ref, rate_ref, bias_ref, q_ref, k_ref, v_ref, g_ref,
+    at_ref, x_hbm, wb_ref, wd_ref, rate_ref, bias_ref, q_ref, k_ref, v_ref, g_ref,
     maps_ref, inv_ref, ratio_ref, rk_ref, p_ref, w_out_ref, y_ref, du_ref, rows_ref, cols_ref,
+    *rest,
 ):
+    chunk_refs, (w_ref, x_ref, sem) = rest[:-3], rest[-3:]
+    fetch = pltpu.make_async_copy(x_hbm, x_ref, sem)
+    fetch.start()
     heads = maps_ref.shape[0]
+    w_ref[...] = jnp.concatenate(
+        [wb_ref[...].astype(F32), wd_ref[...].astype(F32)], axis=0
+    ).astype(BF16)
+    count = len(chunk_refs)
+    size = w_ref.shape[1] // count
+    for d, chunk_ref in enumerate(chunk_refs):
+        to = at_ref[2] + d
+        to = jnp.where(to >= count, to - count, to)
+        chunk_ref[...] = w_ref[:, pl.ds(pl.multiple_of(to * size, size), size)]
     row, lane = ids((T, T))
     lower, strict = row >= lane, row > lane
     eye = jnp.where(row == lane, 1.0, 0.0)
+    hs = range(heads)
+    span = [slice(h * T, (h + 1) * T) for h in hs]
+    k = [k_ref[:, span[h]] for h in hs]
+    q = [q_ref[:, span[h]] for h in hs]
+    v = [v_ref[:, span[h]] for h in hs]
+    g = [g_ref[:, span[h]] for h in hs]
+    norm_k, norm_q = [], []
+    for h in hs:
+        kf, qf = k[h].astype(F32), q[h].astype(F32)
+        norm_k.append(lax.rsqrt(jnp.sum(kf * kf, axis=1, keepdims=True) + 1e-6))
+        norm_q.append(lax.rsqrt(jnp.sum(qf * qf, axis=1, keepdims=True) + 1e-6))
+    norm_rows = place(norm_k + norm_q, lane).T
+    norm_k_row = norm_rows[:heads]
+    norm_q_row = norm_rows[heads : 2 * heads]
+    for h in hs:
+        rk_ref[h] = mm(k[h], k[h], NT) * norm_k[h] * norm_k_row[h : h + 1]
+        p_ref[h] = mm(q[h], k[h], NT) * (norm_q[h] * (1.0 / math.sqrt(T))) * norm_k_row[h : h + 1]
+    rates = jnp.concatenate([jnp.full((1, T), rate_ref[h], F32) for h in hs], axis=0)
+    biases = jnp.concatenate([jnp.full((1, T), bias_ref[h], F32) for h in hs], axis=0)
+    fetch.wait()
     logits = lax.dot_general(w_ref[...], x_ref[...], NT, preferred_element_type=F32)
-    rates = jnp.concatenate([jnp.full((1, T), rate_ref[h], F32) for h in range(heads)], axis=0)
-    biases = jnp.concatenate([jnp.full((1, T), bias_ref[h], F32) for h in range(heads)], axis=0)
     beta_row = jax.nn.sigmoid(logits[:heads])
     shifted = logits[heads:] + biases
     soft = jnp.maximum(shifted, 0.0) + jnp.log1p(jnp.exp(-jnp.abs(shifted)))
@@ -75,35 +106,14 @@
     upper_ones = jnp.where(row <= lane, 1.0, 0.0).astype(BF16)
     cum_row = mm(split3(decay_row), upper_ones, NN)
     gate_slope = -jnp.exp(rates) * jax.nn.sigmoid(shifted)
-    packed = jnp.concatenate(
-        [beta_row, cum_row, jnp.zeros((T - 2 * heads, T), F32)], axis=0
-    )
-    turned = packed.T
-    hs = range(heads)
-    span = [slice(h * T, (h + 1) * T) for h in hs]
-    k = [k_ref[:, span[h]] for h in hs]
-    q = [q_ref[:, span[h]] for h in hs]
-    v = [v_ref[:, span[h]] for h in hs]
-    g = [g_ref[:, span[h]] for h in hs]
+    turned = jnp.concatenate([beta_row, cum_row, jnp.zeros((T - 2 * heads, T), F32)], axis=0).T
     beta_c = [turned[:, h : h + 1] for h in hs]
     cum_c = [turned[:, heads + h : heads + h + 1] for h in hs]
-    norm_k, norm_q = [], []
-    for h in hs:
-        kf, qf = k[h].astype(F32), q[h].astype(F32)
-        norm_k.append(lax.rsqrt(jnp.sum(kf * kf, axis=1, keepdims=True) + 1e-6))
-        norm_q.append(
-            lax.rsqrt(jnp.sum(qf * qf, axis=1, keepdims=True) + 1e-6)
-        )
-    norms = place(norm_k + norm_q, lane)
-    norm_rows = norms.T
-    norm_k_row = norm_rows[:heads]
-    norm_q_row = norm_rows[heads : 2 * heads]
     last = cum_row[:, T - 1 : T]
     rows_ref[...] = jnp.concatenate(
         [beta_row, cum_row, norm_k_row, norm_q_row, decay_row, gate_slope], axis=0
     )
-    col_list = beta_c + cum_c + norm_k + norm_q
-    cols_ref[...] = place(col_list, lane)
+    cols_ref[...] = place(beta_c + cum_c + norm_k + norm_q, lane)
     scale = 1.0 / math.sqrt(T)
     ratio, solve, low = [], [], []
     for h in hs:
@@ -112,8 +122,7 @@
         )
         ratio.append(r)
         ratio_ref[h] = r
-        kk = mm(k[h], k[h], NT) * norm_k[h] * norm_k_row[h : h + 1]
-        rk = jnp.where(strict, r * kk, 0.0)
+        rk = jnp.where(strict, r * rk_ref[h], 0.0)
         rk_ref[h] = rk
         low.append(rk * beta_c[h])
     for h in hs:
@@ -137,7 +146,7 @@
         y = mm(split(solve[h] * (bv * grow_row * norm_k_row[h : h + 1])), k[h], NN)
         w_out_ref[h] = w
         y_ref[h] = y
-        p = ratio[h] * mm(q[h], k[h], NT) * (norm_q[h] * scale) * norm_k_row[h : h + 1]
+        p = ratio[h] * p_ref[h]
         p_ref[h] = p
         du = mm(split(p), g[h], TN)
         du_ref[h] = du
@@ -188,9 +197,11 @@
 
 def finish_kernel(
     ends_ref, maps_ref, q_ref, k_ref, v_ref, g_ref, inv_ref, ratio_ref, rk_ref, p_ref, w_ref,
-    y_ref, du_ref, rows_ref, cols_ref,
-    dq_ref, dk_ref, dv_ref, bound_ref, logit_ref, param_ref,
+    y_ref, du_ref, rows_ref, cols_ref, x_hbm,
+    dq_ref, dk_ref, dv_ref, bound_ref, logit_ref, term_ref, x_ref, sem,
 ):
+    fetch = pltpu.make_async_copy(x_hbm, x_ref, sem)
+    fetch.start()
     heads = maps_ref.shape[0]
     hs = range(heads)
     row, lane = ids((T, T))
@@ -260,27 +271,36 @@
     beta_row = rows[:heads]
     dbeta = turned[heads : 2 * heads] * beta_row * (1.0 - beta_row)
     dshift = ddecay * rows[5 * heads : 6 * heads]
-    logit_ref[...] = jnp.concatenate([dbeta, dshift], axis=0)
+    logit = jnp.concatenate([dbeta, dshift], axis=0)
+    logit_ref[...] = logit
     rate_sum = jnp.sum(ddecay * rows[4 * heads : 5 * heads], axis=1, keepdims=True)
     bias_sum = jnp.sum(dshift, axis=1, keepdims=True)
-    param_ref[...] = jnp.broadcast_to(
-        jnp.concatenate([rate_sum, bias_sum], axis=0), (2 * heads, T)
-    )
-
-
-def window_kernel(at_ref, q_ref, g_ref, *refs):
-    kv_refs, dq_ref, dkv_refs = refs[:4], refs[4], refs[5:]
+    param = jnp.broadcast_to(jnp.concatenate([rate_sum, bias_sum], axis=0), (2 * heads, T))
+    high, low = split(logit)
+    fetch.wait()
+    pieces = term_ref.shape[0]
+    width = x_ref.shape[1] // pieces
+    for s in range(pieces):
+        x = x_ref[:, s * width : (s + 1) * width]
+        term_ref[s, :, :width] = lax.dot_general(
+            high, x, NN, preferred_element_type=F32
+        ) + lax.dot_general(low, x, NN, preferred_element_type=F32)
+        term_ref[s, :, width:] = param
+
+
+def window_kernel(at_ref, q_ref, g_ref, own_ref, near_ref, far_ref, dq_ref, stat_ref):
+    kv_refs = (own_ref, near_ref, far_ref)
     z, x = at_ref[0], at_ref[1]
     row, lane = ids((T, T))
     gap = row - lane
     scale = 1.0 / math.sqrt(T)
     q, g = q_ref[...], g_ref[...]
-    scores, slopes = [], []
+    scores = []
     tiles = [(a, b) for a in range(4) for b in range(3)]
     for a, b in tiles:
         spread = gap + (jnp.where(x >= a, a, a - 4) + 4 * b) * T
         ok = (spread >= 0) & (spread < jnp.where(z >= b, WINDOW, 0))
-        s = lax.dot_general(q, kv_refs[a][b, 0], NT, preferred_element_type=F32) * scale
+        s = lax.dot_general(q, kv_refs[b][a, 0], NT, preferred_element_type=F32) * scale
         scores.append(jnp.where(ok, s, -1e30))
     top = scores[0]
     for s in scores[1:]:
@@ -292,49 +312,61 @@
         total = total + w
     total = 1.0 / jnp.sum(total, axis=1, keepdims=True)
     weights = [w * total for w in weights]
-    terms = None
+    slopes, terms = [], None
     for (a, b), w in zip(tiles, weights):
-        slope = lax.dot_general(g, kv_refs[a][b, 1], NT, preferred_element_type=F32)
+        slope = lax.dot_general(g, kv_refs[b][a, 1], NT, preferred_element_type=F32)
         slopes.append(slope)
         terms = w * slope if terms is None else terms + w * slope
     terms = jnp.sum(terms, axis=1, keepdims=True)
+    stat_ref[...] = place([top, total, terms], lane).T[:8]
     dq = None
     for (a, b), w, slope in zip(tiles, weights, slopes):
-        ds = split(w * (slope - terms) * scale)
-        part = mm(ds, kv_refs[a][b, 0], NN)
+        part = mm(split(w * (slope - terms) * scale), kv_refs[b][a, 0], NN)
         dq = part if dq is None else dq + part
-        dkv_refs[a][b, 0] = mm(ds, q, TN)
-        dkv_refs[a][b, 1] = mm(split(w), g, TN)
     dq_ref[...] = dq
 
 
-def input_kernel(at_ref, w_ref, *refs):
-    rows_refs, out_ref, all_ref = refs[:-2], refs[-2], refs[-1]
-    head, count = at_ref[2], len(rows_refs)
-    for d, rows_ref in enumerate(rows_refs):
-        source = jnp.where(head >= d, head - d, head - d + count)
-        all_ref[pl.ds(pl.multiple_of(source * 8, 8), 8), :] = rows_ref[...]
-    high, low = split(all_ref[...])
-    w = w_ref[...]
+def key_kernel(
+    at_ref, k_ref, v_ref, own_ref, near_ref, far_ref, own_stat, near_stat, far_stat, dk_ref, dv_ref
+):
+    qg_refs, stat_refs = (own_ref, near_ref, far_ref), (own_stat, near_stat, far_stat)
+    z, x, count = at_ref[0], at_ref[1], at_ref[3]
+    row, lane = ids((T, T))
+    gap = lane - row
+    scale = 1.0 / math.sqrt(T)
+    k, v = k_ref[...], v_ref[...]
+    dk, dv = jnp.zeros((T, T), F32), jnp.zeros((T, T), F32)
+    for b in range(3):
+        for a in range(4):
+            spread = gap + (jnp.where(x >= a, -a, 4 - a) + 4 * b) * T
+            ok = (spread >= 0) & (spread < jnp.where(z + b < count, WINDOW, 0))
+            q, g, stat = qg_refs[b][a, 0], qg_refs[b][a, 1], stat_refs[b][a]
+            s = lax.dot_general(k, q, NT, preferred_element_type=F32) * scale
+            w = jnp.exp(jnp.where(ok, s - stat[0:1], -1e30)) * stat[1:2]
+            slope = lax.dot_general(v, g, NT, preferred_element_type=F32)
+            dv = dv + mm(split(w), g, NN)
+            dk = dk + mm(split(w * (slope - stat[2:3]) * scale), q, NN)
+    dk_ref[...] = dk
+    dv_ref[...] = dv
+
+
+def input_kernel(*refs):
+    count = (len(refs) - 3) // 2
+    row_refs, chunk_refs = refs[:count], refs[count : 2 * count]
+    out_ref, rows_ref, w_ref = refs[2 * count :]
+    for d in range(count):
+        rows_ref[8 * d : 8 * d + 8, :] = row_refs[d][...]
+        w_ref[8 * d : 8 * d + 8, :] = chunk_refs[d][...].astype(F32)
+    high, low = split(rows_ref[...])
+    w = w_ref[...].astype(BF16)
     out_ref[...] = lax.dot_general(high, w, TN, preferred_element_type=F32) + lax.dot_general(
         low, w, TN, preferred_element_type=F32
     )
 
 
-def weight_kernel(d_ref, param_ref, x_ref, out_ref):
-    high, low = split(d_ref[...])
-    pieces = out_ref.shape[0]
-    width = x_ref.shape[1] // pieces
-    for s in range(pieces):
-        x = x_ref[:, s * width : (s + 1) * width]
-        out_ref[s, :, :width] = lax.dot_general(
-            high, x, NN, preferred_element_type=F32
-        ) + lax.dot_general(low, x, NN, preferred_element_type=F32)
-        out_ref[s, :, width:] = param_ref[...]
-
-
 VM = pl.BlockSpec(memory_space=pltpu.VMEM)
 SM = pl.BlockSpec(memory_space=pltpu.SMEM)
+ANY = pl.BlockSpec(memory_space=pl.ANY)
 
 
 def f32(*shape):
@@ -384,39 +416,49 @@
     width = layer_input.shape[1]
     pieces = z_count * x_count
     at = jnp.stack(
-        [lax.axis_index("seq_0"), lax.axis_index("seq_1"), lax.axis_index("head")]
+        [lax.axis_index("seq_0"), lax.axis_index("seq_1"), lax.axis_index("head"), z_count]
     ).astype(jnp.int32)
-
-    pair = jnp.stack([attn_key, attn_value])
-    near, far = up_by(pair, 1, z_count), up_by(pair, 2, z_count)
-    both_weights = jnp.concatenate([beta_weight, decay_weight], axis=0)
-    weight_cols = jnp.swapaxes(both_weights.reshape(2 * heads, head_count, -1), 0, 1)
-    weight_cols = exchange(weight_cols, "head")
-    weight_cols = weight_cols.reshape(head_count * 2 * heads, -1)
-
-    maps, inv, ratio, rk, p, w, y, du, rows, cols = call(
+    others = range(1, x_count)
+
+    mine = jnp.stack([attn_key, attn_value, attn_query, attn_out_grad])
+    line = [mine] + [turn(mine, "seq_1", d, x_count) for d in others]
+
+    bf16_chunk = jax.ShapeDtypeStruct((2 * heads, width // head_count), BF16)
+    maps, inv, ratio, rk, p, w, y, du, rows, cols, *chunks = call(
         prepare_kernel,
-        (f32(heads, 3, T, T),) + (f32(heads, T, T),) * 7 + (f32(6 * heads, T), f32(T, T)),
-        [VM, VM, SM, SM, VM, VM, VM, VM],
-        layer_input, both_weights, log_rate, decay_bias, delta_query, delta_key, delta_value,
-        delta_out_grad,
+        (f32(heads, 3, T, T),) + (f32(heads, T, T),) * 7 + (f32(6 * heads, T), f32(T, T))
+        + (bf16_chunk,) * head_count,
+        [SM, ANY, VM, VM, SM, SM, VM, VM, VM, VM],
+        at, layer_input, beta_weight, decay_weight, log_rate, decay_bias, delta_query, delta_key,
+        delta_value, delta_out_grad,
+        scratch=[
+            pltpu.VMEM((2 * heads, width), BF16), pltpu.VMEM((T, width), BF16),
+            pltpu.SemaphoreType.DMA,
+        ],
         limit=WHOLE,
     )
-    maps, weight_cols = lax.optimization_barrier((maps, weight_cols))
     blocks = exchange(maps, "seq_1")
+    kv, qg = jnp.stack([a[:2] for a in line]), jnp.stack([a[2:] for a in line])
+    kv_all = [kv] + [up_by(kv, d, z_count) for d in (1, 2)]
+    qg_all = [qg] + [up_by(qg, -d, z_count) for d in (1, 2)]
     groups = call(group_kernel, f32(z_count, 2, T, T), [SM, VM], at, blocks)
 
-    triple = jnp.stack([pair, near, far])
-    triple, groups = lax.optimization_barrier((triple, groups))
     groups = exchange(groups, "seq_0")
-    windows = [triple] + [turn(triple, "seq_1", d, x_count) for d in range(1, x_count)]
-    dq_attn, *dkv = call(
+    dq_attn, stat = call(
         window_kernel,
-        (f32(T, T),) + (f32(3, 2, T, T),) * x_count,
-        [SM] + [VM] * (2 + x_count),
-        at, attn_query, attn_out_grad, *windows,
-    )
-    dkv = [dkv[0]] + [turn(dkv[d], "seq_1", -d, x_count) for d in range(1, x_count)]
+        (f32(T, T), f32(8, T)),
+        [SM] + [VM] * 5,
+        at, attn_query, attn_out_grad, *kv_all,
+    )
+    stat = jnp.stack([stat] + [turn(stat, "seq_1", d, x_count) for d in others])
+    stat_all = [stat] + [up_by(stat, -d, z_count) for d in (1, 2)]
+    dk_attn, dv_attn = call(
+        key_kernel,
+        (f32(T, T), f32(T, T)),
+        [SM] + [VM] * 8,
+        at, attn_key, attn_value, *qg_all, *stat_all,
+    )
+    chunks = [chunks[0]] + [turn(chunks[d], "head", d, head_count) for d in range(1, head_count)]
 
     ends = call(
         spread_kernel,
@@ -426,40 +468,35 @@
     )
     ends = exchange(ends, "seq_1")
 
-    dq, dk, dv, bound, logit, param = call(
+    dq, dk, dv, bound, logit, terms = call(
         finish_kernel,
-        (f32(T, heads * T),) * 3 + (f32(1, heads, T, T), f32(2 * heads, T), f32(2 * heads, T)),
-        [VM] * 15,
+        (f32(T, heads * T),) * 3
+        + (f32(1, heads, T, T), f32(2 * heads, T), f32(pieces, 2 * heads, width // pieces + T)),
+        [VM] * 15 + [ANY],
         ends, maps, delta_query, delta_key, delta_value, delta_out_grad, inv, ratio, rk, p, w, y,
-        du, rows, cols,
+        du, rows, cols, layer_input,
+        scratch=[pltpu.VMEM((T, width), BF16), pltpu.SemaphoreType.DMA],
         limit=WHOLE,
     )
-    terms = call(
-        weight_kernel,
-        f32(pieces, 2 * heads, width // pieces + T),
-        [VM, VM, VM],
-        logit, param, layer_input,
-    )
-    terms, logit = lax.optimization_barrier((terms, logit))
     terms = exchange(terms, SEQ)
     every = [logit] + [turn(logit, "head", d, head_count) for d in range(1, head_count)]
-    dkv = sum(dkv[1:], dkv[0])
-    dkv_near, dkv_far = up_by(dkv[1], -1, z_count), up_by(dkv[2], -2, z_count)
     input_grad = call(
         input_kernel,
-        f32(T, weight_cols.shape[1]),
-        [SM] + [VM] * (1 + head_count),
-        at, weight_cols, *every,
-        scratch=[pltpu.VMEM((2 * heads * head_count, T), F32)],
+        f32(T, width // head_count),
+        [VM] * (2 * head_count),
+        *every, *chunks,
+        scratch=[
+            pltpu.VMEM((2 * heads * head_count, T), F32),
+            pltpu.VMEM((2 * heads * head_count, width // head_count), F32),
+        ],
     )
     terms = jnp.sum(terms, axis=0)
     part = width // pieces
-    total = dkv[0] + dkv_near + dkv_far
     return (
         dq, dk, dv, bound, input_grad,
         terms[:heads, :part], terms[heads:, :part],
         terms[:heads, part], terms[heads:, part],
-        dq_attn, total[0], total[1],
+        dq_attn, dk_attn, dv_attn,
     )
 
 

time: 135 us -> 154 us (1.14)
  the two profiles are of different devices: /device:TPU:64 before, /device:TPU:233 now
where the time goes in v3:
time: 154 us
  starting transfers between devices  74.6 us (48%)
  waiting for transfers between devices  30.5 us (20%)
  Pallas kernels  29.4 us (19%)
  blocking collectives  15.5 us (10%)
  local copies, waits for them, and re-layouts  2.17 us (1%)
    ppermute x20, starting transfers between devices, turn(): lax.ppermute(value, axis, [(i, (i + by) % count) for i in range(count)])  32.5 us
    pallas_call x7, Pallas kernels, run(): pl.pallas_call(kernel, out_shape=outs, in_specs=specs, out_specs=jax.tree...  29.4 us
    all_to_all x3, starting transfers between devices, exchange(): return lax.all_to_all(value, axis, split_axis=0, concat_axis=0, tiled=True)  25.6 us
    all_to_all x3, waiting for transfers between devices, exchange(): return lax.all_to_all(value, axis, split_axis=0, concat_axis=0, tiled=True)  23.1 us
    ppermute x6, starting transfers between devices, up_by(): return lax.ppermute(value, 'seq_0', pairs)  16.4 us
    all_to_all x1, blocking collectives, exchange(): return lax.all_to_all(value, axis, split_axis=0, concat_axis=0, tiled=True)  15.5 us
    ppermute x6, waiting for transfers between devices, up_by(): return lax.ppermute(value, 'seq_0', pairs)  6.48 us
  transfers between devices with their start and end apart: 29, of which 4 were waited for; matrix products, arithmetic and copies ran while one was open for 0% of the time, Pallas kernels for 12%

profile of v3, /device:TPU:233, one launch (start us, length us, event | category | flops | bytes accessed | tf_op | source)
XLA Modules:
  0.0 153.9 jit_solution(962061610500272299)
XLA Ops:
  1.2 9.0 %shard_map.238 = (f32[4,3,128,128]{3,2,1,0:T(8,128)}, f32[4,128,128]{2,1,0:T(8,128)}, f32[4,128,128]{2,1,0:T(8,128)}, f32[4,128,128]{2,1,0:T(8,128)}, f32[4,128,...) custom-call(s32[4]{0:T(128)} %pad_add_fusion.at_ref, ...), custom_call_target="tpu_custom_call" | custom-call | flops 100000000 | bytes 4000000 | tf_op jit(solution)/shard_map/pallas_call | solution.py:385
  10.2 15.5 %all_to_all.20.maps_ref = f32[4,3,128,128]{3,2,1,0:T(8,128)S(1)} all-to-all(f32[4,3,128,128]{3,2,1,0:T(8,128)} %get-tuple-element.40.maps_ref), channel_id=1, replica_groups=mesh['seq_0'=8,'seq_1'=4,'head'=8] {'seq_1'}, dimensions={0} | all-to-all | bytes 1572864 | tf_op jit(solution)/shard_map/all_to_all | solution.py:381
  25.7 2.1 %shard_map.239 = f32[8,2,128,128]{3,2,1,0:T(8,128)} custom-call(s32[4]{0:T(128)S(1)} %copy-done.6, f32[4,3,128,128]{3,2,1,0:T(8,128)S(1)} %all_to_all.20.maps_ref), custom_call_target="tpu_custom_call" | custom-call | flops 100000000 | bytes 4000000 | tf_op jit(solution)/shard_map/pallas_call | solution.py:385
  27.8 5.3 %all-to-all-start.1 = ((f32[8,2,128,128]{3,2,1,0:T(8,128)}), f32[8,2,128,128]{3,2,1,0:T(8,128)S(1)}, u32[]{:S(2)}, u32[]{:S(2)}) async-start(f32[8,2,128,128]{3,2,1,0:T(8,128)} %shard_map.239), calls=%async_computation.1 | async-start | bytes 2097152 | tf_op jit(solution)/shard_map/all_to_all | solution.py:381
  33.1 1.0 collective-permute-start.16
  34.1 1.2 collective-permute-start.15
  35.3 16.3 %all-to-all-done.1.groups_ref = f32[8,2,128,128]{3,2,1,0:T(8,128)S(1)} async-done(((f32[8,2,128,128]{3,2,1,0:T(8,128)}), f32[8,2,128,128]{3,2,1,0:T(8,128)S(1)}, u32[]{:S(2)}, u32[]{:S(2)}) %all-to-all-start.1) | async-done | bytes 1048608 | tf_op jit(solution)/shard_map/all_to_all | solution.py:381
  51.6 3.1 %shard_map.240 = f32[4,2,128,128]{3,2,1,0:T(8,128)} custom-call(s32[4]{0:T(128)S(1)} %copy-done.6, f32[4,128,128]{2,1,0:T(8,128)S(1)} %copy-done.4, f32[4,128,128]{2,1,0:T(8,128)S(1)} %copy-done.5, f32[8,2,128,128]{3,2,1,0:T(8,128)S(1)} %all-to-all-done.1.groups_ref, f32[4,3,128,128]{3,2,1,0:T(8,128)S(1)} %all_to_all.20.maps_ref), custom_call_target="tpu_custom_call" | custom-call | flops 100000000 | bytes 4000000 | tf_op jit(solution)/shard_map/pallas_call | solution.py:385
  54.7 3.5 %all-to-all-start.2 = ((f32[4,2,128,128]{3,2,1,0:T(8,128)}), f32[4,2,128,128]{3,2,1,0:T(8,128)S(1)}, u32[]{:S(2)}, u32[]{:S(2)}) async-start(f32[4,2,128,128]{3,2,1,0:T(8,128)} %shard_map.240), calls=%async_computation.2 | async-start | bytes 1048576 | tf_op jit(solution)/shard_map/all_to_all | solution.py:381
  58.3 6.8 %all-to-all-done.2.ends_ref = f32[4,2,128,128]{3,2,1,0:T(8,128)S(1)} async-done(((f32[4,2,128,128]{3,2,1,0:T(8,128)}), f32[4,2,128,128]{3,2,1,0:T(8,128)S(1)}, u32[]{:S(2)}, u32[]{:S(2)}) %all-to-all-start.2) | async-done | bytes 524320 | tf_op jit(solution)/shard_map/all_to_all | solution.py:381
  65.9 7.5 %shard_map.241 = (f32[128,512]{1,0:T(8,128)}, f32[128,512]{1,0:T(8,128)}, f32[128,512]{1,0:T(8,128)}, f32[1,4,128,128]{3,2,1,0:T(8,128)}, f32[8,128]{1,0:T(8,128)}, /*index=5*/f32[32,8,384]{2,1,0:T(8,128)}) custom-call(f32[4,2,128,128]{3,2,1,0:T(8,128)} %copy-done.9, f32[4,3,128,128]{3,2,1,0:T(8,128)} %get-tuple-element.40.maps_ref, bf16[128,512]{1,0:T(8,128)(2,1)} %q_ref.4, ...), custom_call_target="tpu_custom_call" | custom-call | flops 100000000 | bytes 4000000 | tf_op jit(solution)/shard_map/pallas_call | solution.py:385
  73.5 16.9 %all-to-all-start.3 = ((f32[32,8,384]{2,1,0:T(8,128)}), f32[32,8,384]{2,1,0:T(8,128)S(1)}, u32[]{:S(2)}, u32[]{:S(2)}) async-start(f32[32,8,384]{2,1,0:T(8,128)} %get-tuple-element.63), calls=%async_computation.3 | async-start | bytes 786432 | tf_op jit(solution)/shard_map/all_to_all | solution.py:381
  90.5 1.3 collective-permute-start.17
  91.8 1.3 collective-permute-start.18
  93.1 4.0 %collective-permute-start.19 = (bf16[4,2,128,128]{3,2,1,0:T(8,128)(2,1)S(1)}, bf16[4,2,128,128]{3,2,1,0:T(8,128)(2,1)S(1)}, u32[]{:S(2)}, u32[]{:S(2)}) collective-permute-start(bf16[4,2,128,128]{3,2,1,0:T(8,128)(2,1)S(1)} %pad_maximum_fusion.1.own_ref), channel_id=1, source_target_pairs={{32,0},{64,32},{96,64},{128,96},{160,128},{192,160},{224,192},{33,... | collective-permute-start | bytes 786440 | tf_op jit(solution)/shard_map/ppermute | solution.py:401
  97.1 4.9 %collective-permute-start.20 = (bf16[4,2,128,128]{3,2,1,0:T(8,128)(2,1)S(1)}, bf16[4,2,128,128]{3,2,1,0:T(8,128)(2,1)S(1)}, u32[]{:S(2)}, u32[]{:S(2)}) collective-permute-start(bf16[4,2,128,128]{3,2,1,0:T(8,128)(2,1)S(1)} %pad_maximum_fusion.1.own_ref), channel_id=1, source_target_pairs={{64,0},{96,32},{128,64},{160,96},{192,128},{224,160},{65,1},{97,33... | collective-permute-start | bytes 786440 | tf_op jit(solution)/shard_map/ppermute | solution.py:401
  102.0 4.0 %collective-permute-start.7 = (bf16[8,1024]{1,0:T(8,128)(2,1)S(1)}, bf16[8,1024]{1,0:T(8,128)(2,1)S(1)}, u32[]{:S(2)}, u32[]{:S(2)}) collective-permute-start(bf16[8,1024]{1,0:T(8,128)(2,1)S(1)} %copy-done.16), channel_id=1, source_target_pairs={{0,1},{1,2},{2,3},{3,4},{4,5},{5,6},{6,7},{7,0},{8,9},{9,10},{10,1... | collective-permute-start | bytes 49160 | tf_op jit(solution)/shard_map/ppermute | solution.py:405
  106.9 1.0 collective-permute-start.8
  107.9 3.4 %collective-permute-start.9 = (bf16[8,1024]{1,0:T(8,128)(2,1)S(1)}, bf16[8,1024]{1,0:T(8,128)(2,1)S(1)}, u32[]{:S(2)}, u32[]{:S(2)}) collective-permute-start(bf16[8,1024]{1,0:T(8,128)(2,1)S(1)} %copy-done.14), channel_id=1, source_target_pairs={{0,3},{1,4},{2,5},{3,6},{4,7},{5,0},{6,1},{7,2},{8,11},{9,12},{10,... | collective-permute-start | bytes 49160 | tf_op jit(solution)/shard_map/ppermute | solution.py:405
  111.3 6.5 %collective-permute-done.18.far_ref = bf16[4,2,128,128]{3,2,1,0:T(8,128)(2,1)S(1)} collective-permute-done((bf16[4,2,128,128]{3,2,1,0:T(8,128)(2,1)S(1)}, bf16[4,2,128,128]{3,2,1,0:T(8,128)(2,1)S(1)}, u32[]{:S(2)}, u32[]{:S(2)}) %collective-permute-start.18) | collective-permute-done | bytes 262176 | tf_op jit(solution)/shard_map/ppermute | solution.py:401
  117.8 2.0 %collective-permute-start.10 = (bf16[8,1024]{1,0:T(8,128)(2,1)S(1)}, bf16[8,1024]{1,0:T(8,128)(2,1)S(1)}, u32[]{:S(2)}, u32[]{:S(2)}) collective-permute-start(bf16[8,1024]{1,0:T(8,128)(2,1)S(1)} %copy-done.13), channel_id=1, source_target_pairs={{0,4},{1,5},{2,6},{3,7},{4,0},{5,1},{6,2},{7,3},{8,12},{9,13},{10,... | collective-permute-start | bytes 49160 | tf_op jit(solution)/shard_map/ppermute | solution.py:405
  119.8 2.7 %shard_map.243 = (f32[128,128]{1,0:T(8,128)}, f32[8,128]{1,0:T(8,128)S(1)}) custom-call(s32[4]{0:T(128)S(1)} %copy-done.6, bf16[128,128]{1,0:T(8,128)(2,1)S(1)} %copy-done, bf16[128,128]{1,0:T(8,128)(2,1)S(1)} %copy-done.1, bf16[4,2,128,128]{3,2,1,0:T(8,128)(2,1)S(1)} %pad_maximum_fusion.own_ref, ...), custom_call_target="tpu_custom_call" | custom-call | flops 100000000 | bytes 4000000 | tf_op jit(solution)/shard_map/pallas_call | solution.py:385
  122.5 2.4 %collective-permute-start.23 = (f32[8,128]{1,0:T(8,128)S(1)}, f32[8,128]{1,0:T(8,128)S(1)}, u32[]{:S(2)}, u32[]{:S(2)}) collective-permute-start(f32[8,128]{1,0:T(8,128)S(1)} %get-tuple-element.65), channel_id=1, source_target_pairs={{0,24},{8,0},{16,8},{24,16},{1,25},{9,1},{17,9},{25,17},{2,26},{10... | collective-permute-start | bytes 12296 | tf_op jit(solution)/shard_map/ppermute | solution.py:405
  126.2 3.6 %collective-permute-start.11 = (bf16[8,1024]{1,0:T(8,128)(2,1)S(1)}, bf16[8,1024]{1,0:T(8,128)(2,1)S(1)}, u32[]{:S(2)}, u32[]{:S(2)}) collective-permute-start(bf16[8,1024]{1,0:T(8,128)(2,1)S(1)} %copy-done.12), channel_id=1, source_target_pairs={{0,5},{1,6},{2,7},{3,0},{4,1},{5,2},{6,3},{7,4},{8,13},{9,14},{10,... | collective-permute-start | bytes 49160 | tf_op jit(solution)/shard_map/ppermute | solution.py:405
  130.6 3.0 %collective-permute-start.13 = (bf16[8,1024]{1,0:T(8,128)(2,1)S(1)}, bf16[8,1024]{1,0:T(8,128)(2,1)S(1)}, u32[]{:S(2)}, u32[]{:S(2)}) collective-permute-start(bf16[8,1024]{1,0:T(8,128)(2,1)S(1)} %copy-done.10), channel_id=1, source_target_pairs={{0,7},{1,0},{2,1},{3,2},{4,3},{5,4},{6,5},{7,6},{8,15},{9,8},{10,9... | collective-permute-start | bytes 49160 | tf_op jit(solution)/shard_map/ppermute | solution.py:405
  133.6 1.3 collective-permute-start.24
  134.9 3.7 %collective-permute-start.25 = (f32[4,8,128]{2,1,0:T(8,128)S(1)}, f32[4,8,128]{2,1,0:T(8,128)S(1)}, u32[]{:S(2)}, u32[]{:S(2)}) collective-permute-start(f32[4,8,128]{2,1,0:T(8,128)S(1)} %pad_maximum_fusion.3.own_stat), channel_id=1, source_target_pairs={{64,0},{96,32},{128,64},{160,96},{192,128},{224,160},{65,1},{97,33... | collective-permute-start | bytes 49160 | tf_op jit(solution)/shard_map/ppermute | solution.py:401
  139.2 2.5 %collective-permute-start.1 = (f32[8,128]{1,0:T(8,128)S(1)}, f32[8,128]{1,0:T(8,128)S(1)}, u32[]{:S(2)}, u32[]{:S(2)}) collective-permute-start(f32[8,128]{1,0:T(8,128)S(1)} %copy-done.8), channel_id=1, source_target_pairs={{0,2},{1,3},{2,4},{3,5},{4,6},{5,7},{6,0},{7,1},{8,10},{9,11},{10,... | collective-permute-start | bytes 12296 | tf_op jit(solution)/shard_map/ppermute | solution.py:405
  142.7 2.4 %collective-permute-start.4 = (f32[8,128]{1,0:T(8,128)S(1)}, f32[8,128]{1,0:T(8,128)S(1)}, u32[]{:S(2)}, u32[]{:S(2)}) collective-permute-start(f32[8,128]{1,0:T(8,128)S(1)} %copy-done.8), channel_id=1, source_target_pairs={{0,5},{1,6},{2,7},{3,0},{4,1},{5,2},{6,3},{7,4},{8,13},{9,14},{10,... | collective-permute-start | bytes 12296 | tf_op jit(solution)/shard_map/ppermute | solution.py:405
  145.1 1.7 %collective-permute-start.5 = (f32[8,128]{1,0:T(8,128)S(1)}, f32[8,128]{1,0:T(8,128)S(1)}, u32[]{:S(2)}, u32[]{:S(2)}) collective-permute-start(f32[8,128]{1,0:T(8,128)S(1)} %copy-done.8), channel_id=1, source_target_pairs={{0,6},{1,7},{2,0},{3,1},{4,2},{5,3},{6,4},{7,5},{8,14},{9,15},{10,... | collective-permute-start | bytes 12296 | tf_op jit(solution)/shard_map/ppermute | solution.py:405
  147.5 3.9 %shard_map.244 = (f32[128,128]{1,0:T(8,128)}, f32[128,128]{1,0:T(8,128)}) custom-call(s32[4]{0:T(128)S(1)} %copy-done.6, bf16[128,128]{1,0:T(8,128)(2,1)S(1)} %copy-done.3, bf16[128,128]{1,0:T(8,128)(2,1)S(1)} %copy-done.2, bf16[4,2,128,128]{3,2,1,0:T(8,128)(2,1)S(1)} %pad_maximum_fusion.1.own_ref, ...), custom_call_target="tpu_custom_call" | custom-call | flops 100000000 | bytes 4000000 | tf_op jit(solution)/shard_map/pallas_call | solution.py:385
  151.5 1.1 shard_map.242
  (81 shorter events, 8.2 us)
Async XLA Ops:
  27.8 23.8 %all-to-all-start.1 = ((f32[8,2,128,128]{3,2,1,0:T(8,128)}), f32[8,2,128,128]{3,2,1,0:T(8,128)S(1)}, u32[]{:S(2)}, u32[]{:S(2)}) async-start(f32[8,2,128,128]{3,2,1,0:T(8,128)} %shard_map.239), calls=%async_computation.1 | async-start | bytes 2097152 | tf_op jit(solution)/shard_map/all_to_all | solution.py:381
  33.1 25.1 %collective-permute-start.16 = (bf16[4,128,128]{2,1,0:T(8,128)(2,1)S(1)}, bf16[4,128,128]{2,1,0:T(8,128)(2,1)S(1)}, u32[]{:S(2)}, u32[]{:S(2)}) collective-permute-start(bf16[4,128,128]{2,1,0:T(8,128)(2,1)S(1)} %pad_maximum_fusion.2), channel_id=1, source_target_pairs={{0,24},{8,0},{16,8},{24,16},{1,25},{9,1},{17,9},{25,17},{2,26},{10... | collective-permute-start | bytes 393224 | tf_op jit(solution)/shard_map/ppermute | solution.py:405
  34.1 24.1 %collective-permute-start.15 = (bf16[4,128,128]{2,1,0:T(8,128)(2,1)S(1)}, bf16[4,128,128]{2,1,0:T(8,128)(2,1)S(1)}, u32[]{:S(2)}, u32[]{:S(2)}) collective-permute-start(bf16[4,128,128]{2,1,0:T(8,128)(2,1)S(1)} %pad_maximum_fusion.2), channel_id=1, source_target_pairs={{0,16},{8,24},{16,0},{24,8},{1,17},{9,25},{17,1},{25,9},{2,18},{10... | collective-permute-start | bytes 393224 | tf_op jit(solution)/shard_map/ppermute | solution.py:405
  35.3 55.1 %collective-permute-start.14 = (bf16[4,128,128]{2,1,0:T(8,128)(2,1)S(1)}, bf16[4,128,128]{2,1,0:T(8,128)(2,1)S(1)}, u32[]{:S(2)}, u32[]{:S(2)}) collective-permute-start(bf16[4,128,128]{2,1,0:T(8,128)(2,1)S(1)} %pad_maximum_fusion.2), channel_id=1, source_target_pairs={{0,8},{8,16},{16,24},{24,0},{1,9},{9,17},{17,25},{25,1},{2,10},{10... | collective-permute-start | bytes 393224 | tf_op jit(solution)/shard_map/ppermute | solution.py:405
  54.7 10.4 %all-to-all-start.2 = ((f32[4,2,128,128]{3,2,1,0:T(8,128)}), f32[4,2,128,128]{3,2,1,0:T(8,128)S(1)}, u32[]{:S(2)}, u32[]{:S(2)}) async-start(f32[4,2,128,128]{3,2,1,0:T(8,128)} %shard_map.240), calls=%async_computation.2 | async-start | bytes 1048576 | tf_op jit(solution)/shard_map/all_to_all | solution.py:381
  73.5 57.1 %copy-start.10 = (bf16[8,1024]{1,0:T(8,128)(2,1)S(1)}, bf16[8,1024]{1,0:T(8,128)(2,1)}, u32[]{:S(2)}) copy-start(bf16[8,1024]{1,0:T(8,128)(2,1)} %get-tuple-element.62) | copy-start | bytes 49156
  73.5 65.1 %copy-start.8 = (f32[8,128]{1,0:T(8,128)S(1)}, f32[8,128]{1,0:T(8,128)}, u32[]{:S(2)}) copy-start(f32[8,128]{1,0:T(8,128)} %get-tuple-element.54.refs_0_) | copy-start | bytes 12292
  73.5 78.0 %copy-start.7 = (bf16[8,1024]{1,0:T(8,128)(2,1)S(1)}, bf16[8,1024]{1,0:T(8,128)(2,1)}, u32[]{:S(2)}) copy-start(bf16[8,1024]{1,0:T(8,128)(2,1)} %get-tuple-element.55.refs_8_) | copy-start | bytes 49156
  73.5 79.1 %all-to-all-start.3 = ((f32[32,8,384]{2,1,0:T(8,128)}), f32[32,8,384]{2,1,0:T(8,128)S(1)}, u32[]{:S(2)}, u32[]{:S(2)}) async-start(f32[32,8,384]{2,1,0:T(8,128)} %get-tuple-element.63), calls=%async_computation.3 | async-start | bytes 786432 | tf_op jit(solution)/shard_map/all_to_all | solution.py:381
  90.5 17.4 %collective-permute-start.17 = (bf16[4,2,128,128]{3,2,1,0:T(8,128)(2,1)S(1)}, bf16[4,2,128,128]{3,2,1,0:T(8,128)(2,1)S(1)}, u32[]{:S(2)}, u32[]{:S(2)}) collective-permute-start(bf16[4,2,128,128]{3,2,1,0:T(8,128)(2,1)S(1)} %pad_maximum_fusion.own_ref), channel_id=1, source_target_pairs={{0,32},{32,64},{64,96},{96,128},{128,160},{160,192},{192,224},{1,3... | collective-permute-start | bytes 786440 | tf_op jit(solution)/shard_map/ppermute | solution.py:401
  91.8 26.0 %collective-permute-start.18 = (bf16[4,2,128,128]{3,2,1,0:T(8,128)(2,1)S(1)}, bf16[4,2,128,128]{3,2,1,0:T(8,128)(2,1)S(1)}, u32[]{:S(2)}, u32[]{:S(2)}) collective-permute-start(bf16[4,2,128,128]{3,2,1,0:T(8,128)(2,1)S(1)} %pad_maximum_fusion.own_ref), channel_id=1, source_target_pairs={{0,64},{32,96},{64,128},{96,160},{128,192},{160,224},{1,65},{33,97... | collective-permute-start | bytes 786440 | tf_op jit(solution)/shard_map/ppermute | solution.py:401
  93.1 46.1 %collective-permute-start.19 = (bf16[4,2,128,128]{3,2,1,0:T(8,128)(2,1)S(1)}, bf16[4,2,128,128]{3,2,1,0:T(8,128)(2,1)S(1)}, u32[]{:S(2)}, u32[]{:S(2)}) collective-permute-start(bf16[4,2,128,128]{3,2,1,0:T(8,128)(2,1)S(1)} %pad_maximum_fusion.1.own_ref), channel_id=1, source_target_pairs={{32,0},{64,32},{96,64},{128,96},{160,128},{192,160},{224,192},{33,... | collective-permute-start | bytes 786440 | tf_op jit(solution)/shard_map/ppermute | solution.py:401
  97.1 44.6 %collective-permute-start.20 = (bf16[4,2,128,128]{3,2,1,0:T(8,128)(2,1)S(1)}, bf16[4,2,128,128]{3,2,1,0:T(8,128)(2,1)S(1)}, u32[]{:S(2)}, u32[]{:S(2)}) collective-permute-start(bf16[4,2,128,128]{3,2,1,0:T(8,128)(2,1)S(1)} %pad_maximum_fusion.1.own_ref), channel_id=1, source_target_pairs={{64,0},{96,32},{128,64},{160,96},{192,128},{224,160},{65,1},{97,33... | collective-permute-start | bytes 786440 | tf_op jit(solution)/shard_map/ppermute | solution.py:401
  102.0 4.8 %collective-permute-start.7 = (bf16[8,1024]{1,0:T(8,128)(2,1)S(1)}, bf16[8,1024]{1,0:T(8,128)(2,1)S(1)}, u32[]{:S(2)}, u32[]{:S(2)}) collective-permute-start(bf16[8,1024]{1,0:T(8,128)(2,1)S(1)} %copy-done.16), channel_id=1, source_target_pairs={{0,1},{1,2},{2,3},{3,4},{4,5},{5,6},{6,7},{7,0},{8,9},{9,10},{10,1... | collective-permute-start | bytes 49160 | tf_op jit(solution)/shard_map/ppermute | solution.py:405
  106.9 15.7 %collective-permute-start.8 = (bf16[8,1024]{1,0:T(8,128)(2,1)S(1)}, bf16[8,1024]{1,0:T(8,128)(2,1)S(1)}, u32[]{:S(2)}, u32[]{:S(2)}) collective-permute-start(bf16[8,1024]{1,0:T(8,128)(2,1)S(1)} %copy-done.15), channel_id=1, source_target_pairs={{0,2},{1,3},{2,4},{3,5},{4,6},{5,7},{6,0},{7,1},{8,10},{9,11},{10,... | collective-permute-start | bytes 49160 | tf_op jit(solution)/shard_map/ppermute | solution.py:405
  107.9 17.1 %collective-permute-start.9 = (bf16[8,1024]{1,0:T(8,128)(2,1)S(1)}, bf16[8,1024]{1,0:T(8,128)(2,1)S(1)}, u32[]{:S(2)}, u32[]{:S(2)}) collective-permute-start(bf16[8,1024]{1,0:T(8,128)(2,1)S(1)} %copy-done.14), channel_id=1, source_target_pairs={{0,3},{1,4},{2,5},{3,6},{4,7},{5,0},{6,1},{7,2},{8,11},{9,12},{10,... | collective-permute-start | bytes 49160 | tf_op jit(solution)/shard_map/ppermute | solution.py:405
  117.8 7.7 %collective-permute-start.10 = (bf16[8,1024]{1,0:T(8,128)(2,1)S(1)}, bf16[8,1024]{1,0:T(8,128)(2,1)S(1)}, u32[]{:S(2)}, u32[]{:S(2)}) collective-permute-start(bf16[8,1024]{1,0:T(8,128)(2,1)S(1)} %copy-done.13), channel_id=1, source_target_pairs={{0,4},{1,5},{2,6},{3,7},{4,0},{5,1},{6,2},{7,3},{8,12},{9,13},{10,... | collective-permute-start | bytes 49160 | tf_op jit(solution)/shard_map/ppermute | solution.py:405
  122.5 3.7 %collective-permute-start.23 = (f32[8,128]{1,0:T(8,128)S(1)}, f32[8,128]{1,0:T(8,128)S(1)}, u32[]{:S(2)}, u32[]{:S(2)}) collective-permute-start(f32[8,128]{1,0:T(8,128)S(1)} %get-tuple-element.65), channel_id=1, source_target_pairs={{0,24},{8,0},{16,8},{24,16},{1,25},{9,1},{17,9},{25,17},{2,26},{10... | collective-permute-start | bytes 12296 | tf_op jit(solution)/shard_map/ppermute | solution.py:405
  125.0 4.9 %collective-permute-start.22 = (f32[8,128]{1,0:T(8,128)S(1)}, f32[8,128]{1,0:T(8,128)S(1)}, u32[]{:S(2)}, u32[]{:S(2)}) collective-permute-start(f32[8,128]{1,0:T(8,128)S(1)} %get-tuple-element.65), channel_id=1, source_target_pairs={{0,16},{8,24},{16,0},{24,8},{1,17},{9,25},{17,1},{25,9},{2,18},{10... | collective-permute-start | bytes 12296 | tf_op jit(solution)/shard_map/ppermute | solution.py:405
  125.5 5.1 %collective-permute-start.21 = (f32[8,128]{1,0:T(8,128)S(1)}, f32[8,128]{1,0:T(8,128)S(1)}, u32[]{:S(2)}, u32[]{:S(2)}) collective-permute-start(f32[8,128]{1,0:T(8,128)S(1)} %get-tuple-element.65), channel_id=1, source_target_pairs={{0,8},{8,16},{16,24},{24,0},{1,9},{9,17},{17,25},{25,1},{2,10},{10... | collective-permute-start | bytes 12296 | tf_op jit(solution)/shard_map/ppermute | solution.py:405
  126.2 7.4 %collective-permute-start.11 = (bf16[8,1024]{1,0:T(8,128)(2,1)S(1)}, bf16[8,1024]{1,0:T(8,128)(2,1)S(1)}, u32[]{:S(2)}, u32[]{:S(2)}) collective-permute-start(bf16[8,1024]{1,0:T(8,128)(2,1)S(1)} %copy-done.12), channel_id=1, source_target_pairs={{0,5},{1,6},{2,7},{3,0},{4,1},{5,2},{6,3},{7,4},{8,13},{9,14},{10,... | collective-permute-start | bytes 49160 | tf_op jit(solution)/shard_map/ppermute | solution.py:405
  129.8 5.1 %collective-permute-start.12 = (bf16[8,1024]{1,0:T(8,128)(2,1)S(1)}, bf16[8,1024]{1,0:T(8,128)(2,1)S(1)}, u32[]{:S(2)}, u32[]{:S(2)}) collective-permute-start(bf16[8,1024]{1,0:T(8,128)(2,1)S(1)} %copy-done.11), channel_id=1, source_target_pairs={{0,6},{1,7},{2,0},{3,1},{4,2},{5,3},{6,4},{7,5},{8,14},{9,15},{10,... | collective-permute-start | bytes 49160 | tf_op jit(solution)/shard_map/ppermute | solution.py:405
  130.6 8.0 %collective-permute-start.13 = (bf16[8,1024]{1,0:T(8,128)(2,1)S(1)}, bf16[8,1024]{1,0:T(8,128)(2,1)S(1)}, u32[]{:S(2)}, u32[]{:S(2)}) collective-permute-start(bf16[8,1024]{1,0:T(8,128)(2,1)S(1)} %copy-done.10), channel_id=1, source_target_pairs={{0,7},{1,0},{2,1},{3,2},{4,3},{5,4},{6,5},{7,6},{8,15},{9,8},{10,9... | collective-permute-start | bytes 49160 | tf_op jit(solution)/shard_map/ppermute | solution.py:405
  133.6 8.9 %collective-permute-start.24 = (f32[4,8,128]{2,1,0:T(8,128)S(1)}, f32[4,8,128]{2,1,0:T(8,128)S(1)}, u32[]{:S(2)}, u32[]{:S(2)}) collective-permute-start(f32[4,8,128]{2,1,0:T(8,128)S(1)} %pad_maximum_fusion.3.own_stat), channel_id=1, source_target_pairs={{32,0},{64,32},{96,64},{128,96},{160,128},{192,160},{224,192},{33,... | collective-permute-start | bytes 49160 | tf_op jit(solution)/shard_map/ppermute | solution.py:401
  134.9 7.8 %collective-permute-start.25 = (f32[4,8,128]{2,1,0:T(8,128)S(1)}, f32[4,8,128]{2,1,0:T(8,128)S(1)}, u32[]{:S(2)}, u32[]{:S(2)}) collective-permute-start(f32[4,8,128]{2,1,0:T(8,128)S(1)} %pad_maximum_fusion.3.own_stat), channel_id=1, source_target_pairs={{64,0},{96,32},{128,64},{160,96},{192,128},{224,160},{65,1},{97,33... | collective-permute-start | bytes 49160 | tf_op jit(solution)/shard_map/ppermute | solution.py:401
  138.6 6.5 %collective-permute-start = (f32[8,128]{1,0:T(8,128)S(1)}, f32[8,128]{1,0:T(8,128)S(1)}, u32[]{:S(2)}, u32[]{:S(2)}) collective-permute-start(f32[8,128]{1,0:T(8,128)S(1)} %copy-done.8), channel_id=1, source_target_pairs={{0,1},{1,2},{2,3},{3,4},{4,5},{5,6},{6,7},{7,0},{8,9},{9,10},{10,1... | collective-permute-start | bytes 12296 | tf_op jit(solution)/shard_map/ppermute | solution.py:405
  139.2 7.6 %collective-permute-start.1 = (f32[8,128]{1,0:T(8,128)S(1)}, f32[8,128]{1,0:T(8,128)S(1)}, u32[]{:S(2)}, u32[]{:S(2)}) collective-permute-start(f32[8,128]{1,0:T(8,128)S(1)} %copy-done.8), channel_id=1, source_target_pairs={{0,2},{1,3},{2,4},{3,5},{4,6},{5,7},{6,0},{7,1},{8,10},{9,11},{10,... | collective-permute-start | bytes 12296 | tf_op jit(solution)/shard_map/ppermute | solution.py:405
  141.7 9.7 %collective-permute-start.2 = (f32[8,128]{1,0:T(8,128)S(1)}, f32[8,128]{1,0:T(8,128)S(1)}, u32[]{:S(2)}, u32[]{:S(2)}) collective-permute-start(f32[8,128]{1,0:T(8,128)S(1)} %copy-done.8), channel_id=1, source_target_pairs={{0,3},{1,4},{2,5},{3,6},{4,7},{5,0},{6,1},{7,2},{8,11},{9,12},{10,... | collective-permute-start | bytes 12296 | tf_op jit(solution)/shard_map/ppermute | solution.py:405
  142.5 8.9 %collective-permute-start.3 = (f32[8,128]{1,0:T(8,128)S(1)}, f32[8,128]{1,0:T(8,128)S(1)}, u32[]{:S(2)}, u32[]{:S(2)}) collective-permute-start(f32[8,128]{1,0:T(8,128)S(1)} %copy-done.8), channel_id=1, source_target_pairs={{0,4},{1,5},{2,6},{3,7},{4,0},{5,1},{6,2},{7,3},{8,12},{9,13},{10,... | collective-permute-start | bytes 12296 | tf_op jit(solution)/shard_map/ppermute | solution.py:405
  142.7 8.7 %collective-permute-start.4 = (f32[8,128]{1,0:T(8,128)S(1)}, f32[8,128]{1,0:T(8,128)S(1)}, u32[]{:S(2)}, u32[]{:S(2)}) collective-permute-start(f32[8,128]{1,0:T(8,128)S(1)} %copy-done.8), channel_id=1, source_target_pairs={{0,5},{1,6},{2,7},{3,0},{4,1},{5,2},{6,3},{7,4},{8,13},{9,14},{10,... | collective-permute-start | bytes 12296 | tf_op jit(solution)/shard_map/ppermute | solution.py:405
  145.1 6.3 %collective-permute-start.5 = (f32[8,128]{1,0:T(8,128)S(1)}, f32[8,128]{1,0:T(8,128)S(1)}, u32[]{:S(2)}, u32[]{:S(2)}) collective-permute-start(f32[8,128]{1,0:T(8,128)S(1)} %copy-done.8), channel_id=1, source_target_pairs={{0,6},{1,7},{2,0},{3,1},{4,2},{5,3},{6,4},{7,5},{8,14},{9,15},{10,... | collective-permute-start | bytes 12296 | tf_op jit(solution)/shard_map/ppermute | solution.py:405
  146.8 4.6 %collective-permute-start.6 = (f32[8,128]{1,0:T(8,128)S(1)}, f32[8,128]{1,0:T(8,128)S(1)}, u32[]{:S(2)}, u32[]{:S(2)}) collective-permute-start(f32[8,128]{1,0:T(8,128)S(1)} %copy-done.8), channel_id=1, source_target_pairs={{0,7},{1,0},{2,1},{3,2},{4,3},{5,4},{6,5},{7,6},{8,15},{9,8},{10,9... | collective-permute-start | bytes 12296 | tf_op jit(solution)/shard_map/ppermute | solution.py:405
  (14 other events, 356.6 us)

commit v4 on v3

--- a/solution.py
+++ b/solution.py
@@ -58,7 +58,7 @@
 
 
 def prepare_kernel(
-    at_ref, x_hbm, wb_ref, wd_ref, rate_ref, bias_ref, q_ref, k_ref, v_ref, g_ref,
+    x_hbm, wb_ref, wd_ref, rate_ref, bias_ref, q_ref, k_ref, v_ref, g_ref,
     maps_ref, inv_ref, ratio_ref, rk_ref, p_ref, w_out_ref, y_ref, du_ref, rows_ref, cols_ref,
     *rest,
 ):
@@ -72,7 +72,7 @@
     count = len(chunk_refs)
     size = w_ref.shape[1] // count
     for d, chunk_ref in enumerate(chunk_refs):
-        to = at_ref[2] + d
+        to = lax.axis_index("head") + d
         to = jnp.where(to >= count, to - count, to)
         chunk_ref[...] = w_ref[:, pl.ds(pl.multiple_of(to * size, size), size)]
     row, lane = ids((T, T))
@@ -157,8 +157,8 @@
         maps_ref[h, 2] = own - mm(split(y), split(du), TN)
 
 
-def group_kernel(at_ref, maps_ref, out_ref):
-    z = at_ref[0]
+def group_kernel(maps_ref, out_ref):
+    z = lax.axis_index("seq_0")
     phi = [split(maps_ref[x, 0]) for x in range(4)]
     off = [maps_ref[x, 1] for x in range(4)]
     loc = [maps_ref[x, 2] for x in range(4)]
@@ -176,8 +176,8 @@
         out_ref[to, 1] = jnp.where(to > z, later, earlier)
 
 
-def spread_kernel(at_ref, start_ref, end_ref, groups_ref, maps_ref, out_ref):
-    z, x = at_ref[0], at_ref[1]
+def spread_kernel(start_ref, end_ref, groups_ref, maps_ref, out_ref):
+    z, x = lax.axis_index("seq_0"), lax.axis_index("seq_1")
     count = groups_ref.shape[0]
     state, grad = start_ref[x], end_ref[x]
     for step in range(count - 1):
@@ -288,9 +288,9 @@
         term_ref[s, :, width:] = param
 
 
-def window_kernel(at_ref, q_ref, g_ref, own_ref, near_ref, far_ref, dq_ref, stat_ref):
+def window_kernel(q_ref, g_ref, own_ref, near_ref, far_ref, dq_ref, stat_ref):
     kv_refs = (own_ref, near_ref, far_ref)
-    z, x = at_ref[0], at_ref[1]
+    z, x = lax.axis_index("seq_0"), lax.axis_index("seq_1")
     row, lane = ids((T, T))
     gap = row - lane
     scale = 1.0 / math.sqrt(T)
@@ -327,10 +327,11 @@
 
 
 def key_kernel(
-    at_ref, k_ref, v_ref, own_ref, near_ref, far_ref, own_stat, near_stat, far_stat, dk_ref, dv_ref
+    k_ref, v_ref, own_ref, near_ref, far_ref, own_stat, near_stat, far_stat, dk_ref, dv_ref
 ):
     qg_refs, stat_refs = (own_ref, near_ref, far_ref), (own_stat, near_stat, far_stat)
-    z, x, count = at_ref[0], at_ref[1], at_ref[3]
+    z, x = lax.axis_index("seq_0"), lax.axis_index("seq_1")
+    count = lax.axis_size("seq_0")
     row, lane = ids((T, T))
     gap = lane - row
     scale = 1.0 / math.sqrt(T)
@@ -415,9 +416,6 @@
     heads = beta_weight.shape[0]
     width = layer_input.shape[1]
     pieces = z_count * x_count
-    at = jnp.stack(
-        [lax.axis_index("seq_0"), lax.axis_index("seq_1"), lax.axis_index("head"), z_count]
-    ).astype(jnp.int32)
     others = range(1, x_count)
 
     mine = jnp.stack([attn_key, attn_value, attn_query, attn_out_grad])
@@ -428,8 +426,8 @@
         prepare_kernel,
         (f32(heads, 3, T, T),) + (f32(heads, T, T),) * 7 + (f32(6 * heads, T), f32(T, T))
         + (bf16_chunk,) * head_count,
-        [SM, ANY, VM, VM, SM, SM, VM, VM, VM, VM],
-        at, layer_input, beta_weight, decay_weight, log_rate, decay_bias, delta_query, delta_key,
+        [ANY, VM, VM, SM, SM, VM, VM, VM, VM],
+        layer_input, beta_weight, decay_weight, log_rate, decay_bias, delta_query, delta_key,
         delta_value, delta_out_grad,
         scratch=[
             pltpu.VMEM((2 * heads, width), BF16), pltpu.VMEM((T, width), BF16),
@@ -441,30 +439,30 @@
     kv, qg = jnp.stack([a[:2] for a in line]), jnp.stack([a[2:] for a in line])
     kv_all = [kv] + [up_by(kv, d, z_count) for d in (1, 2)]
     qg_all = [qg] + [up_by(qg, -d, z_count) for d in (1, 2)]
-    groups = call(group_kernel, f32(z_count, 2, T, T), [SM, VM], at, blocks)
+    groups = call(group_kernel, f32(z_count, 2, T, T), [VM], blocks)
 
     groups = exchange(groups, "seq_0")
     dq_attn, stat = call(
         window_kernel,
         (f32(T, T), f32(8, T)),
-        [SM] + [VM] * 5,
-        at, attn_query, attn_out_grad, *kv_all,
+        [VM] * 5,
+        attn_query, attn_out_grad, *kv_all,
     )
     stat = jnp.stack([stat] + [turn(stat, "seq_1", d, x_count) for d in others])
     stat_all = [stat] + [up_by(stat, -d, z_count) for d in (1, 2)]
     dk_attn, dv_attn = call(
         key_kernel,
         (f32(T, T), f32(T, T)),
-        [SM] + [VM] * 8,
-        at, attn_key, attn_value, *qg_all, *stat_all,
+        [VM] * 8,
+        attn_key, attn_value, *qg_all, *stat_all,
     )
     chunks = [chunks[0]] + [turn(chunks[d], "head", d, head_count) for d in range(1, head_count)]
 
     ends = call(
         spread_kernel,
         f32(x_count, 2, T, T),
-        [SM] + [VM] * 4,
-        at, state_init, state_grad_next, groups, blocks,
+        [VM] * 4,
+        state_init, state_grad_next, groups, blocks,
     )
     ends = exchange(ends, "seq_1")
 

time: 154 us -> 152 us (0.987)
  Pallas kernels: 29.4 us -> 27.3 us
    pallas_call x7, Pallas kernels: 29.4 us -> 27.3 us  [run(): pl.pallas_call(kernel, out_shape=outs, in_specs=specs, out_specs=jax.tree...]
  transfers between devices with their start and end apart: 29 -> 29, of which waited for: 4 -> 4; matrix products, arithmetic and copies ran while one was open for 0% -> 0% of each run, Pallas kernels for 12% -> 11%
where the time goes in v4:
time: 152 us; the launch traced here: 151 us
  starting transfers between devices  74.6 us (49%)
  waiting for transfers between devices  30.5 us (20%)
  Pallas kernels  27.3 us (18%)
  blocking collectives  15.5 us (10%)
  local copies, waits for them, and re-layouts  2.16 us (1%)
    ppermute x20, starting transfers between devices, turn(): lax.ppermute(value, axis, [(i, (i + by) % count) for i in range(count)])  32.5 us
    pallas_call x7, Pallas kernels, run(): pl.pallas_call(kernel, out_shape=outs, in_specs=specs, out_specs=jax.tree...  27.3 us
    all_to_all x3, starting transfers between devices, exchange(): return lax.all_to_all(value, axis, split_axis=0, concat_axis=0, tiled=True)  25.6 us
    all_to_all x3, waiting for transfers between devices, exchange(): return lax.all_to_all(value, axis, split_axis=0, concat_axis=0, tiled=True)  23.1 us
    ppermute x6, starting transfers between devices, up_by(): return lax.ppermute(value, 'seq_0', pairs)  16.4 us
    all_to_all x1, blocking collectives, exchange(): return lax.all_to_all(value, axis, split_axis=0, concat_axis=0, tiled=True)  15.5 us
    ppermute x6, waiting for transfers between devices, up_by(): return lax.ppermute(value, 'seq_0', pairs)  6.46 us
  transfers between devices with their start and end apart: 29, of which 4 were waited for; matrix products, arithmetic and copies ran while one was open for 0% of the time, Pallas kernels for 11%

profile of v4, /device:TPU:233, one launch (start us, length us, event | category | flops | bytes accessed | tf_op | source)
XLA Modules:
  0.0 151.2 jit_solution(2115884471733383531)
XLA Ops:
  0.6 9.0 %shard_map.238 = (f32[4,3,128,128]{3,2,1,0:T(8,128)}, f32[4,128,128]{2,1,0:T(8,128)}, f32[4,128,128]{2,1,0:T(8,128)}, f32[4,128,128]{2,1,0:T(8,128)}, f32[4,128,...) custom-call(bf16[128,8192]{1,0:T(8,128)(2,1)} %x_hbm.3, ...), custom_call_target="tpu_custom_call" | custom-call | flops 100000000 | bytes 4000000 | tf_op jit(solution)/shard_map/pallas_call | solution.py:386
  9.7 15.5 %all_to_all.20.maps_ref = f32[4,3,128,128]{3,2,1,0:T(8,128)S(1)} all-to-all(f32[4,3,128,128]{3,2,1,0:T(8,128)} %get-tuple-element.40.maps_ref), channel_id=1, replica_groups=mesh['seq_0'=8,'seq_1'=4,'head'=8] {'seq_1'}, dimensions={0} | all-to-all | bytes 1572864 | tf_op jit(solution)/shard_map/all_to_all | solution.py:382
  25.2 1.5 %shard_map.239 = f32[8,2,128,128]{3,2,1,0:T(8,128)} custom-call(f32[4,3,128,128]{3,2,1,0:T(8,128)S(1)} %all_to_all.20.maps_ref), custom_call_target="tpu_custom_call" | custom-call | flops 100000000 | bytes 4000000 | tf_op jit(solution)/shard_map/pallas_call | solution.py:386
  26.7 5.3 %all-to-all-start.1 = ((f32[8,2,128,128]{3,2,1,0:T(8,128)}), f32[8,2,128,128]{3,2,1,0:T(8,128)S(1)}, u32[]{:S(2)}, u32[]{:S(2)}) async-start(f32[8,2,128,128]{3,2,1,0:T(8,128)} %shard_map.239), calls=%async_computation.1 | async-start | bytes 2097152 | tf_op jit(solution)/shard_map/all_to_all | solution.py:382
  32.0 1.0 collective-permute-start.16
  33.0 1.2 collective-permute-start.15
  34.2 16.3 %all-to-all-done.1.groups_ref = f32[8,2,128,128]{3,2,1,0:T(8,128)S(1)} async-done(((f32[8,2,128,128]{3,2,1,0:T(8,128)}), f32[8,2,128,128]{3,2,1,0:T(8,128)S(1)}, u32[]{:S(2)}, u32[]{:S(2)}) %all-to-all-start.1) | async-done | bytes 1048608 | tf_op jit(solution)/shard_map/all_to_all | solution.py:382
  50.5 2.7 %shard_map.240 = f32[4,2,128,128]{3,2,1,0:T(8,128)} custom-call(f32[4,128,128]{2,1,0:T(8,128)S(1)} %copy-done.4, f32[4,128,128]{2,1,0:T(8,128)S(1)} %copy-done.5, f32[8,2,128,128]{3,2,1,0:T(8,128)S(1)} %all-to-all-done.1.groups_ref, f32[4,3,128,128]{3,2,1,0:T(8,128)S(1)} %all_to_all.20.maps_ref), custom_call_target="tpu_custom_call" | custom-call | flops 100000000 | bytes 4000000 | tf_op jit(solution)/shard_map/pallas_call | solution.py:386
  53.1 3.5 %all-to-all-start.2 = ((f32[4,2,128,128]{3,2,1,0:T(8,128)}), f32[4,2,128,128]{3,2,1,0:T(8,128)S(1)}, u32[]{:S(2)}, u32[]{:S(2)}) async-start(f32[4,2,128,128]{3,2,1,0:T(8,128)} %shard_map.240), calls=%async_computation.2 | async-start | bytes 1048576 | tf_op jit(solution)/shard_map/all_to_all | solution.py:382
  56.7 6.8 %all-to-all-done.2.ends_ref = f32[4,2,128,128]{3,2,1,0:T(8,128)S(1)} async-done(((f32[4,2,128,128]{3,2,1,0:T(8,128)}), f32[4,2,128,128]{3,2,1,0:T(8,128)S(1)}, u32[]{:S(2)}, u32[]{:S(2)}) %all-to-all-start.2) | async-done | bytes 524320 | tf_op jit(solution)/shard_map/all_to_all | solution.py:382
  64.3 7.5 %shard_map.241 = (f32[128,512]{1,0:T(8,128)}, f32[128,512]{1,0:T(8,128)}, f32[128,512]{1,0:T(8,128)}, f32[1,4,128,128]{3,2,1,0:T(8,128)}, f32[8,128]{1,0:T(8,128)}, /*index=5*/f32[32,8,384]{2,1,0:T(8,128)}) custom-call(f32[4,2,128,128]{3,2,1,0:T(8,128)} %copy-done.8, f32[4,3,128,128]{3,2,1,0:T(8,128)} %get-tuple-element.40.maps_ref, bf16[128,512]{1,0:T(8,128)(2,1)} %q_ref.4, ...), custom_call_target="tpu_custom_call" | custom-call | flops 100000000 | bytes 4000000 | tf_op jit(solution)/shard_map/pallas_call | solution.py:386
  71.9 16.9 %all-to-all-start.3 = ((f32[32,8,384]{2,1,0:T(8,128)}), f32[32,8,384]{2,1,0:T(8,128)S(1)}, u32[]{:S(2)}, u32[]{:S(2)}) async-start(f32[32,8,384]{2,1,0:T(8,128)} %get-tuple-element.63), calls=%async_computation.3 | async-start | bytes 786432 | tf_op jit(solution)/shard_map/all_to_all | solution.py:382
  88.8 1.3 collective-permute-start.17
  90.1 1.3 collective-permute-start.18
  91.5 4.0 %collective-permute-start.19 = (bf16[4,2,128,128]{3,2,1,0:T(8,128)(2,1)S(1)}, bf16[4,2,128,128]{3,2,1,0:T(8,128)(2,1)S(1)}, u32[]{:S(2)}, u32[]{:S(2)}) collective-permute-start(bf16[4,2,128,128]{3,2,1,0:T(8,128)(2,1)S(1)} %pad_maximum_fusion.1.own_ref), channel_id=1, source_target_pairs={{32,0},{64,32},{96,64},{128,96},{160,128},{192,160},{224,192},{33,... | collective-permute-start | bytes 786440 | tf_op jit(solution)/shard_map/ppermute | solution.py:402
  95.5 4.9 %collective-permute-start.20 = (bf16[4,2,128,128]{3,2,1,0:T(8,128)(2,1)S(1)}, bf16[4,2,128,128]{3,2,1,0:T(8,128)(2,1)S(1)}, u32[]{:S(2)}, u32[]{:S(2)}) collective-permute-start(bf16[4,2,128,128]{3,2,1,0:T(8,128)(2,1)S(1)} %pad_maximum_fusion.1.own_ref), channel_id=1, source_target_pairs={{64,0},{96,32},{128,64},{160,96},{192,128},{224,160},{65,1},{97,33... | collective-permute-start | bytes 786440 | tf_op jit(solution)/shard_map/ppermute | solution.py:402
  100.4 4.0 %collective-permute-start.7 = (bf16[8,1024]{1,0:T(8,128)(2,1)S(1)}, bf16[8,1024]{1,0:T(8,128)(2,1)S(1)}, u32[]{:S(2)}, u32[]{:S(2)}) collective-permute-start(bf16[8,1024]{1,0:T(8,128)(2,1)S(1)} %copy-done.15), channel_id=1, source_target_pairs={{0,1},{1,2},{2,3},{3,4},{4,5},{5,6},{6,7},{7,0},{8,9},{9,10},{10,1... | collective-permute-start | bytes 49160 | tf_op jit(solution)/shard_map/ppermute | solution.py:406
  105.2 1.0 collective-permute-start.8
  106.2 3.5 %collective-permute-start.9 = (bf16[8,1024]{1,0:T(8,128)(2,1)S(1)}, bf16[8,1024]{1,0:T(8,128)(2,1)S(1)}, u32[]{:S(2)}, u32[]{:S(2)}) collective-permute-start(bf16[8,1024]{1,0:T(8,128)(2,1)S(1)} %copy-done.13), channel_id=1, source_target_pairs={{0,3},{1,4},{2,5},{3,6},{4,7},{5,0},{6,1},{7,2},{8,11},{9,12},{10,... | collective-permute-start | bytes 49160 | tf_op jit(solution)/shard_map/ppermute | solution.py:406
  109.7 6.4 %collective-permute-done.18.far_ref = bf16[4,2,128,128]{3,2,1,0:T(8,128)(2,1)S(1)} collective-permute-done((bf16[4,2,128,128]{3,2,1,0:T(8,128)(2,1)S(1)}, bf16[4,2,128,128]{3,2,1,0:T(8,128)(2,1)S(1)}, u32[]{:S(2)}, u32[]{:S(2)}) %collective-permute-start.18) | collective-permute-done | bytes 262176 | tf_op jit(solution)/shard_map/ppermute | solution.py:402
  116.2 2.0 %collective-permute-start.10 = (bf16[8,1024]{1,0:T(8,128)(2,1)S(1)}, bf16[8,1024]{1,0:T(8,128)(2,1)S(1)}, u32[]{:S(2)}, u32[]{:S(2)}) collective-permute-start(bf16[8,1024]{1,0:T(8,128)(2,1)S(1)} %copy-done.12), channel_id=1, source_target_pairs={{0,4},{1,5},{2,6},{3,7},{4,0},{5,1},{6,2},{7,3},{8,12},{9,13},{10,... | collective-permute-start | bytes 49160 | tf_op jit(solution)/shard_map/ppermute | solution.py:406
  118.2 2.2 %shard_map.243 = (f32[128,128]{1,0:T(8,128)}, f32[8,128]{1,0:T(8,128)S(1)}) custom-call(bf16[128,128]{1,0:T(8,128)(2,1)S(1)} %copy-done.2, bf16[128,128]{1,0:T(8,128)(2,1)S(1)} %copy-done.3, bf16[4,2,128,128]{3,2,1,0:T(8,128)(2,1)S(1)} %pad_maximum_fusion.own_ref, bf16[4,2,128,128]{3,2,1,0:T(8,128)(2,1)S(1)} %collective-permute-done.17.near_ref, ...), custom_call_target="tpu_custom_call" | custom-call | flops 100000000 | bytes 4000000 | tf_op jit(solution)/shard_map/pallas_call | solution.py:386
  120.4 2.4 %collective-permute-start.23 = (f32[8,128]{1,0:T(8,128)S(1)}, f32[8,128]{1,0:T(8,128)S(1)}, u32[]{:S(2)}, u32[]{:S(2)}) collective-permute-start(f32[8,128]{1,0:T(8,128)S(1)} %get-tuple-element.65), channel_id=1, source_target_pairs={{0,24},{8,0},{16,8},{24,16},{1,25},{9,1},{17,9},{25,17},{2,26},{10... | collective-permute-start | bytes 12296 | tf_op jit(solution)/shard_map/ppermute | solution.py:406
  124.1 3.6 %collective-permute-start.11 = (bf16[8,1024]{1,0:T(8,128)(2,1)S(1)}, bf16[8,1024]{1,0:T(8,128)(2,1)S(1)}, u32[]{:S(2)}, u32[]{:S(2)}) collective-permute-start(bf16[8,1024]{1,0:T(8,128)(2,1)S(1)} %copy-done.11), channel_id=1, source_target_pairs={{0,5},{1,6},{2,7},{3,0},{4,1},{5,2},{6,3},{7,4},{8,13},{9,14},{10,... | collective-permute-start | bytes 49160 | tf_op jit(solution)/shard_map/ppermute | solution.py:406
  128.4 3.0 %collective-permute-start.13 = (bf16[8,1024]{1,0:T(8,128)(2,1)S(1)}, bf16[8,1024]{1,0:T(8,128)(2,1)S(1)}, u32[]{:S(2)}, u32[]{:S(2)}) collective-permute-start(bf16[8,1024]{1,0:T(8,128)(2,1)S(1)} %copy-done.9), channel_id=1, source_target_pairs={{0,7},{1,0},{2,1},{3,2},{4,3},{5,4},{6,5},{7,6},{8,15},{9,8},{10,9... | collective-permute-start | bytes 49160 | tf_op jit(solution)/shard_map/ppermute | solution.py:406
  131.5 1.3 collective-permute-start.24
  132.8 3.7 %collective-permute-start.25 = (f32[4,8,128]{2,1,0:T(8,128)S(1)}, f32[4,8,128]{2,1,0:T(8,128)S(1)}, u32[]{:S(2)}, u32[]{:S(2)}) collective-permute-start(f32[4,8,128]{2,1,0:T(8,128)S(1)} %pad_maximum_fusion.3.own_stat), channel_id=1, source_target_pairs={{64,0},{96,32},{128,64},{160,96},{192,128},{224,160},{65,1},{97,33... | collective-permute-start | bytes 49160 | tf_op jit(solution)/shard_map/ppermute | solution.py:402
  137.1 2.5 %collective-permute-start.1 = (f32[8,128]{1,0:T(8,128)S(1)}, f32[8,128]{1,0:T(8,128)S(1)}, u32[]{:S(2)}, u32[]{:S(2)}) collective-permute-start(f32[8,128]{1,0:T(8,128)S(1)} %copy-done.7), channel_id=1, source_target_pairs={{0,2},{1,3},{2,4},{3,5},{4,6},{5,7},{6,0},{7,1},{8,10},{9,11},{10,... | collective-permute-start | bytes 12296 | tf_op jit(solution)/shard_map/ppermute | solution.py:406
  140.5 2.4 %collective-permute-start.4 = (f32[8,128]{1,0:T(8,128)S(1)}, f32[8,128]{1,0:T(8,128)S(1)}, u32[]{:S(2)}, u32[]{:S(2)}) collective-permute-start(f32[8,128]{1,0:T(8,128)S(1)} %copy-done.7), channel_id=1, source_target_pairs={{0,5},{1,6},{2,7},{3,0},{4,1},{5,2},{6,3},{7,4},{8,13},{9,14},{10,... | collective-permute-start | bytes 12296 | tf_op jit(solution)/shard_map/ppermute | solution.py:406
  143.0 1.7 %collective-permute-start.5 = (f32[8,128]{1,0:T(8,128)S(1)}, f32[8,128]{1,0:T(8,128)S(1)}, u32[]{:S(2)}, u32[]{:S(2)}) collective-permute-start(f32[8,128]{1,0:T(8,128)S(1)} %copy-done.7), channel_id=1, source_target_pairs={{0,6},{1,7},{2,0},{3,1},{4,2},{5,3},{6,4},{7,5},{8,14},{9,15},{10,... | collective-permute-start | bytes 12296 | tf_op jit(solution)/shard_map/ppermute | solution.py:406
  145.4 3.3 %shard_map.244 = (f32[128,128]{1,0:T(8,128)}, f32[128,128]{1,0:T(8,128)}) custom-call(bf16[128,128]{1,0:T(8,128)(2,1)S(1)} %copy-done.1, bf16[128,128]{1,0:T(8,128)(2,1)S(1)} %copy-done, bf16[4,2,128,128]{3,2,1,0:T(8,128)(2,1)S(1)} %pad_maximum_fusion.1.own_ref, bf16[4,2,128,128]{3,2,1,0:T(8,128)(2,1)S(1)} %collective-permute-done.19.near_ref, ...), custom_call_target="tpu_custom_call" | custom-call | flops 100000000 | bytes 4000000 | tf_op jit(solution)/shard_map/pallas_call | solution.py:386
  148.7 1.1 shard_map.242
  (78 shorter events, 7.6 us)
Async XLA Ops:
  26.7 23.8 %all-to-all-start.1 = ((f32[8,2,128,128]{3,2,1,0:T(8,128)}), f32[8,2,128,128]{3,2,1,0:T(8,128)S(1)}, u32[]{:S(2)}, u32[]{:S(2)}) async-start(f32[8,2,128,128]{3,2,1,0:T(8,128)} %shard_map.239), calls=%async_computation.1 | async-start | bytes 2097152 | tf_op jit(solution)/shard_map/all_to_all | solution.py:382
  32.0 24.6 %collective-permute-start.16 = (bf16[4,128,128]{2,1,0:T(8,128)(2,1)S(1)}, bf16[4,128,128]{2,1,0:T(8,128)(2,1)S(1)}, u32[]{:S(2)}, u32[]{:S(2)}) collective-permute-start(bf16[4,128,128]{2,1,0:T(8,128)(2,1)S(1)} %pad_maximum_fusion.2), channel_id=1, source_target_pairs={{0,24},{8,0},{16,8},{24,16},{1,25},{9,1},{17,9},{25,17},{2,26},{10... | collective-permute-start | bytes 393224 | tf_op jit(solution)/shard_map/ppermute | solution.py:406
  33.0 23.7 %collective-permute-start.15 = (bf16[4,128,128]{2,1,0:T(8,128)(2,1)S(1)}, bf16[4,128,128]{2,1,0:T(8,128)(2,1)S(1)}, u32[]{:S(2)}, u32[]{:S(2)}) collective-permute-start(bf16[4,128,128]{2,1,0:T(8,128)(2,1)S(1)} %pad_maximum_fusion.2), channel_id=1, source_target_pairs={{0,16},{8,24},{16,0},{24,8},{1,17},{9,25},{17,1},{25,9},{2,18},{10... | collective-permute-start | bytes 393224 | tf_op jit(solution)/shard_map/ppermute | solution.py:406
  34.2 54.6 %collective-permute-start.14 = (bf16[4,128,128]{2,1,0:T(8,128)(2,1)S(1)}, bf16[4,128,128]{2,1,0:T(8,128)(2,1)S(1)}, u32[]{:S(2)}, u32[]{:S(2)}) collective-permute-start(bf16[4,128,128]{2,1,0:T(8,128)(2,1)S(1)} %pad_maximum_fusion.2), channel_id=1, source_target_pairs={{0,8},{8,16},{16,24},{24,0},{1,9},{9,17},{17,25},{25,1},{2,10},{10... | collective-permute-start | bytes 393224 | tf_op jit(solution)/shard_map/ppermute | solution.py:406
  53.1 10.4 %all-to-all-start.2 = ((f32[4,2,128,128]{3,2,1,0:T(8,128)}), f32[4,2,128,128]{3,2,1,0:T(8,128)S(1)}, u32[]{:S(2)}, u32[]{:S(2)}) async-start(f32[4,2,128,128]{3,2,1,0:T(8,128)} %shard_map.240), calls=%async_computation.2 | async-start | bytes 1048576 | tf_op jit(solution)/shard_map/all_to_all | solution.py:382
  71.9 56.6 %copy-start.9 = (bf16[8,1024]{1,0:T(8,128)(2,1)S(1)}, bf16[8,1024]{1,0:T(8,128)(2,1)}, u32[]{:S(2)}) copy-start(bf16[8,1024]{1,0:T(8,128)(2,1)} %get-tuple-element.62) | copy-start | bytes 49156
  71.9 64.6 %copy-start.7 = (f32[8,128]{1,0:T(8,128)S(1)}, f32[8,128]{1,0:T(8,128)}, u32[]{:S(2)}) copy-start(f32[8,128]{1,0:T(8,128)} %get-tuple-element.54.refs_0_) | copy-start | bytes 12292
  71.9 76.8 %copy-start.6 = (bf16[8,1024]{1,0:T(8,128)(2,1)S(1)}, bf16[8,1024]{1,0:T(8,128)(2,1)}, u32[]{:S(2)}) copy-start(bf16[8,1024]{1,0:T(8,128)(2,1)} %get-tuple-element.55.refs_8_) | copy-start | bytes 49156
  71.9 78.0 %all-to-all-start.3 = ((f32[32,8,384]{2,1,0:T(8,128)}), f32[32,8,384]{2,1,0:T(8,128)S(1)}, u32[]{:S(2)}, u32[]{:S(2)}) async-start(f32[32,8,384]{2,1,0:T(8,128)} %get-tuple-element.63), calls=%async_computation.3 | async-start | bytes 786432 | tf_op jit(solution)/shard_map/all_to_all | solution.py:382
  88.8 17.4 %collective-permute-start.17 = (bf16[4,2,128,128]{3,2,1,0:T(8,128)(2,1)S(1)}, bf16[4,2,128,128]{3,2,1,0:T(8,128)(2,1)S(1)}, u32[]{:S(2)}, u32[]{:S(2)}) collective-permute-start(bf16[4,2,128,128]{3,2,1,0:T(8,128)(2,1)S(1)} %pad_maximum_fusion.own_ref), channel_id=1, source_target_pairs={{0,32},{32,64},{64,96},{96,128},{128,160},{160,192},{192,224},{1,3... | collective-permute-start | bytes 786440 | tf_op jit(solution)/shard_map/ppermute | solution.py:402
  90.1 26.0 %collective-permute-start.18 = (bf16[4,2,128,128]{3,2,1,0:T(8,128)(2,1)S(1)}, bf16[4,2,128,128]{3,2,1,0:T(8,128)(2,1)S(1)}, u32[]{:S(2)}, u32[]{:S(2)}) collective-permute-start(bf16[4,2,128,128]{3,2,1,0:T(8,128)(2,1)S(1)} %pad_maximum_fusion.own_ref), channel_id=1, source_target_pairs={{0,64},{32,96},{64,128},{96,160},{128,192},{160,224},{1,65},{33,97... | collective-permute-start | bytes 786440 | tf_op jit(solution)/shard_map/ppermute | solution.py:402
  91.5 45.6 %collective-permute-start.19 = (bf16[4,2,128,128]{3,2,1,0:T(8,128)(2,1)S(1)}, bf16[4,2,128,128]{3,2,1,0:T(8,128)(2,1)S(1)}, u32[]{:S(2)}, u32[]{:S(2)}) collective-permute-start(bf16[4,2,128,128]{3,2,1,0:T(8,128)(2,1)S(1)} %pad_maximum_fusion.1.own_ref), channel_id=1, source_target_pairs={{32,0},{64,32},{96,64},{128,96},{160,128},{192,160},{224,192},{33,... | collective-permute-start | bytes 786440 | tf_op jit(solution)/shard_map/ppermute | solution.py:402
  95.5 44.0 %collective-permute-start.20 = (bf16[4,2,128,128]{3,2,1,0:T(8,128)(2,1)S(1)}, bf16[4,2,128,128]{3,2,1,0:T(8,128)(2,1)S(1)}, u32[]{:S(2)}, u32[]{:S(2)}) collective-permute-start(bf16[4,2,128,128]{3,2,1,0:T(8,128)(2,1)S(1)} %pad_maximum_fusion.1.own_ref), channel_id=1, source_target_pairs={{64,0},{96,32},{128,64},{160,96},{192,128},{224,160},{65,1},{97,33... | collective-permute-start | bytes 786440 | tf_op jit(solution)/shard_map/ppermute | solution.py:402
  100.4 4.8 %collective-permute-start.7 = (bf16[8,1024]{1,0:T(8,128)(2,1)S(1)}, bf16[8,1024]{1,0:T(8,128)(2,1)S(1)}, u32[]{:S(2)}, u32[]{:S(2)}) collective-permute-start(bf16[8,1024]{1,0:T(8,128)(2,1)S(1)} %copy-done.15), channel_id=1, source_target_pairs={{0,1},{1,2},{2,3},{3,4},{4,5},{5,6},{6,7},{7,0},{8,9},{9,10},{10,1... | collective-permute-start | bytes 49160 | tf_op jit(solution)/shard_map/ppermute | solution.py:406
  105.2 15.1 %collective-permute-start.8 = (bf16[8,1024]{1,0:T(8,128)(2,1)S(1)}, bf16[8,1024]{1,0:T(8,128)(2,1)S(1)}, u32[]{:S(2)}, u32[]{:S(2)}) collective-permute-start(bf16[8,1024]{1,0:T(8,128)(2,1)S(1)} %copy-done.14), channel_id=1, source_target_pairs={{0,2},{1,3},{2,4},{3,5},{4,6},{5,7},{6,0},{7,1},{8,10},{9,11},{10,... | collective-permute-start | bytes 49160 | tf_op jit(solution)/shard_map/ppermute | solution.py:406
  106.2 16.5 %collective-permute-start.9 = (bf16[8,1024]{1,0:T(8,128)(2,1)S(1)}, bf16[8,1024]{1,0:T(8,128)(2,1)S(1)}, u32[]{:S(2)}, u32[]{:S(2)}) collective-permute-start(bf16[8,1024]{1,0:T(8,128)(2,1)S(1)} %copy-done.13), channel_id=1, source_target_pairs={{0,3},{1,4},{2,5},{3,6},{4,7},{5,0},{6,1},{7,2},{8,11},{9,12},{10,... | collective-permute-start | bytes 49160 | tf_op jit(solution)/shard_map/ppermute | solution.py:406
  116.2 7.1 %collective-permute-start.10 = (bf16[8,1024]{1,0:T(8,128)(2,1)S(1)}, bf16[8,1024]{1,0:T(8,128)(2,1)S(1)}, u32[]{:S(2)}, u32[]{:S(2)}) collective-permute-start(bf16[8,1024]{1,0:T(8,128)(2,1)S(1)} %copy-done.12), channel_id=1, source_target_pairs={{0,4},{1,5},{2,6},{3,7},{4,0},{5,1},{6,2},{7,3},{8,12},{9,13},{10,... | collective-permute-start | bytes 49160 | tf_op jit(solution)/shard_map/ppermute | solution.py:406
  120.4 3.7 %collective-permute-start.23 = (f32[8,128]{1,0:T(8,128)S(1)}, f32[8,128]{1,0:T(8,128)S(1)}, u32[]{:S(2)}, u32[]{:S(2)}) collective-permute-start(f32[8,128]{1,0:T(8,128)S(1)} %get-tuple-element.65), channel_id=1, source_target_pairs={{0,24},{8,0},{16,8},{24,16},{1,25},{9,1},{17,9},{25,17},{2,26},{10... | collective-permute-start | bytes 12296 | tf_op jit(solution)/shard_map/ppermute | solution.py:406
  122.8 4.9 %collective-permute-start.22 = (f32[8,128]{1,0:T(8,128)S(1)}, f32[8,128]{1,0:T(8,128)S(1)}, u32[]{:S(2)}, u32[]{:S(2)}) collective-permute-start(f32[8,128]{1,0:T(8,128)S(1)} %get-tuple-element.65), channel_id=1, source_target_pairs={{0,16},{8,24},{16,0},{24,8},{1,17},{9,25},{17,1},{25,9},{2,18},{10... | collective-permute-start | bytes 12296 | tf_op jit(solution)/shard_map/ppermute | solution.py:406
  123.3 5.1 %collective-permute-start.21 = (f32[8,128]{1,0:T(8,128)S(1)}, f32[8,128]{1,0:T(8,128)S(1)}, u32[]{:S(2)}, u32[]{:S(2)}) collective-permute-start(f32[8,128]{1,0:T(8,128)S(1)} %get-tuple-element.65), channel_id=1, source_target_pairs={{0,8},{8,16},{16,24},{24,0},{1,9},{9,17},{17,25},{25,1},{2,10},{10... | collective-permute-start | bytes 12296 | tf_op jit(solution)/shard_map/ppermute | solution.py:406
  124.1 7.4 %collective-permute-start.11 = (bf16[8,1024]{1,0:T(8,128)(2,1)S(1)}, bf16[8,1024]{1,0:T(8,128)(2,1)S(1)}, u32[]{:S(2)}, u32[]{:S(2)}) collective-permute-start(bf16[8,1024]{1,0:T(8,128)(2,1)S(1)} %copy-done.11), channel_id=1, source_target_pairs={{0,5},{1,6},{2,7},{3,0},{4,1},{5,2},{6,3},{7,4},{8,13},{9,14},{10,... | collective-permute-start | bytes 49160 | tf_op jit(solution)/shard_map/ppermute | solution.py:406
  127.7 5.1 %collective-permute-start.12 = (bf16[8,1024]{1,0:T(8,128)(2,1)S(1)}, bf16[8,1024]{1,0:T(8,128)(2,1)S(1)}, u32[]{:S(2)}, u32[]{:S(2)}) collective-permute-start(bf16[8,1024]{1,0:T(8,128)(2,1)S(1)} %copy-done.10), channel_id=1, source_target_pairs={{0,6},{1,7},{2,0},{3,1},{4,2},{5,3},{6,4},{7,5},{8,14},{9,15},{10,... | collective-permute-start | bytes 49160 | tf_op jit(solution)/shard_map/ppermute | solution.py:406
  128.4 8.0 %collective-permute-start.13 = (bf16[8,1024]{1,0:T(8,128)(2,1)S(1)}, bf16[8,1024]{1,0:T(8,128)(2,1)S(1)}, u32[]{:S(2)}, u32[]{:S(2)}) collective-permute-start(bf16[8,1024]{1,0:T(8,128)(2,1)S(1)} %copy-done.9), channel_id=1, source_target_pairs={{0,7},{1,0},{2,1},{3,2},{4,3},{5,4},{6,5},{7,6},{8,15},{9,8},{10,9... | collective-permute-start | bytes 49160 | tf_op jit(solution)/shard_map/ppermute | solution.py:406
  131.5 8.9 %collective-permute-start.24 = (f32[4,8,128]{2,1,0:T(8,128)S(1)}, f32[4,8,128]{2,1,0:T(8,128)S(1)}, u32[]{:S(2)}, u32[]{:S(2)}) collective-permute-start(f32[4,8,128]{2,1,0:T(8,128)S(1)} %pad_maximum_fusion.3.own_stat), channel_id=1, source_target_pairs={{32,0},{64,32},{96,64},{128,96},{160,128},{192,160},{224,192},{33,... | collective-permute-start | bytes 49160 | tf_op jit(solution)/shard_map/ppermute | solution.py:402
  132.8 7.8 %collective-permute-start.25 = (f32[4,8,128]{2,1,0:T(8,128)S(1)}, f32[4,8,128]{2,1,0:T(8,128)S(1)}, u32[]{:S(2)}, u32[]{:S(2)}) collective-permute-start(f32[4,8,128]{2,1,0:T(8,128)S(1)} %pad_maximum_fusion.3.own_stat), channel_id=1, source_target_pairs={{64,0},{96,32},{128,64},{160,96},{192,128},{224,160},{65,1},{97,33... | collective-permute-start | bytes 49160 | tf_op jit(solution)/shard_map/ppermute | solution.py:402
  136.5 6.5 %collective-permute-start = (f32[8,128]{1,0:T(8,128)S(1)}, f32[8,128]{1,0:T(8,128)S(1)}, u32[]{:S(2)}, u32[]{:S(2)}) collective-permute-start(f32[8,128]{1,0:T(8,128)S(1)} %copy-done.7), channel_id=1, source_target_pairs={{0,1},{1,2},{2,3},{3,4},{4,5},{5,6},{6,7},{7,0},{8,9},{9,10},{10,1... | collective-permute-start | bytes 12296 | tf_op jit(solution)/shard_map/ppermute | solution.py:406
  137.1 7.6 %collective-permute-start.1 = (f32[8,128]{1,0:T(8,128)S(1)}, f32[8,128]{1,0:T(8,128)S(1)}, u32[]{:S(2)}, u32[]{:S(2)}) collective-permute-start(f32[8,128]{1,0:T(8,128)S(1)} %copy-done.7), channel_id=1, source_target_pairs={{0,2},{1,3},{2,4},{3,5},{4,6},{5,7},{6,0},{7,1},{8,10},{9,11},{10,... | collective-permute-start | bytes 12296 | tf_op jit(solution)/shard_map/ppermute | solution.py:406
  139.5 9.2 %collective-permute-start.2 = (f32[8,128]{1,0:T(8,128)S(1)}, f32[8,128]{1,0:T(8,128)S(1)}, u32[]{:S(2)}, u32[]{:S(2)}) collective-permute-start(f32[8,128]{1,0:T(8,128)S(1)} %copy-done.7), channel_id=1, source_target_pairs={{0,3},{1,4},{2,5},{3,6},{4,7},{5,0},{6,1},{7,2},{8,11},{9,12},{10,... | collective-permute-start | bytes 12296 | tf_op jit(solution)/shard_map/ppermute | solution.py:406
  140.3 8.4 %collective-permute-start.3 = (f32[8,128]{1,0:T(8,128)S(1)}, f32[8,128]{1,0:T(8,128)S(1)}, u32[]{:S(2)}, u32[]{:S(2)}) collective-permute-start(f32[8,128]{1,0:T(8,128)S(1)} %copy-done.7), channel_id=1, source_target_pairs={{0,4},{1,5},{2,6},{3,7},{4,0},{5,1},{6,2},{7,3},{8,12},{9,13},{10,... | collective-permute-start | bytes 12296 | tf_op jit(solution)/shard_map/ppermute | solution.py:406
  140.5 8.2 %collective-permute-start.4 = (f32[8,128]{1,0:T(8,128)S(1)}, f32[8,128]{1,0:T(8,128)S(1)}, u32[]{:S(2)}, u32[]{:S(2)}) collective-permute-start(f32[8,128]{1,0:T(8,128)S(1)} %copy-done.7), channel_id=1, source_target_pairs={{0,5},{1,6},{2,7},{3,0},{4,1},{5,2},{6,3},{7,4},{8,13},{9,14},{10,... | collective-permute-start | bytes 12296 | tf_op jit(solution)/shard_map/ppermute | solution.py:406
  143.0 5.7 %collective-permute-start.5 = (f32[8,128]{1,0:T(8,128)S(1)}, f32[8,128]{1,0:T(8,128)S(1)}, u32[]{:S(2)}, u32[]{:S(2)}) collective-permute-start(f32[8,128]{1,0:T(8,128)S(1)} %copy-done.7), channel_id=1, source_target_pairs={{0,6},{1,7},{2,0},{3,1},{4,2},{5,3},{6,4},{7,5},{8,14},{9,15},{10,... | collective-permute-start | bytes 12296 | tf_op jit(solution)/shard_map/ppermute | solution.py:406
  144.7 4.0 %collective-permute-start.6 = (f32[8,128]{1,0:T(8,128)S(1)}, f32[8,128]{1,0:T(8,128)S(1)}, u32[]{:S(2)}, u32[]{:S(2)}) collective-permute-start(f32[8,128]{1,0:T(8,128)S(1)} %copy-done.7), channel_id=1, source_target_pairs={{0,7},{1,0},{2,1},{3,2},{4,3},{5,4},{6,5},{7,6},{8,15},{9,8},{10,9... | collective-permute-start | bytes 12296 | tf_op jit(solution)/shard_map/ppermute | solution.py:406
  (13 other events, 327.7 us)

commit v5 on v4

--- a/solution.py
+++ b/solution.py
@@ -69,12 +69,11 @@
     w_ref[...] = jnp.concatenate(
         [wb_ref[...].astype(F32), wd_ref[...].astype(F32)], axis=0
     ).astype(BF16)
-    count = len(chunk_refs)
-    size = w_ref.shape[1] // count
-    for d, chunk_ref in enumerate(chunk_refs):
-        to = lax.axis_index("head") + d
-        to = jnp.where(to >= count, to - count, to)
-        chunk_ref[...] = w_ref[:, pl.ds(pl.multiple_of(to * size, size), size)]
+    half = chunk_refs[0].shape[0]
+    size = chunk_refs[0].shape[2]
+    for d in range(2 * half):
+        to = lax.axis_index("head") ^ d
+        chunk_refs[d // half][d % half] = w_ref[:, pl.ds(pl.multiple_of(to * size, size), size)]
     row, lane = ids((T, T))
     lower, strict = row >= lane, row > lane
     eye = jnp.where(row == lane, 1.0, 0.0)
@@ -351,13 +350,16 @@
     dv_ref[...] = dv
 
 
-def input_kernel(*refs):
-    count = (len(refs) - 3) // 2
-    row_refs, chunk_refs = refs[:count], refs[count : 2 * count]
-    out_ref, rows_ref, w_ref = refs[2 * count :]
-    for d in range(count):
-        rows_ref[8 * d : 8 * d + 8, :] = row_refs[d][...]
-        w_ref[8 * d : 8 * d + 8, :] = chunk_refs[d][...].astype(F32)
+def input_kernel(near_ref, far_ref, own_ref, four_ref, two_ref, one_ref, out_ref, rows_ref, w_ref):
+    half = near_ref.shape[0]
+    rows_ref[:half, :] = near_ref[...]
+    rows_ref[half:, :] = far_ref[...]
+    places = (
+        (0, own_ref, 0), (4, four_ref, 0), (2, two_ref, 0), (6, two_ref, 2),
+        (1, one_ref, 0), (5, one_ref, 1), (3, one_ref, 2), (7, one_ref, 3),
+    )
+    for source, ref, at in places:
+        w_ref[8 * source : 8 * source + 8, :] = ref[at].astype(F32)
     high, low = split(rows_ref[...])
     w = w_ref[...].astype(BF16)
     out_ref[...] = lax.dot_general(high, w, TN, preferred_element_type=F32) + lax.dot_general(
@@ -404,6 +406,10 @@
 
 def turn(value, axis, by, count):
     return lax.ppermute(value, axis, [(i, (i + by) % count) for i in range(count)])
+
+
+def swap(value, bit, count):
+    return lax.ppermute(value, "head", [(i, i ^ bit) for i in range(count)])
 
 
 def shards(
@@ -421,11 +427,11 @@
     mine = jnp.stack([attn_key, attn_value, attn_query, attn_out_grad])
     line = [mine] + [turn(mine, "seq_1", d, x_count) for d in others]
 
-    bf16_chunk = jax.ShapeDtypeStruct((2 * heads, width // head_count), BF16)
+    bf16_half = jax.ShapeDtypeStruct((4, 2 * heads, width // head_count), BF16)
     maps, inv, ratio, rk, p, w, y, du, rows, cols, *chunks = call(
         prepare_kernel,
         (f32(heads, 3, T, T),) + (f32(heads, T, T),) * 7 + (f32(6 * heads, T), f32(T, T))
-        + (bf16_chunk,) * head_count,
+        + (bf16_half,) * 2,
         [ANY, VM, VM, SM, SM, VM, VM, VM, VM],
         layer_input, beta_weight, decay_weight, log_rate, decay_bias, delta_query, delta_key,
         delta_value, delta_out_grad,
@@ -456,7 +462,10 @@
         [VM] * 8,
         attn_key, attn_value, *qg_all, *stat_all,
     )
-    chunks = [chunks[0]] + [turn(chunks[d], "head", d, head_count) for d in range(1, head_count)]
+    own = chunks[0]
+    four = swap(chunks[1], 4, head_count)
+    two = swap(jnp.concatenate([own[2:], four[2:]]), 2, head_count)
+    one = swap(jnp.stack([own[1], four[1], two[1], two[3]]), 1, head_count)
 
     ends = call(
         spread_kernel,
@@ -477,12 +486,14 @@
         limit=WHOLE,
     )
     terms = exchange(terms, SEQ)
-    every = [logit] + [turn(logit, "head", d, head_count) for d in range(1, head_count)]
+    every = jnp.concatenate([logit, swap(logit, 1, head_count)])
+    every = jnp.concatenate([every, swap(every, 2, head_count)])
+    others = swap(every, 4, head_count)
     input_grad = call(
         input_kernel,
         f32(T, width // head_count),
-        [VM] * (2 * head_count),
-        *every, *chunks,
+        [VM] * 6,
+        every, others, own, four, two, one,
         scratch=[
             pltpu.VMEM((2 * heads * head_count, T), F32),
             pltpu.VMEM((2 * heads * head_count, width // head_count), F32),

time: 152 us -> 130 us (0.86)
  the two profiles are of different devices: /device:TPU:233 before, /device:TPU:8 now
where the time goes in v5:
time: 130 us; the launch traced here: 129 us
  starting transfers between devices  45.1 us (35%)
  waiting for transfers between devices  35.1 us (27%)
  Pallas kernels  27.3 us (21%)
  blocking collectives  16.6 us (13%)
  local copies, waits for them, and re-layouts  2.84 us (2%)
    pallas_call x7, Pallas kernels, run(): pl.pallas_call(kernel, out_shape=outs, in_specs=specs, out_specs=jax.tree...  27.3 us
    all_to_all x3, starting transfers between devices, exchange(): return lax.all_to_all(value, axis, split_axis=0, concat_axis=0, tiled=True)  21.6 us
    all_to_all x3, waiting for transfers between devices, exchange(): return lax.all_to_all(value, axis, split_axis=0, concat_axis=0, tiled=True)  20.5 us
    all_to_all x1, blocking collectives, exchange(): return lax.all_to_all(value, axis, split_axis=0, concat_axis=0, tiled=True)  16.6 us
    ppermute x6, starting transfers between devices, up_by(): return lax.ppermute(value, 'seq_0', pairs)  10.3 us
    ppermute x6, starting transfers between devices, turn(): lax.ppermute(value, axis, [(i, (i + by) % count) for i in range(count)])  7.42 us
    ppermute x6, waiting for transfers between devices, swap(): return lax.ppermute(value, 'head', [(i, i ^ bit) for i in range(count)])  7.3 us
    ppermute x6, starting transfers between devices, swap(): return lax.ppermute(value, 'head', [(i, i ^ bit) for i in range(count)])  5.85 us
  transfers between devices with their start and end apart: 21, of which 8 were waited for; matrix products, arithmetic and copies ran while one was open for 1% of the time, Pallas kernels for 13%

profile of v5, /device:TPU:8, one launch (start us, length us, event | category | flops | bytes accessed | tf_op | source)
XLA Modules:
  0.0 128.8 jit_solution(9136680467621112141)
XLA Ops:
  0.6 9.1 %shard_map.238 = (f32[4,3,128,128]{3,2,1,0:T(8,128)}, f32[4,128,128]{2,1,0:T(8,128)}, f32[4,128,128]{2,1,0:T(8,128)}, f32[4,128,128]{2,1,0:T(8,128)}, f32[4,128,...) custom-call(bf16[128,8192]{1,0:T(8,128)(2,1)} %x_hbm.3, ...), custom_call_target="tpu_custom_call" | custom-call | flops 100000000 | bytes 4000000 | tf_op jit(solution)/shard_map/pallas_call | solution.py:388
  9.7 16.6 %all_to_all.20.maps_ref = f32[4,3,128,128]{3,2,1,0:T(8,128)S(1)} all-to-all(f32[4,3,128,128]{3,2,1,0:T(8,128)} %get-tuple-element.34.maps_ref), channel_id=1, replica_groups=mesh['seq_0'=8,'seq_1'=4,'head'=8] {'seq_1'}, dimensions={0} | all-to-all | bytes 1572864 | tf_op jit(solution)/shard_map/all_to_all | solution.py:384
  26.3 1.5 %shard_map.239 = f32[8,2,128,128]{3,2,1,0:T(8,128)} custom-call(f32[4,3,128,128]{3,2,1,0:T(8,128)S(1)} %all_to_all.20.maps_ref), custom_call_target="tpu_custom_call" | custom-call | flops 100000000 | bytes 4000000 | tf_op jit(solution)/shard_map/pallas_call | solution.py:388
  27.8 8.6 %all-to-all-start.1 = ((f32[8,2,128,128]{3,2,1,0:T(8,128)}), f32[8,2,128,128]{3,2,1,0:T(8,128)S(1)}, u32[]{:S(2)}, u32[]{:S(2)}) async-start(f32[8,2,128,128]{3,2,1,0:T(8,128)} %shard_map.239), calls=%async_computation.1 | async-start | bytes 2097152 | tf_op jit(solution)/shard_map/all_to_all | solution.py:384
  36.5 1.2 collective-permute-start.8
  37.7 1.5 %collective-permute-start.7 = (bf16[4,128,128]{2,1,0:T(8,128)(2,1)S(1)}, bf16[4,128,128]{2,1,0:T(8,128)(2,1)S(1)}, u32[]{:S(2)}, u32[]{:S(2)}) collective-permute-start(bf16[4,128,128]{2,1,0:T(8,128)(2,1)S(1)} %pad_maximum_fusion.2), channel_id=1, source_target_pairs={{0,16},{8,24},{16,0},{24,8},{1,17},{9,25},{17,1},{25,9},{2,18},{10... | collective-permute-start | bytes 393224 | tf_op jit(solution)/shard_map/ppermute | solution.py:408
  39.2 2.3 %collective-permute-start.3 = (bf16[4,8,1024]{2,1,0:T(8,128)(2,1)S(1)}, bf16[4,8,1024]{2,1,0:T(8,128)(2,1)S(1)}, u32[]{:S(2)}, u32[]{:S(2)}) collective-permute-start(bf16[4,8,1024]{2,1,0:T(8,128)(2,1)S(1)} %copy-done.10), channel_id=1, source_target_pairs={{0,4},{1,5},{2,6},{3,7},{4,0},{5,1},{6,2},{7,3},{8,12},{9,13},{10,... | collective-permute-start | bytes 196616 | tf_op jit(solution)/shard_map/ppermute | solution.py:412
  41.6 3.4 %collective-permute-done.3.four_ref = bf16[4,8,1024]{2,1,0:T(8,128)(2,1)S(1)} collective-permute-done((bf16[4,8,1024]{2,1,0:T(8,128)(2,1)S(1)}, bf16[4,8,1024]{2,1,0:T(8,128)(2,1)S(1)}, u32[]{:S(2)}, u32[]{:S(2)}) %collective-permute-start.3) | collective-permute-done | bytes 65568 | tf_op jit(solution)/shard_map/ppermute | solution.py:412
  45.6 18.4 %all-to-all-done.1.groups_ref = f32[8,2,128,128]{3,2,1,0:T(8,128)S(1)} async-done(((f32[8,2,128,128]{3,2,1,0:T(8,128)}), f32[8,2,128,128]{3,2,1,0:T(8,128)S(1)}, u32[]{:S(2)}, u32[]{:S(2)}) %all-to-all-start.1) | async-done | bytes 1048608 | tf_op jit(solution)/shard_map/all_to_all | solution.py:384
  64.0 2.7 %shard_map.240 = f32[4,2,128,128]{3,2,1,0:T(8,128)} custom-call(f32[4,128,128]{2,1,0:T(8,128)S(1)} %copy-done.4, f32[4,128,128]{2,1,0:T(8,128)S(1)} %copy-done.5, f32[8,2,128,128]{3,2,1,0:T(8,128)S(1)} %all-to-all-done.1.groups_ref, f32[4,3,128,128]{3,2,1,0:T(8,128)S(1)} %all_to_all.20.maps_ref), custom_call_target="tpu_custom_call" | custom-call | flops 100000000 | bytes 4000000 | tf_op jit(solution)/shard_map/pallas_call | solution.py:388
  66.7 3.5 %all-to-all-start.2 = ((f32[4,2,128,128]{3,2,1,0:T(8,128)}), f32[4,2,128,128]{3,2,1,0:T(8,128)S(1)}, u32[]{:S(2)}, u32[]{:S(2)}) async-start(f32[4,2,128,128]{3,2,1,0:T(8,128)} %shard_map.240), calls=%async_computation.2 | async-start | bytes 1048576 | tf_op jit(solution)/shard_map/all_to_all | solution.py:384
  70.2 2.5 %collective-permute-start.9 = (bf16[4,2,128,128]{3,2,1,0:T(8,128)(2,1)S(1)}, bf16[4,2,128,128]{3,2,1,0:T(8,128)(2,1)S(1)}, u32[]{:S(2)}, u32[]{:S(2)}) collective-permute-start(bf16[4,2,128,128]{3,2,1,0:T(8,128)(2,1)S(1)} %pad_maximum_fusion.own_ref), channel_id=1, source_target_pairs={{0,32},{32,64},{64,96},{96,128},{128,160},{160,192},{192,224},{1,3... | collective-permute-start | bytes 786440 | tf_op jit(solution)/shard_map/ppermute | solution.py:404
  72.7 2.5 %collective-permute-start.10 = (bf16[4,2,128,128]{3,2,1,0:T(8,128)(2,1)S(1)}, bf16[4,2,128,128]{3,2,1,0:T(8,128)(2,1)S(1)}, u32[]{:S(2)}, u32[]{:S(2)}) collective-permute-start(bf16[4,2,128,128]{3,2,1,0:T(8,128)(2,1)S(1)} %pad_maximum_fusion.own_ref), channel_id=1, source_target_pairs={{0,64},{32,96},{64,128},{96,160},{128,192},{160,224},{1,65},{33,97... | collective-permute-start | bytes 786440 | tf_op jit(solution)/shard_map/ppermute | solution.py:404
  75.2 1.3 %collective-permute-start.11 = (bf16[4,2,128,128]{3,2,1,0:T(8,128)(2,1)S(1)}, bf16[4,2,128,128]{3,2,1,0:T(8,128)(2,1)S(1)}, u32[]{:S(2)}, u32[]{:S(2)}) collective-permute-start(bf16[4,2,128,128]{3,2,1,0:T(8,128)(2,1)S(1)} %pad_maximum_fusion.1.own_ref), channel_id=1, source_target_pairs={{32,0},{64,32},{96,64},{128,96},{160,128},{192,160},{224,192},{33,... | collective-permute-start | bytes 786440 | tf_op jit(solution)/shard_map/ppermute | solution.py:404
  76.5 1.5 %collective-permute-start.12 = (bf16[4,2,128,128]{3,2,1,0:T(8,128)(2,1)S(1)}, bf16[4,2,128,128]{3,2,1,0:T(8,128)(2,1)S(1)}, u32[]{:S(2)}, u32[]{:S(2)}) collective-permute-start(bf16[4,2,128,128]{3,2,1,0:T(8,128)(2,1)S(1)} %pad_maximum_fusion.1.own_ref), channel_id=1, source_target_pairs={{64,0},{96,32},{128,64},{160,96},{192,128},{224,160},{65,1},{97,33... | collective-permute-start | bytes 786440 | tf_op jit(solution)/shard_map/ppermute | solution.py:404
  78.0 2.0 %all-to-all-done.2.ends_ref = f32[4,2,128,128]{3,2,1,0:T(8,128)S(1)} async-done(((f32[4,2,128,128]{3,2,1,0:T(8,128)}), f32[4,2,128,128]{3,2,1,0:T(8,128)S(1)}, u32[]{:S(2)}, u32[]{:S(2)}) %all-to-all-start.2) | async-done | bytes 524320 | tf_op jit(solution)/shard_map/all_to_all | solution.py:384
  80.1 0.8 copy-done.9
  80.9 7.5 %shard_map.241 = (f32[128,512]{1,0:T(8,128)}, f32[128,512]{1,0:T(8,128)}, f32[128,512]{1,0:T(8,128)}, f32[1,4,128,128]{3,2,1,0:T(8,128)}, f32[8,128]{1,0:T(8,128)}, /*index=5*/f32[32,8,384]{2,1,0:T(8,128)}) custom-call(f32[4,2,128,128]{3,2,1,0:T(8,128)} %copy-done.9, f32[4,3,128,128]{3,2,1,0:T(8,128)} %get-tuple-element.34.maps_ref, bf16[128,512]{1,0:T(8,128)(2,1)} %q_ref.4, ...), custom_call_target="tpu_custom_call" | custom-call | flops 100000000 | bytes 4000000 | tf_op jit(solution)/shard_map/pallas_call | solution.py:388
  88.4 9.5 %all-to-all-start.3 = ((f32[32,8,384]{2,1,0:T(8,128)}), f32[32,8,384]{2,1,0:T(8,128)S(1)}, u32[]{:S(2)}, u32[]{:S(2)}) async-start(f32[32,8,384]{2,1,0:T(8,128)} %get-tuple-element.51), calls=%async_computation.3 | async-start | bytes 786432 | tf_op jit(solution)/shard_map/all_to_all | solution.py:384
  98.0 2.2 %shard_map.243 = (f32[128,128]{1,0:T(8,128)}, f32[8,128]{1,0:T(8,128)S(1)}) custom-call(bf16[128,128]{1,0:T(8,128)(2,1)S(1)} %copy-done.2, bf16[128,128]{1,0:T(8,128)(2,1)S(1)} %copy-done.3, bf16[4,2,128,128]{3,2,1,0:T(8,128)(2,1)S(1)} %pad_maximum_fusion.own_ref, bf16[4,2,128,128]{3,2,1,0:T(8,128)(2,1)S(1)} %collective-permute-done.9.near_ref, ...), custom_call_target="tpu_custom_call" | custom-call | flops 100000000 | bytes 4000000 | tf_op jit(solution)/shard_map/pallas_call | solution.py:388
  100.2 3.0 %collective-permute-start.15 = (f32[8,128]{1,0:T(8,128)S(1)}, f32[8,128]{1,0:T(8,128)S(1)}, u32[]{:S(2)}, u32[]{:S(2)}) collective-permute-start(f32[8,128]{1,0:T(8,128)S(1)} %get-tuple-element.53), channel_id=1, source_target_pairs={{0,24},{8,0},{16,8},{24,16},{1,25},{9,1},{17,9},{25,17},{2,26},{10... | collective-permute-start | bytes 12296 | tf_op jit(solution)/shard_map/ppermute | solution.py:408
  103.2 0.9 collective-permute-start.14
  104.0 0.9 collective-permute-start.13
  105.0 3.3 %collective-permute-done.14 = f32[8,128]{1,0:T(8,128)S(1)} collective-permute-done((f32[8,128]{1,0:T(8,128)S(1)}, f32[8,128]{1,0:T(8,128)S(1)}, u32[]{:S(2)}, u32[]{:S(2)}) %collective-permute-start.14) | collective-permute-done | bytes 4128 | tf_op jit(solution)/shard_map/ppermute | solution.py:408
  108.9 1.3 collective-permute-start.16
  110.3 0.7 constant_dynamic-update-slice_fusion.2
  112.8 3.2 %collective-permute-done.1 = f32[16,128]{1,0:T(8,128)S(1)} collective-permute-done((f32[16,128]{1,0:T(8,128)S(1)}, f32[16,128]{1,0:T(8,128)S(1)}, u32[]{:S(2)}, u32[]{:S(2)}) %collective-permute-start.1) | collective-permute-done | bytes 8224 | tf_op jit(solution)/shard_map/ppermute | solution.py:412
  116.0 1.3 collective-permute-start.17
  117.3 2.4 %collective-permute-start.2 = (f32[32,128]{1,0:T(8,128)S(1)}, f32[32,128]{1,0:T(8,128)S(1)}, u32[]{:S(2)}, u32[]{:S(2)}) collective-permute-start(f32[32,128]{1,0:T(8,128)S(1)} %constant_dynamic-update-slice_fusion.near_ref), channel_id=1, source_target_pairs={{0,4},{1,5},{2,6},{3,7},{4,0},{5,1},{6,2},{7,3},{8,12},{9,13},{10,... | collective-permute-start | bytes 49160 | tf_op jit(solution)/shard_map/ppermute | solution.py:412
  119.7 3.4 %collective-permute-done.17.far_stat = f32[4,8,128]{2,1,0:T(8,128)S(1)} collective-permute-done((f32[4,8,128]{2,1,0:T(8,128)S(1)}, f32[4,8,128]{2,1,0:T(8,128)S(1)}, u32[]{:S(2)}, u32[]{:S(2)}) %collective-permute-start.17) | collective-permute-done | bytes 16416 | tf_op jit(solution)/shard_map/ppermute | solution.py:404
  123.1 3.3 %shard_map.244 = (f32[128,128]{1,0:T(8,128)}, f32[128,128]{1,0:T(8,128)}) custom-call(bf16[128,128]{1,0:T(8,128)(2,1)S(1)} %copy-done.1, bf16[128,128]{1,0:T(8,128)(2,1)S(1)} %copy-done, bf16[4,2,128,128]{3,2,1,0:T(8,128)(2,1)S(1)} %pad_maximum_fusion.1.own_ref, bf16[4,2,128,128]{3,2,1,0:T(8,128)(2,1)S(1)} %collective-permute-done.11.near_ref, ...), custom_call_target="tpu_custom_call" | custom-call | flops 100000000 | bytes 4000000 | tf_op jit(solution)/shard_map/pallas_call | solution.py:388
  126.4 1.1 shard_map.242
  (64 shorter events, 4.7 us)
Async XLA Ops:
  26.3 10.1 %copy-start = (bf16[128,128]{1,0:T(8,128)(2,1)S(1)}, bf16[128,128]{1,0:T(8,128)(2,1)}, u32[]{:S(2)}) copy-start(bf16[128,128]{1,0:T(8,128)(2,1)} %v_ref.5) | copy-start | bytes 98308
  26.3 10.1 %copy-start.1 = (bf16[128,128]{1,0:T(8,128)(2,1)S(1)}, bf16[128,128]{1,0:T(8,128)(2,1)}, u32[]{:S(2)}) copy-start(bf16[128,128]{1,0:T(8,128)(2,1)} %k_ref.5) | copy-start | bytes 98308
  26.3 10.1 %copy-start.2 = (bf16[128,128]{1,0:T(8,128)(2,1)S(1)}, bf16[128,128]{1,0:T(8,128)(2,1)}, u32[]{:S(2)}) copy-start(bf16[128,128]{1,0:T(8,128)(2,1)} %q_ref.5) | copy-start | bytes 98308
  26.3 10.1 %copy-start.3 = (bf16[128,128]{1,0:T(8,128)(2,1)S(1)}, bf16[128,128]{1,0:T(8,128)(2,1)}, u32[]{:S(2)}) copy-start(bf16[128,128]{1,0:T(8,128)(2,1)} %g_ref.5) | copy-start | bytes 98308
  26.3 12.9 %copy-start.10 = (bf16[4,8,1024]{2,1,0:T(8,128)(2,1)S(1)}, bf16[4,8,1024]{2,1,0:T(8,128)(2,1)}, u32[]{:S(2)}) copy-start(bf16[4,8,1024]{2,1,0:T(8,128)(2,1)} %get-tuple-element.50) | copy-start | bytes 196612
  26.3 15.2 %copy-start.6 = (bf16[4,8,1024]{2,1,0:T(8,128)(2,1)S(1)}, bf16[4,8,1024]{2,1,0:T(8,128)(2,1)}, u32[]{:S(2)}) copy-start(bf16[4,8,1024]{2,1,0:T(8,128)(2,1)} %get-tuple-element.49.own_ref) | copy-start | bytes 196612
  27.8 36.2 %copy-start.4 = (f32[4,128,128]{2,1,0:T(8,128)S(1)}, f32[4,128,128]{2,1,0:T(8,128)}, u32[]{:S(2)}) copy-start(f32[4,128,128]{2,1,0:T(8,128)} %start_ref.1) | copy-start | bytes 786436
  27.8 36.2 %copy-start.5 = (f32[4,128,128]{2,1,0:T(8,128)S(1)}, f32[4,128,128]{2,1,0:T(8,128)}, u32[]{:S(2)}) copy-start(f32[4,128,128]{2,1,0:T(8,128)} %end_ref.1) | copy-start | bytes 786436
  27.8 36.2 %all-to-all-start.1 = ((f32[8,2,128,128]{3,2,1,0:T(8,128)}), f32[8,2,128,128]{3,2,1,0:T(8,128)S(1)}, u32[]{:S(2)}, u32[]{:S(2)}) async-start(f32[8,2,128,128]{3,2,1,0:T(8,128)} %shard_map.239), calls=%async_computation.1 | async-start | bytes 2097152 | tf_op jit(solution)/shard_map/all_to_all | solution.py:384
  36.5 9.0 %collective-permute-start.8 = (bf16[4,128,128]{2,1,0:T(8,128)(2,1)S(1)}, bf16[4,128,128]{2,1,0:T(8,128)(2,1)S(1)}, u32[]{:S(2)}, u32[]{:S(2)}) collective-permute-start(bf16[4,128,128]{2,1,0:T(8,128)(2,1)S(1)} %pad_maximum_fusion.2), channel_id=1, source_target_pairs={{0,24},{8,0},{16,8},{24,16},{1,25},{9,1},{17,9},{25,17},{2,26},{10... | collective-permute-start | bytes 393224 | tf_op jit(solution)/shard_map/ppermute | solution.py:408
  37.7 7.8 %collective-permute-start.7 = (bf16[4,128,128]{2,1,0:T(8,128)(2,1)S(1)}, bf16[4,128,128]{2,1,0:T(8,128)(2,1)S(1)}, u32[]{:S(2)}, u32[]{:S(2)}) collective-permute-start(bf16[4,128,128]{2,1,0:T(8,128)(2,1)S(1)} %pad_maximum_fusion.2), channel_id=1, source_target_pairs={{0,16},{8,24},{16,0},{24,8},{1,17},{9,25},{17,1},{25,9},{2,18},{10... | collective-permute-start | bytes 393224 | tf_op jit(solution)/shard_map/ppermute | solution.py:408
  39.2 31.0 %collective-permute-start.6 = (bf16[4,128,128]{2,1,0:T(8,128)(2,1)S(1)}, bf16[4,128,128]{2,1,0:T(8,128)(2,1)S(1)}, u32[]{:S(2)}, u32[]{:S(2)}) collective-permute-start(bf16[4,128,128]{2,1,0:T(8,128)(2,1)S(1)} %pad_maximum_fusion.2), channel_id=1, source_target_pairs={{0,8},{8,16},{16,24},{24,0},{1,9},{9,17},{17,25},{25,1},{2,10},{10... | collective-permute-start | bytes 393224 | tf_op jit(solution)/shard_map/ppermute | solution.py:408
  39.2 5.8 %collective-permute-start.3 = (bf16[4,8,1024]{2,1,0:T(8,128)(2,1)S(1)}, bf16[4,8,1024]{2,1,0:T(8,128)(2,1)S(1)}, u32[]{:S(2)}, u32[]{:S(2)}) collective-permute-start(bf16[4,8,1024]{2,1,0:T(8,128)(2,1)S(1)} %copy-done.10), channel_id=1, source_target_pairs={{0,4},{1,5},{2,6},{3,7},{4,0},{5,1},{6,2},{7,3},{8,12},{9,13},{10,... | collective-permute-start | bytes 196616 | tf_op jit(solution)/shard_map/ppermute | solution.py:412
  45.0 21.7 %copy-start.7 = (bf16[4,8,1024]{2,1,0:T(8,128)(2,1)}, bf16[4,8,1024]{2,1,0:T(8,128)(2,1)S(1)}, u32[]{:S(2)}) copy-start(bf16[4,8,1024]{2,1,0:T(8,128)(2,1)S(1)} %collective-permute-done.3.four_ref) | copy-start | bytes 196612
  45.0 52.9 %collective-permute-start.4 = (bf16[4,8,1024]{2,1,0:T(8,128)(2,1)S(1)}, bf16[4,8,1024]{2,1,0:T(8,128)(2,1)S(1)}, u32[]{:S(2)}, u32[]{:S(2)}) collective-permute-start(bf16[4,8,1024]{2,1,0:T(8,128)(2,1)S(1)} %pad_maximum_fusion.3), channel_id=1, source_target_pairs={{0,2},{1,3},{2,0},{3,1},{4,6},{5,7},{6,4},{7,5},{8,10},{9,11},{10,... | collective-permute-start | bytes 196616 | tf_op jit(solution)/shard_map/ppermute | solution.py:412
  66.7 13.4 %all-to-all-start.2 = ((f32[4,2,128,128]{3,2,1,0:T(8,128)}), f32[4,2,128,128]{3,2,1,0:T(8,128)S(1)}, u32[]{:S(2)}, u32[]{:S(2)}) async-start(f32[4,2,128,128]{3,2,1,0:T(8,128)} %shard_map.240), calls=%async_computation.2 | async-start | bytes 1048576 | tf_op jit(solution)/shard_map/all_to_all | solution.py:384
  70.2 27.7 %collective-permute-start.9 = (bf16[4,2,128,128]{3,2,1,0:T(8,128)(2,1)S(1)}, bf16[4,2,128,128]{3,2,1,0:T(8,128)(2,1)S(1)}, u32[]{:S(2)}, u32[]{:S(2)}) collective-permute-start(bf16[4,2,128,128]{3,2,1,0:T(8,128)(2,1)S(1)} %pad_maximum_fusion.own_ref), channel_id=1, source_target_pairs={{0,32},{32,64},{64,96},{96,128},{128,160},{160,192},{192,224},{1,3... | collective-permute-start | bytes 786440 | tf_op jit(solution)/shard_map/ppermute | solution.py:404
  72.7 25.2 %collective-permute-start.10 = (bf16[4,2,128,128]{3,2,1,0:T(8,128)(2,1)S(1)}, bf16[4,2,128,128]{3,2,1,0:T(8,128)(2,1)S(1)}, u32[]{:S(2)}, u32[]{:S(2)}) collective-permute-start(bf16[4,2,128,128]{3,2,1,0:T(8,128)(2,1)S(1)} %pad_maximum_fusion.own_ref), channel_id=1, source_target_pairs={{0,64},{32,96},{64,128},{96,160},{128,192},{160,224},{1,65},{33,97... | collective-permute-start | bytes 786440 | tf_op jit(solution)/shard_map/ppermute | solution.py:404
  75.2 42.0 %collective-permute-start.11 = (bf16[4,2,128,128]{3,2,1,0:T(8,128)(2,1)S(1)}, bf16[4,2,128,128]{3,2,1,0:T(8,128)(2,1)S(1)}, u32[]{:S(2)}, u32[]{:S(2)}) collective-permute-start(bf16[4,2,128,128]{3,2,1,0:T(8,128)(2,1)S(1)} %pad_maximum_fusion.1.own_ref), channel_id=1, source_target_pairs={{32,0},{64,32},{96,64},{128,96},{160,128},{192,160},{224,192},{33,... | collective-permute-start | bytes 786440 | tf_op jit(solution)/shard_map/ppermute | solution.py:404
  76.5 43.1 %collective-permute-start.12 = (bf16[4,2,128,128]{3,2,1,0:T(8,128)(2,1)S(1)}, bf16[4,2,128,128]{3,2,1,0:T(8,128)(2,1)S(1)}, u32[]{:S(2)}, u32[]{:S(2)}) collective-permute-start(bf16[4,2,128,128]{3,2,1,0:T(8,128)(2,1)S(1)} %pad_maximum_fusion.1.own_ref), channel_id=1, source_target_pairs={{64,0},{96,32},{128,64},{160,96},{192,128},{224,160},{65,1},{97,33... | collective-permute-start | bytes 786440 | tf_op jit(solution)/shard_map/ppermute | solution.py:404
  80.9 24.0 %slice-start = ((bf16[4,8,1024]{2,1,0:T(8,128)(2,1)}), bf16[1,8,1024]{2,1,0:T(8,128)(2,1)S(1)}, s32[]{:S(2)}) async-start(bf16[4,8,1024]{2,1,0:T(8,128)(2,1)} %copy-done.7), calls=%async_computation.4 | async-start | bytes 32768 | tf_op jit(solution)/shard_map/slice | solution.py:468
  88.4 38.0 %copy-start.8 = (bf16[4,8,1024]{2,1,0:T(8,128)(2,1)S(1)}, bf16[4,8,1024]{2,1,0:T(8,128)(2,1)}, u32[]{:S(2)}) copy-start(bf16[4,8,1024]{2,1,0:T(8,128)(2,1)} %copy-done.7) | copy-start | bytes 196612
  88.4 39.1 %all-to-all-start.3 = ((f32[32,8,384]{2,1,0:T(8,128)}), f32[32,8,384]{2,1,0:T(8,128)S(1)}, u32[]{:S(2)}, u32[]{:S(2)}) async-start(f32[32,8,384]{2,1,0:T(8,128)} %get-tuple-element.51), calls=%async_computation.3 | async-start | bytes 786432 | tf_op jit(solution)/shard_map/all_to_all | solution.py:384
  100.2 4.7 %collective-permute-start.15 = (f32[8,128]{1,0:T(8,128)S(1)}, f32[8,128]{1,0:T(8,128)S(1)}, u32[]{:S(2)}, u32[]{:S(2)}) collective-permute-start(f32[8,128]{1,0:T(8,128)S(1)} %get-tuple-element.53), channel_id=1, source_target_pairs={{0,24},{8,0},{16,8},{24,16},{1,25},{9,1},{17,9},{25,17},{2,26},{10... | collective-permute-start | bytes 12296 | tf_op jit(solution)/shard_map/ppermute | solution.py:408
  103.2 5.1 %collective-permute-start.14 = (f32[8,128]{1,0:T(8,128)S(1)}, f32[8,128]{1,0:T(8,128)S(1)}, u32[]{:S(2)}, u32[]{:S(2)}) collective-permute-start(f32[8,128]{1,0:T(8,128)S(1)} %get-tuple-element.53), channel_id=1, source_target_pairs={{0,16},{8,24},{16,0},{24,8},{1,17},{9,25},{17,1},{25,9},{2,18},{10... | collective-permute-start | bytes 12296 | tf_op jit(solution)/shard_map/ppermute | solution.py:408
  104.0 4.9 %collective-permute-start.13 = (f32[8,128]{1,0:T(8,128)S(1)}, f32[8,128]{1,0:T(8,128)S(1)}, u32[]{:S(2)}, u32[]{:S(2)}) collective-permute-start(f32[8,128]{1,0:T(8,128)S(1)} %get-tuple-element.53), channel_id=1, source_target_pairs={{0,8},{8,16},{16,24},{24,0},{1,9},{9,17},{17,25},{25,1},{2,10},{10... | collective-permute-start | bytes 12296 | tf_op jit(solution)/shard_map/ppermute | solution.py:408
  104.9 21.5 %collective-permute-start.5 = (bf16[4,8,1024]{2,1,0:T(8,128)(2,1)S(1)}, bf16[4,8,1024]{2,1,0:T(8,128)(2,1)S(1)}, u32[]{:S(2)}, u32[]{:S(2)}) collective-permute-start(bf16[4,8,1024]{2,1,0:T(8,128)(2,1)S(1)} %pad_maximum_fusion.4), channel_id=1, source_target_pairs={{0,1},{1,0},{2,3},{3,2},{4,5},{5,4},{6,7},{7,6},{8,9},{9,8},{10,11... | collective-permute-start | bytes 196616 | tf_op jit(solution)/shard_map/ppermute | solution.py:412
  108.9 10.8 %collective-permute-start.16 = (f32[4,8,128]{2,1,0:T(8,128)S(1)}, f32[4,8,128]{2,1,0:T(8,128)S(1)}, u32[]{:S(2)}, u32[]{:S(2)}) collective-permute-start(f32[4,8,128]{2,1,0:T(8,128)S(1)} %pad_maximum_fusion.5.own_stat), channel_id=1, source_target_pairs={{32,0},{64,32},{96,64},{128,96},{160,128},{192,160},{224,192},{33,... | collective-permute-start | bytes 49160 | tf_op jit(solution)/shard_map/ppermute | solution.py:404
  110.2 1.5 %collective-permute-start = (f32[8,128]{1,0:T(8,128)}, f32[8,128]{1,0:T(8,128)S(1)}, u32[]{:S(2)}, u32[]{:S(2)}) collective-permute-start(f32[8,128]{1,0:T(8,128)} %get-tuple-element.48), channel_id=1, source_target_pairs={{0,1},{1,0},{2,3},{3,2},{4,5},{5,4},{6,7},{7,6},{8,9},{9,8},{10,11... | collective-permute-start | bytes 12296 | tf_op jit(solution)/shard_map/ppermute | solution.py:412
  112.3 3.7 %collective-permute-start.1 = (f32[16,128]{1,0:T(8,128)S(1)}, f32[16,128]{1,0:T(8,128)S(1)}, u32[]{:S(2)}, u32[]{:S(2)}) collective-permute-start(f32[16,128]{1,0:T(8,128)S(1)} %pad_maximum_fusion.6), channel_id=1, source_target_pairs={{0,2},{1,3},{2,0},{3,1},{4,6},{5,7},{6,4},{7,5},{8,10},{9,11},{10,... | collective-permute-start | bytes 24584 | tf_op jit(solution)/shard_map/ppermute | solution.py:412
  116.0 7.1 %collective-permute-start.17 = (f32[4,8,128]{2,1,0:T(8,128)S(1)}, f32[4,8,128]{2,1,0:T(8,128)S(1)}, u32[]{:S(2)}, u32[]{:S(2)}) collective-permute-start(f32[4,8,128]{2,1,0:T(8,128)S(1)} %pad_maximum_fusion.5.own_stat), channel_id=1, source_target_pairs={{64,0},{96,32},{128,64},{160,96},{192,128},{224,160},{65,1},{97,33... | collective-permute-start | bytes 49160 | tf_op jit(solution)/shard_map/ppermute | solution.py:404
  117.3 9.1 %collective-permute-start.2 = (f32[32,128]{1,0:T(8,128)S(1)}, f32[32,128]{1,0:T(8,128)S(1)}, u32[]{:S(2)}, u32[]{:S(2)}) collective-permute-start(f32[32,128]{1,0:T(8,128)S(1)} %constant_dynamic-update-slice_fusion.near_ref), channel_id=1, source_target_pairs={{0,4},{1,5},{2,6},{3,7},{4,0},{5,1},{6,2},{7,3},{8,12},{9,13},{10,... | collective-permute-start | bytes 49160 | tf_op jit(solution)/shard_map/ppermute | solution.py:412
  (1 other events, 0.8 us)
